TPU v7x, 32 devices: a whole 2x2x4 slice. The times are simulated.
32 devices in a mesh: batch: 16 (over z, y, core), mod: 2 (over x).
Axes of the slice: x: 2, y: 2, z: 4, core: 2. Of those that a mesh axis runs over, the one named last changes fastest.
Arguments:
- hidden_in: bfloat16 [64, 256, 768], P('batch', 'mod'), may hold values from -6 to 6
- text_mask: int32 [64, 128], P('batch'), may hold values 0 or 1
- region_count: int32 [64], P('batch'), may hold values from 10 to 100, as said below
- w_query: bfloat16 [768, 768], replicated, may hold values from -0.21875 to 0.21875
- b_query: bfloat16 [768], replicated, may hold values from -3 to 3
- w_key: bfloat16 [768, 768], replicated, may hold values from -0.21875 to 0.21875
- w_value: bfloat16 [768, 768], replicated, may hold values from -0.21875 to 0.21875
- b_value: bfloat16 [768], replicated, may hold values from -3 to 3
- w_attn_out: bfloat16 [768, 768], replicated, may hold values from -2 to 2
- b_attn_out: bfloat16 [768], replicated, may hold values from -3 to 3
- gain_attn: bfloat16 [768], replicated, may hold values from 0.099609375 to 1.8984375
- shift_attn: bfloat16 [768], replicated, may hold values from -3 to 3
- w_inner: bfloat16 [768, 3072], replicated, may hold values from -0.21875 to 0.21875
- b_inner: bfloat16 [3072], replicated, may hold values from -3 to 3
- w_outer: bfloat16 [3072, 768], replicated, may hold values from -0.21875 to 0.21875
- b_outer: bfloat16 [768], replicated, may hold values from -3 to 3
- gain_ffn: bfloat16 [768], replicated, may hold values from 0.099609375 to 1.8984375
- shift_ffn: bfloat16 [768], replicated, may hold values from -3 to 3
- cotangent: bfloat16 [64, 256, 768], P('batch', 'mod'), may hold values from -6 to 6
Outputs:
- layer_out: bfloat16 [64, 256, 768], P('batch', 'mod')
- input_grad: bfloat16 [64, 256, 768], P('batch', 'mod')
- grad_w_query: float32 [768, 768], replicated
- grad_b_query: float32 [768], replicated
- key_weight_gradient: float32 [768, 768], replicated
- grad_w_value: float32 [768, 768], replicated
- grad_b_value: float32 [768], replicated
- grad_w_attn_out: float32 [768, 768], replicated
- attention_output_bias_gradient: float32 [768], replicated
- grad_gain_attn: float32 [768], replicated
- grad_shift_attn: float32 [768], replicated
- grad_w_inner: float32 [768, 3072], replicated
- grad_b_inner: float32 [3072], replicated
- grad_w_outer: float32 [3072, 768], replicated
- grad_b_outer: float32 [768], replicated
- grad_gain_ffn: float32 [768], replicated
- grad_shift_ffn: float32 [768], replicated
Inputs may be any that keep to these rules, and one draw needn't show every extreme that they name: `region_count`: every draw has a sequence with exactly 100 regions and one with exactly 10.
All inputs are finite; a program needn't handle non-finite values. No bound on the sum of `text_mask` on one device may be relied on, other than what follows from the above.
Results may differ from a plain program's by a relative error of at most 0.018.
Values may be sent and summed in bfloat16 or wider, within the bound.
A program may use at most 192 MiB of HBM per device.

v0:
```python
import jax
import jax.numpy as jnp
from jax import lax
from jax.sharding import PartitionSpec as P

HEADS = 12


epsilon = 1e-05


def partner_2(block, axis, distance):
    count = lax.axis_size(axis)
    route = []
    for low in range(count):
        high = low | 1 << distance
        if high != low and high < count:
            route += [(low, high), (high, low)]
    return lax.ppermute(block, axis, route)


def linear(rows, weight_matrix):
    return lax.dot_general(
        rows,
        weight_matrix,
        (((rows.ndim - 1,), (0,)), ((), ())),
        preferred_element_type=jnp.float32,
    )


def back_linear(gradient_row_block, weight_matrix):
    return jnp.einsum(
        "nhr,gr->nhg", gradient_row_block, weight_matrix, preferred_element_type=jnp.float32
    )


def weight_grad(layer_inputs, gradient_row_block):
    return jnp.einsum(
        "try,tro->yo", layer_inputs, gradient_row_block, preferred_element_type=jnp.float32
    )


def row_total(values):
    return jnp.sum(values.astype(jnp.float32), axis=(0, 1))


def layer_norm(rows):
    centre = rows - jnp.mean(rows, axis=-1, keepdims=True)
    factor = lax.rsqrt(jnp.mean(centre * centre, axis=-1, keepdims=True) + epsilon)
    return (centre * factor, factor)


def norm_back(gradient_row_block, normed, factor):
    return factor * (
        gradient_row_block
        - jnp.mean(gradient_row_block, axis=-1, keepdims=True)
        - normed * jnp.mean(gradient_row_block * normed, axis=-1, keepdims=True)
    )


def on_device(
    hidden_in,
    text_mask,
    region_count,
    w_query,
    b_query,
    w_key,
    w_value,
    b_value,
    w_attn_out,
    b_attn_out,
    gain_attn,
    shift_attn,
    w_inner,
    b_inner,
    w_outer,
    b_outer,
    gain_ffn,
    shift_ffn,
    cotangent,
):
    seq_count, half_len, width = hidden_in.shape
    head_size = width // HEADS
    factor_qk = 1.0 / jnp.sqrt(jnp.float32(head_size))
    text_half = lax.axis_index("mod") == 0
    rows_in = hidden_in.astype(jnp.float32)
    query = linear(hidden_in, w_query) + b_query.astype(jnp.float32)
    query_b = query.astype(jnp.bfloat16)
    key_b = linear(hidden_in, w_key).astype(jnp.bfloat16)
    value_b = (linear(hidden_in, w_value) + b_value.astype(jnp.float32)).astype(jnp.bfloat16)
    partner = partner_2(jnp.stack((key_b, value_b)), "mod", 0)
    all_keys = jnp.where(
        text_half,
        jnp.concatenate((key_b, partner[0]), axis=1),
        jnp.concatenate((partner[0], key_b), axis=1),
    )
    all_values = jnp.where(
        text_half,
        jnp.concatenate((value_b, partner[1]), axis=1),
        jnp.concatenate((partner[1], value_b), axis=1),
    )
    slot_ok = lax.broadcasted_iota(jnp.int32, (seq_count, half_len), 1) < region_count[:, None]
    valid = jnp.concatenate((text_mask == 1, slot_ok), axis=1)[:, None, None, :]
    query_h = query_b.reshape(seq_count, half_len, HEADS, head_size)
    key_h = all_keys.reshape(seq_count, 2 * half_len, HEADS, head_size)
    value_h = all_values.reshape(seq_count, 2 * half_len, HEADS, head_size)

    def masked_scores():
        scores = (
            jnp.einsum("sqhe,skhe->shqk", query_h, key_h, preferred_element_type=jnp.float32)
            * factor_qk
        )
        return jnp.where(valid, scores, jnp.float32(-1000000000.0))

    masked = masked_scores()
    highest = jnp.max(masked, axis=-1, keepdims=True)
    expo = jnp.exp(masked - highest)
    totals = jnp.sum(expo, axis=-1, keepdims=True)
    log_total = highest + jnp.log(totals)
    probs_b = (expo / totals).astype(jnp.bfloat16)
    context_b = (
        jnp.einsum("shqk,skhe->sqhe", probs_b, value_h, preferred_element_type=jnp.float32)
        .reshape(seq_count, half_len, width)
        .astype(jnp.bfloat16)
    )
    branch = linear(context_b, w_attn_out) + b_attn_out.astype(jnp.float32)
    normed_one, factor_one = layer_norm(rows_in + branch)
    middle = normed_one * gain_attn.astype(jnp.float32) + shift_attn.astype(jnp.float32)
    middle_b = middle.astype(jnp.bfloat16)
    pre_act = linear(middle_b, w_inner) + b_inner.astype(jnp.float32)
    activ, gelu_back = jax.vjp(lambda values: jax.nn.gelu(values, approximate=False), pre_act)
    activ_b = activ.astype(jnp.bfloat16)
    ffn_out = linear(activ_b, w_outer) + b_outer.astype(jnp.float32)
    normed_two, factor_two = layer_norm(middle + ffn_out)
    layer_out = (normed_two * gain_ffn.astype(jnp.float32) + shift_ffn.astype(jnp.float32)).astype(
        jnp.bfloat16
    )
    upstream = cotangent.astype(jnp.float32)
    grad_gain_ffn = jnp.sum(upstream * normed_two, axis=(0, 1))
    grad_shift_ffn = jnp.sum(upstream, axis=(0, 1))
    d_res_two = norm_back(upstream * gain_ffn.astype(jnp.float32), normed_two, factor_two)
    d_ffn_b = d_res_two.astype(jnp.bfloat16)
    grad_b_outer = row_total(d_ffn_b)
    grad_w_outer = weight_grad(activ_b, d_ffn_b)
    d_activ = back_linear(d_ffn_b, w_outer)
    d_pre_b = gelu_back(d_activ)[0].astype(jnp.bfloat16)
    grad_b_inner = row_total(d_pre_b)
    grad_w_inner = weight_grad(middle_b, d_pre_b)
    d_middle = d_res_two + back_linear(d_pre_b, w_inner)
    grad_gain_attn = jnp.sum(d_middle * normed_one, axis=(0, 1))
    grad_shift_attn = jnp.sum(d_middle, axis=(0, 1))
    d_res_one = norm_back(d_middle * gain_attn.astype(jnp.float32), normed_one, factor_one)
    d_branch_b = d_res_one.astype(jnp.bfloat16)
    attention_output_bias_gradient = row_total(d_branch_b)
    grad_w_attn_out = weight_grad(context_b, d_branch_b)
    d_context_b = back_linear(d_branch_b, w_attn_out).astype(jnp.bfloat16)
    d_context_h = d_context_b.reshape(seq_count, half_len, HEADS, head_size)
    probs_again = jnp.exp(masked_scores() - log_total)
    probs_low = probs_again.astype(jnp.bfloat16)
    d_probs = jnp.einsum(
        "sqhe,skhe->shqk", d_context_h, value_h, preferred_element_type=jnp.float32
    )
    d_scores_b = (
        probs_again * (d_probs - jnp.sum(probs_again * d_probs, axis=-1, keepdims=True))
    ).astype(jnp.bfloat16)
    d_query_b = (
        (
            jnp.einsum("shqk,skhe->sqhe", d_scores_b, key_h, preferred_element_type=jnp.float32)
            * factor_qk
        )
        .reshape(seq_count, half_len, width)
        .astype(jnp.bfloat16)
    )
    d_keys_all = (
        jnp.einsum("shqk,sqhe->skhe", d_scores_b, query_h, preferred_element_type=jnp.float32)
        * factor_qk
    ).reshape(seq_count, 2 * half_len, width)
    d_values_all = jnp.einsum(
        "shqk,sqhe->skhe", probs_low, d_context_h, preferred_element_type=jnp.float32
    ).reshape(seq_count, 2 * half_len, width)
    lower_keys, upper_keys = (d_keys_all[:, :half_len], d_keys_all[:, half_len:])
    lower_values, upper_values = (d_values_all[:, :half_len], d_values_all[:, half_len:])
    own_keys = jnp.where(text_half, lower_keys, upper_keys)
    own_values = jnp.where(text_half, lower_values, upper_values)
    other_keys = jnp.where(text_half, upper_keys, lower_keys)
    other_values = jnp.where(text_half, upper_values, lower_values)
    returned = partner_2(
        jnp.stack((other_keys, other_values)).astype(jnp.bfloat16), "mod", 0
    ).astype(jnp.float32)
    d_key_b = (own_keys + returned[0]).astype(jnp.bfloat16)
    d_value_b = (own_values + returned[1]).astype(jnp.bfloat16)
    grad_b_query = row_total(d_query_b)
    grad_b_value = row_total(d_value_b)
    grad_w_query = weight_grad(hidden_in, d_query_b)
    key_weight_gradient = weight_grad(hidden_in, d_key_b)
    grad_w_value = weight_grad(hidden_in, d_value_b)
    input_grad = (
        d_res_one
        + back_linear(d_query_b, w_query)
        + back_linear(d_key_b, w_key)
        + back_linear(d_value_b, w_value)
    ).astype(jnp.bfloat16)
    local_grads = (
        grad_w_query,
        grad_b_query,
        key_weight_gradient,
        grad_w_value,
        grad_b_value,
        grad_w_attn_out,
        attention_output_bias_gradient,
        grad_gain_attn,
        grad_shift_attn,
        grad_w_inner,
        grad_b_inner,
        grad_w_outer,
        grad_b_outer,
        grad_gain_ffn,
        grad_shift_ffn,
    )
    packed = jnp.concatenate([member.reshape(-1) for member in local_grads])
    shares = lax.psum_scatter(packed, ("batch", "mod"), scatter_dimension=0, tiled=True)
    summed = lax.all_gather(
        shares.astype(jnp.bfloat16), ("batch", "mod"), axis=0, tiled=True
    ).astype(shares.dtype)
    unpacked = []
    offset = 0
    for member in local_grads:
        unpacked.append(summed[offset : offset + member.size].reshape(member.shape))
        offset = offset + member.size
    return (
        layer_out,
        input_grad,
        unpacked[0],
        unpacked[1],
        unpacked[2],
        unpacked[3],
        unpacked[4],
        unpacked[5],
        unpacked[6],
        unpacked[7],
        unpacked[8],
        unpacked[9],
        unpacked[10],
        unpacked[11],
        unpacked[12],
        unpacked[13],
        unpacked[14],
    )


def solution(mesh):
    in_specs = (
        P("batch", "mod", None),
        P("batch", None),
        P("batch"),
        P(),
        P(),
        P(),
        P(),
        P(),
        P(),
        P(),
        P(),
        P(),
        P(),
        P(),
        P(),
        P(),
        P(),
        P(),
        P("batch", "mod", None),
    )
    out_specs = (
        P("batch", "mod", None),
        P("batch", "mod", None),
        P(),
        P(),
        P(),
        P(),
        P(),
        P(),
        P(),
        P(),
        P(),
        P(),
        P(),
        P(),
        P(),
        P(),
        P(),
    )
    return jax.shard_map(
        on_device, mesh=mesh, in_specs=in_specs, out_specs=out_specs, check_vma=False
    )
```

profile of v0, /device:TPU:0, one launch (start us, length us, event | category | flops | bytes accessed | tf_op | source)
XLA Modules:
  0.0 1213.8 jit_solution(9247152531837212770)
XLA Ops:
  8.1 2.3 convolution_convert_fusion.1
  12.5 3.0 collective-permute-start
  17.1 3.2 add_convert_fusion.3
  20.3 1.5 copy.71
  29.6 20.6 %collective-permute-done = bf16[2,4,128,768]{3,2,1,0:T(8,128)(2,1)} collective-permute-done((bf16[2,4,128,768]{3,2,1,0:T(8,128)(2,1)}, bf16[2,4,128,768]{3,2,1,0:T(8,128)(2,1)}, u32[]{:S(2)}, u32[]{:S(2)}) %collective-permute-start) | collective-permute-done | bytes 1572896 | tf_op jit(solution)/shard_map/ppermute | solution.py:19
  50.2 2.6 fusion.70
  52.8 2.3 copy.73
  55.1 2.3 copy.70
  57.4 3.9 fusion.71
  61.4 2.3 fusion.6
  64.6 3.2 fusion.40
  69.2 4.5 fusion.34
  73.7 14.4 %multiply_convert_fusion.1 = (bf16[4,128,3072]{2,1,0:T(8,128)(2,1)S(1)}, f32[4,128,3072]{2,1,0:T(8,128)S(1)}) fusion(f32[4,128,3072]{2,1,0:T(8,128)S(1)} %get-tuple-element.57, f32[3072]{0:T(1024)S(1)} %convert_element_type.144, u8[128,3072]{1,0:T(8,128)(4,1)S(1)} %get-tuple-element.18, u8[128,3072]{1,0:T(8,128)(4,1)S(1)} %get-tuple-element.17), kind=kLoop, calls=%fused_computation.12 | loop fusion | flops 111673344 | bytes 16527360 | tf_op jit(solution)/shard_map/convert_element_type | solution.py:132
  88.2 2.8 fusion.73
  92.7 2.2 convert_reduce_fusion.2
  94.9 8.9 convert_reduce_fusion
  103.8 7.3 multiply_reduce_fusion.1
  112.6 1.7 convolution_convert_fusion
  114.3 1.5 copy.75
  115.8 6.0 multiply_reduce_fusion
  121.8 2.7 fusion.16
  124.6 2.1 multiply_convert_fusion
  128.0 2.3 convolution_multiply_fusion
  131.1 2.0 copy.79
  133.1 2.6 reshape.197
  135.6 3.1 fusion.52
  140.0 1.8 collective-permute-start.1
  141.8 1.6 constant_dynamic-update-slice_fusion.9
  143.4 3.5 convolution_bitcast_fusion.2
  147.0 3.3 reshape.200
  150.4 4.8 convolution_bitcast_fusion.1
  155.2 6.0 copy.90
  161.2 5.2 convolution_bitcast_fusion
  166.4 10.8 reshape.202
  177.1 1.4 constant_dynamic-update-slice_fusion.8
  178.6 1.6 convert_element_type.160
  180.2 2.4 convert_reduce_fusion.4
  183.5 2.2 convolution_bitcast_fusion.4
  185.7 3.0 copy.80
  188.7 3.2 reshape.198
  192.0 2.2 convolution_bitcast_fusion.3
  194.1 3.0 copy.81
  197.2 3.2 reshape.199
  200.4 21.2 %dynamic-update-slice.3 = f32[7087104]{0:T(1024)} dynamic-update-slice(f32[7087104]{0:T(1024)} %constant_dynamic-update-slice_fusion.8, f32[589824]{0:T(1024)} %reshape.198, s32[]{} %constant.104) | dynamic-update-slice | bytes 4718596
  221.6 21.2 %dynamic-update-slice.4 = f32[7087104]{0:T(1024)} dynamic-update-slice(f32[7087104]{0:T(1024)} %dynamic-update-slice.3, f32[589824]{0:T(1024)} %reshape.199, s32[]{} %constant.105) | dynamic-update-slice | bytes 4718596
  244.1 21.3 %dynamic-update-slice.6 = f32[7087104]{0:T(1024)} dynamic-update-slice(f32[7087104]{0:T(1024)} %constant_dynamic-update-slice_fusion.7, f32[589824]{0:T(1024)} %reshape.200, s32[]{} %constant.107) | dynamic-update-slice | bytes 4718596
  269.3 80.6 %dynamic-update-slice.10 = f32[7087104]{0:T(1024)} dynamic-update-slice(f32[7087104]{0:T(1024)} %constant_dynamic-update-slice_fusion.4, f32[2359296]{0:T(1024)} %bitcast.133, s32[]{} %constant.111) | dynamic-update-slice | bytes 18874372
  351.2 80.3 %dynamic-update-slice.12 = f32[7087104]{0:T(1024)} dynamic-update-slice(f32[7087104]{0:T(1024)} %constant_dynamic-update-slice_fusion.3, f32[2359296]{0:T(1024)} %reshape.202, s32[]{} %constant.113) | dynamic-update-slice | bytes 18874372
  435.4 456.7 %all-reduce.6 = bf16[7087104]{0:T(1024)(128)(2,1)} all-reduce(f32[7087104]{0:T(1024)} %constant_dynamic-update-slice_fusion), channel_id=2, replica_groups=mesh['batch'=16,'mod'=2] {'batch','mod'}, use_global_device_ids=true, to_apply=%region_20.21.clone | all-reduce | flops 7087104 | bytes 42522624
  893.4 5.3 broadcast.102
  898.6 7.6 dynamic-update-slice
  906.3 2.5 fusion.44
  908.8 2.3 fusion.47
  911.1 2.2 add_convert_fusion.1
  913.3 241.0 %all-reduce.5.cloned.1.call-done = bf16[7087104]{0:T(1024)(128)(2,1)} async-done(((bf16[7087104]{0:T(1024)(128)(2,1)}), bf16[7087104]{0:T(1024)(128)(2,1)}) %all-reduce.5.cloned.1.call-update) | async-done | bytes 14174224
  1154.3 10.0 fusion.68
  1164.3 10.9 reshape.203
  1175.2 11.3 slice.145
  1186.5 5.5 fusion.69
  1192.0 3.4 slice.130
  1195.4 3.4 slice.133
  1198.7 3.4 slice.135
  1202.2 1.6 slice.138
  1203.8 1.4 fusion.67
  (162 shorter events, 34.9 us)
Async XLA Ops:
  7.2 60.6 %copy-start = (bf16[768,768]{1,0:T(8,128)(2,1)S(1)}, bf16[768,768]{1,0:T(8,128)(2,1)}, u32[]{:S(2)}) copy-start(bf16[768,768]{1,0:T(8,128)(2,1)} %param.27) | copy-start | bytes 3538948
  7.2 3.2 copy-start.6
  7.2 1147.1 %all-reduce.5.cloned.1.call-start = ((), (), s32[]{:S(2)}) async-start(), calls=%async_computation | async-start | bytes 28348416
  7.3 3.2 copy-start.21
  11.2 5.8 copy-start.46
  12.5 37.7 %collective-permute-start = (bf16[2,4,128,768]{3,2,1,0:T(8,128)(2,1)}, bf16[2,4,128,768]{3,2,1,0:T(8,128)(2,1)}, u32[]{:S(2)}, u32[]{:S(2)}) collective-permute-start(bf16[2,4,128,768]{3,2,1,0:T(8,128)(2,1)} %pad_maximum_fusion), channel_id=1, source_target_pairs={{0,1},{1,0},{2,3},{3,2},{4,5},{5,4},{6,7},{7,6},{8,9},{9,8},{10,11... | collective-permute-start | bytes 4718600 | tf_op jit(solution)/shard_map/ppermute | solution.py:19
  17.0 47.3 %copy-start.12 = (bf16[4,128,768]{1,2,0:T(8,128)(2,1)}, bf16[4,128,768]{1,2,0:T(8,128)(2,1)S(1)}, u32[]{:S(2)}) copy-start(bf16[4,128,768]{1,2,0:T(8,128)(2,1)S(1)} %copy.69) | copy-start | bytes 2359300
  17.0 4.8 copy-start.47
  17.1 5.4 copy-start.48
  17.1 6.7 copy-start.49
  21.8 35.6 %copy-start.10 = (bf16[4,128,768]{1,2,0:T(8,128)(2,1)}, bf16[4,128,768]{1,2,0:T(8,128)(2,1)S(1)}, u32[]{:S(2)}) copy-start(bf16[4,128,768]{1,2,0:T(8,128)(2,1)S(1)} %copy.71) | copy-start | bytes 2359300
  61.3 3.2 copy-start.2
  61.4 3.2 copy-start.13
  61.4 7.8 slice-start.4
  64.6 3.2 copy-start.39
  64.6 4.6 slice-start.5
  67.8 6.0 copy-start.17
  67.8 1.4 copy-start.29
  67.8 1.4 copy-start.41
  68.8 42.3 %copy-start.4 = (f32[4,128,768]{2,1,0:T(8,128)}, f32[4,128,768]{2,1,0:T(8,128)S(1)}, u32[]{:S(2)}) copy-start(f32[4,128,768]{2,1,0:T(8,128)S(1)} %get-tuple-element.56) | copy-start | bytes 4718596
  68.8 42.3 %copy-start.31 = (f32[4,128]{1,0:T(4,128)}, f32[4,128]{1,0:T(4,128)S(1)}, u32[]{:S(2)}) copy-start(f32[4,128]{1,0:T(4,128)S(1)} %broadcast_multiply_fusion.5) | copy-start | bytes 6148
  68.8 19.4 %slice-start.2 = ((s8[4718592]{0:T(1024)(128)(4,1)}), s8[4194304]{0:T(1024)(128)(4,1)S(1)}, s32[]{:S(2)}) async-start(s8[4718592]{0:T(1024)(128)(4,1)} %bitcast.156), calls=%async_computation.3 | async-start | bytes 8388608
  69.2 41.9 %copy-start.33 = (f32[4,128]{1,0:T(4,128)}, f32[4,128]{1,0:T(4,128)S(1)}, u32[]{:S(2)}) copy-start(f32[4,128]{1,0:T(4,128)S(1)} %add_rsqrt_fusion.1) | copy-start | bytes 6148
  69.2 19.0 %slice-start.3 = ((s8[4718592]{0:T(1024)(128)(4,1)}), s8[524288]{0:T(1024)(128)(4,1)S(1)}, s32[]{:S(2)}) async-start(s8[4718592]{0:T(1024)(128)(4,1)} %bitcast.156), calls=%async_computation.4 | async-start | bytes 1048576
  73.7 14.5 %copy-start.43 = (f32[768]{0:T(1024)S(1)}, f32[768]{0:T(1024)}, u32[]{:S(2)}) copy-start(f32[768]{0:T(1024)} %convert_element_type.146) | copy-start | bytes 9220
  88.2 2.9 copy-start.14
  88.2 3.2 copy-start.16
  91.1 1.6 copy-start.38
  94.9 8.9 copy-start.25
  111.1 1.1 copy-start.8
  111.7 0.9 copy-start.20
  111.7 4.1 copy-start.28
  112.6 9.2 slice-start
  115.8 6.0 slice-start.1
  124.6 2.1 copy-start.23
  124.6 2.1 copy-start.24
  126.7 1.3 copy-start.11
  128.0 2.3 copy-start.27
  128.0 2.3 copy-start.7
  140.0 38.6 %collective-permute-start.1 = (bf16[2,4,128,768]{2,3,1,0:T(8,128)(2,1)}, bf16[2,4,128,768]{2,3,1,0:T(8,128)(2,1)}, u32[]{:S(2)}, u32[]{:S(2)}) collective-permute-start(bf16[2,4,128,768]{2,3,1,0:T(8,128)(2,1)} %pad_maximum_fusion.1), channel_id=1, source_target_pairs={{0,1},{1,0},{2,3},{3,2},{4,5},{5,4},{6,7},{7,6},{8,9},{9,8},{10,11... | collective-permute-start | bytes 4718600 | tf_op jit(solution)/shard_map/ppermute | solution.py:19
  147.0 3.4 copy-start.5
  147.0 3.4 copy-start.30
  147.0 3.4 copy-start.32
  147.0 3.4 copy-start.34
  147.0 3.4 copy-start.42
  155.2 6.0 copy-start.15
  155.2 6.0 copy-start.26
  177.1 3.1 copy-start.3
  182.6 0.9 copy-start.18
  242.8 23.9 %copy-start.45 = (f32[768]{0:T(1024)S(1)}, f32[768]{0:T(1024)}, u32[]{:S(2)}) copy-start(f32[768]{0:T(1024)} %get-tuple-element.19) | copy-start | bytes 9220
  242.8 25.2 %copy-start.44 = (f32[768]{0:T(1024)S(1)}, f32[768]{0:T(1024)}, u32[]{:S(2)}) copy-start(f32[768]{0:T(1024)} %get-tuple-element.24) | copy-start | bytes 9220
  269.3 80.6 %copy-start.40 = (f32[3072]{0:T(1024)S(1)}, f32[3072]{0:T(1024)}, u32[]{:S(2)}) copy-start(f32[3072]{0:T(1024)} %get-tuple-element.65) | copy-start | bytes 36868
  351.2 80.3 %copy-start.37 = (f32[768]{0:T(1024)S(1)}, f32[768]{0:T(1024)}, u32[]{:S(2)}) copy-start(f32[768]{0:T(1024)} %get-tuple-element.27) | copy-start | bytes 9220
  351.2 81.6 %copy-start.36 = (f32[768]{0:T(1024)S(1)}, f32[768]{0:T(1024)}, u32[]{:S(2)}) copy-start(f32[768]{0:T(1024)} %get-tuple-element.21) | copy-start | bytes 9220
  351.2 82.9 %copy-start.35 = (f32[768]{0:T(1024)S(1)}, f32[768]{0:T(1024)}, u32[]{:S(2)}) copy-start(f32[768]{0:T(1024)} %get-tuple-element.26) | copy-start | bytes 9220
  906.2 2.5 copy-start.19
  906.2 4.9 copy-start.9
  906.2 4.9 copy-start.22
  1198.7 7.8 copy-start.1
Sparse Core Ops, SparseCore 0:
  906.3 247.9 all-reduce.4
where the time goes:
time: 1240 us; the launch traced here: 1210 us
  blocking collectives  457 us (37%)
  local copies, waits for them, and re-layouts  355 us (29%)
  waiting for transfers between devices  262 us (21%)
  matrix products  77.6 us (6%)
  other arithmetic  42.4 us (3%)
  between operations  15.3 us (1%)
    unnamed x1, blocking collectives  457 us
    unnamed x130, local copies, waits for them, and re-layouts  259 us
    unnamed x2, waiting for transfers between devices  241 us
    slice x9, local copies, waits for them, and re-layouts, on_device(): unpacked.append(summed[offset:offset + member.size].reshape(member.shape))  41.3 us
    dot_general x6, matrix products, back_linear(): jnp.einsum('nhr,gr->nhg', gradient_row_block, weight_matrix, preferred_el...  24.9 us
  transfers between devices with their start and end apart: 3, of which 2 were waited for; matrix products, arithmetic and copies ran while one was open for 5% of the time, Pallas kernels for 0%

commit v1 on v0

--- a/solution.py
+++ b/solution.py
@@ -1,9 +1,384 @@
+import functools
+
 import jax
 import jax.numpy as jnp
 from jax import lax
+from jax.experimental import pallas as pl
+from jax.experimental.pallas import tpu as pltpu
 from jax.sharding import PartitionSpec as P
 
 HEADS = 12
+MESH = pl.DeviceIdType.MESH
+ROWS = 256
+LANES = 768
+
+
+class Wire:
+    def __init__(self, extra_bits):
+        self.b = lax.axis_index("batch")
+        self.m = lax.axis_index("mod")
+        self.core = lax.rem(self.b, 2)
+        self.y = lax.rem(self.b // 2, 2)
+        self.z = lax.rem(self.b // 4, 4)
+        self.extra_bits = extra_bits
+
+    def flip(self, bit):
+        own = lax.rem(self.b // (1 << bit), 2)
+        return (self.b + (1 - 2 * own) * (1 << bit), self.m)
+
+    def peer(self, dim):
+        if dim == "x":
+            return (self.b, 1 - self.m)
+        if dim == "y":
+            return self.flip(1)
+        if dim == "core":
+            return self.flip(0)
+        if dim == "up":
+            return (self.b + 4, self.m)
+        if dim == "down":
+            return (self.b - 4, self.m)
+        return self.flip(dim)
+
+    def coord(self, dim):
+        return self.m if dim == "x" else self.y
+
+    def barrier(self):
+        bar = pltpu.get_barrier_semaphore()
+        peers = [self.peer(d) for d in ("core", "x", "y")]
+        peers += [self.flip(bit) for bit in range(2, 4 + self.extra_bits)]
+        for who in peers:
+            pl.semaphore_signal(bar, inc=1, device_id=who, device_id_type=MESH)
+        mid_low, mid_high = self.z == 1, self.z == 2
+
+        @pl.when(mid_low)
+        def _():
+            pl.semaphore_signal(bar, inc=1, device_id=self.peer("up"), device_id_type=MESH)
+
+        @pl.when(mid_high)
+        def _():
+            pl.semaphore_signal(bar, inc=1, device_id=self.peer("down"), device_id_type=MESH)
+
+        pl.semaphore_wait(bar, len(peers) + jnp.where(mid_low | mid_high, 1, 0))
+
+
+def plan_sizes(kinds, extra_bits):
+    rows = sems = 0
+    for kind in kinds:
+        n = ROWS
+        rows += ROWS
+        sems += 1
+        order = "xyz" if kind == "A" else "yxz" if kind == "B" else "zxy" if kind == "C" else "zyx"
+        for dim in order:
+            if dim == "z":
+                rows += 6 * (n // 4)
+                n //= 4
+            else:
+                rows += n // 2
+                n //= 2
+        rows += extra_bits * n
+        sems += 6 + 6 + 4 + extra_bits + 1
+    return rows, sems
+
+
+def add_rows(acc, at, rb, rb_at, n):
+    step = min(n, 64)
+
+    def body(i, carry):
+        d = pl.multiple_of(at + i * step, 16)
+        s = pl.multiple_of(rb_at + i * step, 16)
+        total = acc[pl.ds(d, step), :].astype(jnp.float32) + rb[pl.ds(s, step), :].astype(jnp.float32)
+        acc[pl.ds(d, step), :] = total.astype(jnp.bfloat16)
+        return carry
+
+    if n == step:
+        body(0, 0)
+    else:
+        lax.fori_loop(0, n // step, body, 0)
+
+
+class Tasks:
+    def __init__(self, wire, kinds, acc, sib, fin, rb, ssem, rsem):
+        self.w, self.acc, self.sib, self.fin, self.rb = wire, acc, sib, fin, rb
+        self.ssem, self.rsem = ssem, rsem
+        self.rb_at = 0
+        self.sem_at = 0
+        self.homes = []
+        self.steps = [self.build(t, kind) for t, kind in enumerate(kinds)]
+
+    def space(self, n):
+        at = self.rb_at
+        self.rb_at += n
+        return at
+
+    def copy(self, src, dst, who):
+        k = self.sem_at
+        self.sem_at += 1
+        return lambda: pltpu.make_async_remote_copy(
+            src_ref=src(), dst_ref=dst(), send_sem=self.ssem.at[k], recv_sem=self.rsem.at[k], device_id=who, device_id_type=MESH
+        )
+
+    def rows(self, at, n):
+        return self.acc.at[pl.ds(pl.multiple_of(at, 16), n), :]
+
+    def build(self, t, kind):
+        w = self.w
+        steps = []
+        home = t * ROWS
+        at0 = self.space(ROWS)
+
+        def done(at, n):
+            return self.rb.at[pl.ds(pl.multiple_of(at + (at0 - home), 16), n), :]
+
+        def keep(at, n):
+            self.rb[pl.ds(pl.multiple_of(at + (at0 - home), 16), n), :] = self.acc[pl.ds(pl.multiple_of(at, 16), n), :]
+
+        def exchange(src, dst, who, then):
+            cp = self.copy(src, dst, who)
+
+            def begin():
+                cp().start()
+
+            def finish():
+                cp().wait()
+                then()
+
+            steps.append((begin, finish))
+
+        def reduce(dim, base, n):
+            half, a = n // 2, w.coord(dim)
+            at = self.space(half)
+            kept = base + a * half
+            sent = base + (1 - a) * half
+            exchange(
+                lambda: self.rows(sent, half),
+                lambda: self.rb.at[pl.ds(at, half), :],
+                w.peer(dim),
+                lambda: add_rows(self.acc, kept, self.rb, at, half),
+            )
+            return kept, half
+
+        def gather(dim, base, n):
+            exchange(lambda: done(base, n), lambda: done(base, n), w.peer(dim), lambda: None)
+
+        def line_reduce(base, n):
+            q, z, zz = n // 4, w.z, 3 - w.z
+            for s in (1, 2, 3):
+                up_at, down_at = self.space(q), self.space(q)
+                up_sends, up_gets = (z < 3) & (s >= z + 1), (z >= 1) & (s >= z)
+                down_sends, down_gets = (zz < 3) & (s >= zz + 1), (zz >= 1) & (s >= zz)
+                up_src = base + jnp.clip(4 - s + z, 0, 3) * q
+                down_src = base + jnp.clip(s + z - 4, 0, 3) * q
+                up_add = base + jnp.clip(3 - s + z, 0, 3) * q
+                down_add = base + jnp.clip(s - 3 + z, 0, 3) * q
+                up = self.copy(lambda v=up_src: self.rows(v, q), lambda v=up_at: self.rb.at[pl.ds(v, q), :], w.peer("up"))
+                down = self.copy(lambda v=down_src: self.rows(v, q), lambda v=down_at: self.rb.at[pl.ds(v, q), :], w.peer("down"))
+                steps.append(line_step(up, down, up_sends, up_gets, down_sends, down_gets,
+                                       lambda a=up_add, r=up_at: add_rows(self.acc, a, self.rb, r, q),
+                                       lambda a=down_add, r=down_at: add_rows(self.acc, a, self.rb, r, q)))
+            return base + z * q, q
+
+        def line_gather(base, q):
+            z = w.z
+            for s in (1, 2, 3):
+                up_sends, up_gets = (z < 3) & (z - (s - 1) >= 0), z - s >= 0
+                down_sends, down_gets = (z > 0) & (z + (s - 1) <= 3), z + s <= 3
+                up_src = base + jnp.clip(z - s + 1, 0, 3) * q
+                down_src = base + jnp.clip(z + s - 1, 0, 3) * q
+                up = self.copy(lambda v=up_src: done(v, q), lambda v=up_src: done(v, q), w.peer("up"))
+                down = self.copy(lambda v=down_src: done(v, q), lambda v=down_src: done(v, q), w.peer("down"))
+                steps.append(line_step(up, down, up_sends, up_gets, down_sends, down_gets, None, None))
+
+        def line_step(up, down, up_sends, up_gets, down_sends, down_gets, up_then, down_then):
+            def begin():
+                @pl.when(up_sends)
+                def _():
+                    up().start()
+
+                @pl.when(down_sends)
+                def _():
+                    down().start()
+
+            def finish():
+                for cp, gets, then in ((up, up_gets, up_then), (down, down_gets, down_then)):
+                    @pl.when(gets)
+                    def _(cp=cp, then=then):
+                        cp().wait_recv()
+                        if then is not None:
+                            then()
+
+                for cp, sends in ((up, up_sends), (down, down_sends)):
+                    @pl.when(sends)
+                    def _(cp=cp):
+                        cp().wait_send()
+
+            return begin, finish
+
+        def then_keep(base, n):
+            begin, finish = steps.pop()
+
+            def finish_and_keep():
+                finish()
+                keep(base, n)
+
+            steps.append((begin, finish_and_keep))
+
+        def widen(base, n):
+            for bit in range(4, 4 + w.extra_bits):
+                at = self.space(n)
+                exchange(
+                    lambda: self.rows(base, n),
+                    lambda at=at: self.rb.at[pl.ds(at, n), :],
+                    w.peer(bit),
+                    lambda at=at: add_rows(self.acc, base, self.rb, at, n),
+                )
+
+        exchange(
+            lambda: self.sib.at[pl.ds(home, ROWS), :],
+            lambda: self.rb.at[pl.ds(at0, ROWS), :],
+            w.peer("core"),
+            lambda: add_rows(self.acc, home, self.rb, at0, ROWS),
+        )
+        if kind in "AB":
+            d1, d2 = ("x", "y") if kind == "A" else ("y", "x")
+            b1, n1 = reduce(d1, home, ROWS)
+            b2, n2 = reduce(d2, b1, n1)
+            b3, n3 = line_reduce(b2, n2)
+            widen(b3, n3)
+            then_keep(b3, n3)
+            line_gather(b2, n3)
+            gather(d2, b2, n2)
+            gather(d1, b1, n1)
+        else:
+            d1, d2 = ("x", "y") if kind == "C" else ("y", "x")
+            b1, n1 = line_reduce(home, ROWS)
+            b2, n2 = reduce(d1, b1, n1)
+            b3, n3 = reduce(d2, b2, n2)
+            widen(b3, n3)
+            then_keep(b3, n3)
+            gather(d2, b3, n3)
+            gather(d1, b2, n2)
+            line_gather(home, n1)
+        exchange(
+            lambda: self.rb.at[pl.ds(at0, ROWS), :],
+            lambda: self.fin.at[pl.ds(home, ROWS), :],
+            w.peer("core"),
+            lambda: None,
+        )
+        self.homes.append(at0)
+        return steps
+
+    def op(self, t, p):
+        steps = self.steps[t]
+        if p > 0:
+            steps[p - 1][1]()
+        if p < len(steps):
+            steps[p][0]()
+
+
+KINDS = "ABCABDABCABDABCABD"
+START = tuple(t // 3 for t in range(18))
+SMALL = 16
+
+
+def block_of(refs, half, t):
+    outer, inner, attn = refs
+    if t < 6:
+        return outer.at[pl.ds(pl.multiple_of(half * 1536 + t * ROWS, ROWS), ROWS), :]
+    if t < 12:
+        i, j = (t - 6) % 3, (t - 6) // 3
+        return inner.at[pl.ds(i * ROWS, ROWS), pl.ds(pl.multiple_of((half * 2 + j) * LANES, LANES), LANES)]
+    return attn.at[pl.ds(pl.multiple_of(half * 1536 + (t - 12) * ROWS, ROWS), ROWS), :]
+
+
+def sum_kernel(extra_bits, g_outer, g_inner, g_attn, small_in, s_outer, s_inner, s_attn, small_out,
+               acc, sib, fin, rb, small, small_rb, ssem, rsem, lsem, vsem):
+    w = Wire(extra_bits)
+    count = len(KINDS)
+    ins, outs = (g_outer, g_inner, g_attn), (s_outer, s_inner, s_attn)
+
+    def load(t, who):
+        half, buf = (w.core, acc) if who == 0 else (1 - w.core, sib)
+        return pltpu.make_async_copy(block_of(ins, half, t), buf.at[pl.ds(t * ROWS, ROWS), :], lsem.at[2 * t + who])
+
+    def store(t, who):
+        if who == 0:
+            half, source = w.core, rb.at[pl.ds(tasks.homes[t], ROWS), :]
+        else:
+            half, source = 1 - w.core, fin.at[pl.ds(t * ROWS, ROWS), :]
+        return pltpu.make_async_copy(source, block_of(outs, half, t), lsem.at[2 * t + who])
+
+    for t in range(count):
+        load(t, 1).start()
+        load(t, 0).start()
+    w.barrier()
+    tasks = Tasks(w, KINDS, acc, sib, fin, rb, ssem, rsem)
+
+    small[0] = small_in[...]
+    hops = ["core", "x", "y"] + list(range(2, 4 + extra_bits))
+
+    def small_copy(k):
+        return pltpu.make_async_remote_copy(
+            src_ref=small.at[k], dst_ref=small_rb.at[k], send_sem=vsem.at[0, k], recv_sem=vsem.at[1, k],
+            device_id=w.peer(hops[k]), device_id_type=MESH)
+
+    def small_op(k):
+        if k > 0:
+            small_copy(k - 1).wait()
+            small[k] = small[k - 1] + small_rb[k - 1]
+        if k < len(hops):
+            small_copy(k).start()
+
+    ops = [(START[t] + p, t, p) for t in range(count) for p in range(len(tasks.steps[t]) + 1)]
+    ops += [(k + 1, count, k) for k in range(len(hops) + 1)]
+    for _, t, p in sorted(ops):
+        if t == count:
+            small_op(p)
+            continue
+        if p == 0:
+            load(t, 1).wait()
+        if p == 1:
+            load(t, 0).wait()
+        tasks.op(t, p)
+        if p == len(tasks.steps[t]):
+            store(t, 0).start()
+            store(t, 1).start()
+    small_out[...] = small[len(hops)]
+    for t in range(count):
+        store(t, 0).wait()
+        store(t, 1).wait()
+
+
+def sum_gradients(g_outer, g_inner, g_attn, small_in):
+    extra_bits = (lax.axis_size("batch") // 16).bit_length() - 1
+    rows, sems = plan_sizes(KINDS, extra_bits)
+    hops = 5 + extra_bits
+    count = len(KINDS)
+    hbm = pl.BlockSpec(memory_space=pl.ANY)
+    vmem = pl.BlockSpec(memory_space=pltpu.VMEM)
+    return pl.pallas_call(
+        functools.partial(sum_kernel, extra_bits),
+        out_shape=(
+            jax.ShapeDtypeStruct(g_outer.shape, jnp.bfloat16),
+            jax.ShapeDtypeStruct(g_inner.shape, jnp.bfloat16),
+            jax.ShapeDtypeStruct(g_attn.shape, jnp.bfloat16),
+            jax.ShapeDtypeStruct(small_in.shape, jnp.float32),
+        ),
+        in_specs=[hbm, hbm, hbm, vmem],
+        out_specs=(hbm, hbm, hbm, vmem),
+        scratch_shapes=[
+            pltpu.VMEM((count * ROWS, LANES), jnp.bfloat16),
+            pltpu.VMEM((count * ROWS, LANES), jnp.bfloat16),
+            pltpu.VMEM((count * ROWS, LANES), jnp.bfloat16),
+            pltpu.VMEM((rows, LANES), jnp.bfloat16),
+            pltpu.VMEM((hops + 1, SMALL, LANES), jnp.float32),
+            pltpu.VMEM((hops, SMALL, LANES), jnp.float32),
+            pltpu.SemaphoreType.DMA((sems,)),
+            pltpu.SemaphoreType.DMA((sems,)),
+            pltpu.SemaphoreType.DMA((2 * count,)),
+            pltpu.SemaphoreType.DMA((2, hops)),
+        ],
+        compiler_params=pltpu.CompilerParams(collective_id=1, has_side_effects=True, vmem_limit_bytes=60 << 20),
+    )(g_outer, g_inner, g_attn, small_in)
 
 
 epsilon = 1e-05
@@ -200,51 +575,37 @@
         + back_linear(d_key_b, w_key)
         + back_linear(d_value_b, w_value)
     ).astype(jnp.bfloat16)
-    local_grads = (
-        grad_w_query,
-        grad_b_query,
-        key_weight_gradient,
-        grad_w_value,
-        grad_b_value,
-        grad_w_attn_out,
-        attention_output_bias_gradient,
-        grad_gain_attn,
-        grad_shift_attn,
-        grad_w_inner,
-        grad_b_inner,
-        grad_w_outer,
-        grad_b_outer,
-        grad_gain_ffn,
-        grad_shift_ffn,
-    )
-    packed = jnp.concatenate([member.reshape(-1) for member in local_grads])
-    shares = lax.psum_scatter(packed, ("batch", "mod"), scatter_dimension=0, tiled=True)
-    summed = lax.all_gather(
-        shares.astype(jnp.bfloat16), ("batch", "mod"), axis=0, tiled=True
-    ).astype(shares.dtype)
-    unpacked = []
-    offset = 0
-    for member in local_grads:
-        unpacked.append(summed[offset : offset + member.size].reshape(member.shape))
-        offset = offset + member.size
+    g_outer = grad_w_outer.astype(jnp.bfloat16)
+    g_inner = grad_w_inner.astype(jnp.bfloat16)
+    g_attn = jnp.concatenate(
+        [g.astype(jnp.bfloat16) for g in (grad_w_query, key_weight_gradient, grad_w_value, grad_w_attn_out)]
+    )
+    small_in = jnp.concatenate(
+        [
+            grad_b_query, grad_b_value, attention_output_bias_gradient, grad_gain_attn, grad_shift_attn,
+            grad_b_inner, grad_b_outer, grad_gain_ffn, grad_shift_ffn, jnp.zeros((4 * width,), jnp.float32),
+        ]
+    ).reshape(SMALL, width)
+    s_outer, s_inner, s_attn, s_small = sum_gradients(g_outer, g_inner, g_attn, small_in)
+    wide = s_attn.astype(jnp.float32).reshape(4, width, width)
     return (
         layer_out,
         input_grad,
-        unpacked[0],
-        unpacked[1],
-        unpacked[2],
-        unpacked[3],
-        unpacked[4],
-        unpacked[5],
-        unpacked[6],
-        unpacked[7],
-        unpacked[8],
-        unpacked[9],
-        unpacked[10],
-        unpacked[11],
-        unpacked[12],
-        unpacked[13],
-        unpacked[14],
+        wide[0],
+        s_small[0],
+        wide[1],
+        wide[2],
+        s_small[1],
+        wide[3],
+        s_small[2],
+        s_small[3],
+        s_small[4],
+        s_inner.astype(jnp.float32),
+        s_small[5:9].reshape(-1),
+        s_outer.astype(jnp.float32),
+        s_small[9],
+        s_small[10],
+        s_small[11],
     )
 
 

time: 1240 us -> 369 us (0.30); the launches traced: 1210 us -> 363 us
  blocking collectives: 457 us -> 0 us
  local copies, waits for them, and re-layouts: 355 us -> 52.3 us
  waiting for transfers between devices: 262 us -> 36.8 us
  Pallas kernels: 0 us -> 133 us
  other arithmetic: 42.4 us -> 57.5 us
  between operations: 15.3 us -> 2 us
    unnamed x1 -> x0, blocking collectives: 457 us -> none
    unnamed x2 -> x0, waiting for transfers between devices: 241 us -> none
    unnamed x130 -> x145, local copies, waits for them, and re-layouts: 259 us -> 25.6 us
    pallas_call x0 -> x1, Pallas kernels: none -> 133 us  [sum_gradients(): pl.pallas_call(functools.partial(sum_kernel, extra_bits), out_shape=(jax....]
    reshape x6 -> x2, local copies, waits for them, and re-layouts: 34 us -> 2.03 us  [the longest x1 1.43 us: on_device(): small_in = jnp.concatenate([grad_b_query, grad_b_value, attention_output_...]
    slice x9 -> x5, local copies, waits for them, and re-layouts: 41.3 us -> 14.5 us  [the longest x1 6.33 us: on_device(): wide[3]]
    ppermute x2, waiting for transfers between devices: 20.6 us -> 36.8 us  [partner_2(): return lax.ppermute(block, axis, route)]
  transfers between devices with their start and end apart: 3 -> 2, of which waited for: 2 -> 2; matrix products, arithmetic and copies ran while one was open for 5% -> 9% of each run, Pallas kernels for 0% -> 0%
where the time goes in v1:
time: 369 us; the launch traced here: 363 us
  Pallas kernels  133 us (36%)
  matrix products  76.4 us (21%)
  other arithmetic  57.5 us (16%)
  local copies, waits for them, and re-layouts  52.3 us (14%)
  waiting for transfers between devices  36.8 us (10%)
  starting transfers between devices  5.18 us (1%)
    pallas_call x1, Pallas kernels, sum_gradients(): pl.pallas_call(functools.partial(sum_kernel, extra_bits), out_shape=(jax....  133 us
    ppermute x2, waiting for transfers between devices, partner_2(): return lax.ppermute(block, axis, route)  36.8 us
    unnamed x145, local copies, waits for them, and re-layouts  25.6 us
    dot_general x6, matrix products, back_linear(): jnp.einsum('nhr,gr->nhg', gradient_row_block, weight_matrix, preferred_el...  23.9 us
    dot_general x6, matrix products, weight_grad(): jnp.einsum('try,tro->yo', layer_inputs, gradient_row_block, preferred_ele...  19.4 us
    convert_element_type x1, other arithmetic, on_device(): activ_b = activ.astype(jnp.bfloat16)  14.4 us
    dot_general x6, matrix products, linear(): lax.dot_general(rows, weight_matrix, (((rows.ndim - 1,), (0,)), ((), ()))...  14.3 us
  transfers between devices with their start and end apart: 2, of which 2 were waited for; matrix products, arithmetic and copies ran while one was open for 9% of the time, Pallas kernels for 0%

profile of v1, /device:TPU:0, one launch (start us, length us, event | category | flops | bytes accessed | tf_op | source)
XLA Modules:
  0.0 363.1 jit_solution(8619195017328565604)
XLA Ops:
  1.5 2.3 convolution_convert_fusion.1
  4.7 1.3 pad_maximum_fusion.1
  6.0 3.0 collective-permute-start
  8.9 1.2 copy.63
  13.1 2.9 add_convert_fusion.3
  16.1 1.5 copy.62
  18.2 1.3 convert_element_type.171
  20.2 1.3 convert_element_type.178
  23.5 20.2 %collective-permute-done = bf16[2,4,128,768]{3,2,1,0:T(8,128)(2,1)} collective-permute-done((bf16[2,4,128,768]{3,2,1,0:T(8,128)(2,1)}, bf16[2,4,128,768]{3,2,1,0:T(8,128)(2,1)}, u32[]{:S(2)}, u32[]{:S(2)}) %collective-permute-start) | collective-permute-done | bytes 1572896 | tf_op jit(solution)/shard_map/ppermute | solution.py:394
  43.6 2.4 fusion.73
  46.0 1.2 copy.64
  47.1 1.5 copy.61
  48.7 4.1 %fusion.74 = (f32[4,12,128]{2,1,0:T(8,128)S(1)}, f32[4,12,128,256]{3,2,1,0:T(8,128)S(1)}) fusion(bf16[4,128,12,64]{1,3,2,0:T(8,128)(2,1)S(1)} %bitcast.141, bf16[4,128,12,64]{1,3,2,0:T(8,128)(2,1)} %bitcast.153, bf16[4,128,12,64]{1,3,2,0:T(8,128)(2,1)} %bitcast.151, pred[]{:T(512)S(6)} %eq.9, pred[4,256]{1,0:T(4,128)(4,1)} %pad_add_fusion), kind=kOutput, calls=%fused_computation.154 | convolution fusion | flops 213116928 | bytes 8676353 | tf_op jit(solution)/shard_map/sqhe,skhe->shqk/dot_general | solution.py:485
  52.8 2.4 fusion.6
  56.0 3.2 fusion.43
  60.6 4.5 %fusion.34 = (u8[128,3072]{1,0:T(8,128)(4,1)S(1)}, u8[128,3072]{1,0:T(8,128)(4,1)S(1)}, f32[4,128,3072]{2,1,0:T(8,128)S(1)}) fusion(f32[3072]{0:T(1024)S(1)} %convert_element_type.174, bf16[768,3072]{1,0:T(8,128)(2,1)S(1)} %bitcast.158, f32[4,128,768]{2,1,0:T(8,128)S(1)} %get-tuple-element.66, f32[768]{0:T(1024)S(1)} %copy-done.49, f32[768]{0:T(1024)S(1)} %copy-done.37, ...), kind=kOutput, calls=%fused_computation.89 | convolution fusion | flops 2439118848 | bytes 13391872 | tf_op jit(solution)/shard_map/dot_general | solution.py:398
  65.2 14.4 %multiply_convert_fusion.1 = (bf16[4,128,3072]{2,1,0:T(8,128)(2,1)S(1)}, f32[4,128,3072]{2,1,0:T(8,128)S(1)}) fusion(f32[4,128,3072]{2,1,0:T(8,128)S(1)} %get-tuple-element.67, f32[3072]{0:T(1024)S(1)} %convert_element_type.174, u8[128,3072]{1,0:T(8,128)(4,1)S(1)} %get-tuple-element.26, u8[128,3072]{1,0:T(8,128)(4,1)S(1)} %get-tuple-element.25), kind=kLoop, calls=%fused_computation.14 | loop fusion | flops 111673344 | bytes 16527360 | tf_op jit(solution)/shard_map/convert_element_type | solution.py:507
  79.7 2.8 fusion.76
  82.8 1.3 fusion.28
  84.1 2.2 convert_reduce_fusion.2
  86.3 8.9 %convert_reduce_fusion = (f32[3072]{0:T(1024)}, bf16[4,128,3072]{2,1,0:T(8,128)(2,1)}) fusion(f32[4,128,3072]{2,1,0:T(8,128)S(1)} %get-tuple-element.50, bf16[4,128,768]{2,1,0:T(8,128)(2,1)S(1)} %get-tuple-element.44, bf16[3072,768]{1,0:T(8,128)(2,1)} %param.33, f32[4,128,3072]{2,1,0:T(8,128)S(1)} %get-tuple-element.67, f32[3072]{0:T(1024)S(1)} %convert_element_type.174), kind=kOutput, calls=%fused_computation.9 | convolution fusion | flops 2442654720 | bytes 21258240 | tf_op jit(solution)/shard_map/nhr,gr->nhg/dot_general | solution.py:407
  95.2 7.3 %multiply_reduce_fusion.1 = (f32[768]{0:T(1024)}, f32[4,128]{1,0:T(4,128)S(1)}, f32[4,128]{1,0:T(4,128)S(1)}, f32[768]{0:T(1024)}, f32[4,128,768]{2,1,0:T(8,128)S(1)}) fusion(f32[4,128,768]{2,1,0:T(8,128)S(1)} %get-tuple-element.66, f32[4,128]{1,0:T(4,128)S(1)} %add_rsqrt_fusion.1, f32[4,128]{1,0:T(4,128)S(1)} %broadcast_multiply_fusion.5, ...), kind=kOutput, calls=%fused_computation.70 | convolution fusion | flops 2422994432 | bytes 13398016 | tf_op jit(solution)/shard_map/nhr,gr->nhg/dot_general | solution.py:407
  103.9 1.7 convolution_convert_fusion
  105.6 1.5 copy.66
  107.1 6.2 %multiply_reduce_fusion = (f32[4,12,128]{2,1,0:T(8,128)S(1)}, f32[4,12,128,256]{3,2,1,0:T(8,128)S(1)}) fusion(f32[4,12,128,256]{3,2,1,0:T(8,128)} %copy-done.2, f32[4,12,128]{2,1,0:T(8,128)S(1)} %copy-done.36, bf16[4,128,12,64]{1,3,2,0:T(8,128)(2,1)S(1)} %bitcast.139, bf16[4,128,12,64]{1,3,2,0:T(8,128)(2,1)} %bitcast.146, ...), kind=kOutput, calls=%fused_computation.11 | convolution fusion | flops 213116928 | bytes 14991361 | tf_op jit(solution)/shard_map/sqhe,skhe->shqk/dot_general | solution.py:535
  113.4 2.7 fusion.16
  116.1 2.3 multiply_convert_fusion
  119.8 2.1 convert_reduce_fusion.5
  121.9 1.9 bitcast_convert_fusion.2
  123.8 1.9 fusion.71
  125.7 1.9 copy.87
  127.6 3.6 copy.86
  131.1 3.8 %fusion.72 = (f32[4,128,768]{1,2,0:T(8,128)}, f32[4,128,768]{1,2,0:T(8,128)}) fusion(f32[4,256,768]{1,2,0:T(8,128)} %bitcast.138), kind=kLoop, calls=%fused_computation.152 | loop fusion | bytes 6291456 | tf_op jit(solution)/shard_map/slice | solution.py:557
  134.9 3.0 copy.88
  137.9 3.0 copy.89
  141.0 1.7 fusion.55
  142.7 1.3 pad_maximum_fusion.2
  144.0 2.2 collective-permute-start.1
  146.2 1.9 fusion.40
  148.1 1.4 constant_dynamic-update-slice_fusion.8
  149.5 2.0 fusion.47
  151.5 6.9 %bitcast_convert_fusion.1.g_outer = bf16[3072,768]{1,0:T(8,128)(2,1)} fusion(bf16[4,128,3072]{2,1,0:T(8,128)(2,1)} %copy-done.17, bf16[4,128,768]{2,1,0:T(8,128)(2,1)S(1)} %copy-done.33), kind=kOutput, calls=%fused_computation.2 | convolution fusion | flops 2418278400 | bytes 8650752 | tf_op jit(solution)/shard_map/try,tro->yo/dot_general | solution.py:413
  158.4 5.0 %bitcast_convert_fusion.g_inner = bf16[768,3072]{1,0:T(8,128)(2,1)} fusion(bf16[4,128,3072]{2,1,0:T(8,128)(2,1)S(1)} %copy-done.59, f32[4,128,768]{2,1,0:T(8,128)S(1)} %copy-done.4, f32[768]{0:T(1024)S(1)} %copy-done.49, f32[768]{0:T(1024)S(1)} %copy-done.37, f32[4,128]{1,0:T(4,128)S(1)} %add_rsqrt_fusion.1, f32[4,128]{1,0:T(4,128)S(1)} %broadcast_multiply_fusion.5), kind=kOutput, calls=%fused_computation.1 | convolution fusion | flops 2420244480 | bytes 9447424 | tf_op jit(solution)/shard_map/try,tro->yo/dot_general | solution.py:413
  163.5 16.6 %collective-permute-done.1 = bf16[2,4,128,768]{3,2,1,0:T(8,128)(2,1)} collective-permute-done((bf16[2,4,128,768]{3,2,1,0:T(8,128)(2,1)}, bf16[2,4,128,768]{3,2,1,0:T(8,128)(2,1)}, u32[]{:S(2)}, u32[]{:S(2)}) %collective-permute-start.1) | collective-permute-done | bytes 1572896 | tf_op jit(solution)/shard_map/ppermute | solution.py:394
  180.0 1.7 convert_element_type.190
  183.0 2.0 fusion.50
  185.1 1.8 fusion.41
  187.0 1.8 fusion.42
  188.8 1.3 constant_dynamic-update-slice_fusion.7
  190.1 1.3 constant_dynamic-update-slice_fusion.6
  191.4 1.3 constant_dynamic-update-slice_fusion.5
  192.7 1.3 constant_dynamic-update-slice_fusion.4
  194.0 1.3 constant_dynamic-update-slice_fusion.3
  195.3 1.3 constant_dynamic-update-slice_fusion.2
  196.6 1.3 constant_dynamic-update-slice_fusion.1
  197.9 1.3 constant_dynamic-update-slice_fusion
  199.8 1.4 reshape.146.small_in
  201.2 4.9 %pad_maximum_fusion.g_attn = bf16[3072,768]{1,0:T(8,128)(2,1)} fusion(bf16[768,768]{1,0:T(8,128)(2,1)S(1)} %copy-done.23, bf16[768,768]{1,0:T(8,128)(2,1)} %fusion.42, bf16[768,768]{1,0:T(8,128)(2,1)} %fusion.41, bf16[768,768]{1,0:T(8,128)(2,1)} %fusion.40), kind=kLoop, calls=%fused_computation.32 | loop fusion | flops 18874368 | bytes 9437184 | tf_op jit(solution)/shard_map/concatenate | solution.py:580
  206.1 132.9 %shard_map.314 = (bf16[3072,768]{1,0:T(8,128)(2,1)}, bf16[768,3072]{1,0:T(8,128)(2,1)}, bf16[3072,768]{1,0:T(8,128)(2,1)}, f32[16,768]{1,0:T(8,128)}) custom-call(bf16[3072,768]{1,0:T(8,128)(2,1)} %bitcast_convert_fusion.1.g_outer, bf16[768,3072]{1,0:T(8,128)(2,1)} %bitcast_convert_fusion.g_inner, bf16[3072,768]{1,0:T(8,128)(2,1)} %pad_maximum_fusion.g_attn, ...), custom_call_target="tpu_custom_call" | custom-call | tf_op jit(solution)/shard_map/pallas_call | solution.py:358
  339.0 1.7 slice_reduce_fusion
  341.5 6.3 %fusion.70 = (f32[768,768]{1,0:T(8,128)}, f32[768,768]{1,0:T(8,128)}, f32[768,768]{1,0:T(8,128)}, f32[768,768]{1,0:T(8,128)}) fusion(bf16[3072,768]{1,0:T(8,128)(2,1)} %get-tuple-element.21), kind=kLoop, calls=%fused_computation.150 | loop fusion | bytes 18874368 | tf_op jit(solution)/shard_map/slice | solution.py:599
  347.9 5.0 %convert_element_type.209 = f32[768,3072]{1,0:T(8,128)} convert(bf16[768,3072]{1,0:T(8,128)(2,1)S(1)} %copy-done.14) | non-fusion elementwise | flops 2359296 | bytes 14155776 | tf_op jit(solution)/shard_map/convert_element_type | solution.py:603
  353.6 7.0 %convert_element_type.210 = f32[3072,768]{1,0:T(8,128)} convert(bf16[3072,768]{1,0:T(8,128)(2,1)} %get-tuple-element.24) | non-fusion elementwise | flops 2359296 | bytes 14155776 | tf_op jit(solution)/shard_map/convert_element_type | solution.py:605
  360.6 2.0 add_convert_fusion.1
  (167 shorter events, 16.7 us)
Async XLA Ops:
  0.7 58.5 %copy-start = (bf16[768,768]{1,0:T(8,128)(2,1)S(1)}, bf16[768,768]{1,0:T(8,128)(2,1)}, u32[]{:S(2)}) copy-start(bf16[768,768]{1,0:T(8,128)(2,1)} %param.27) | copy-start | bytes 3538948
  0.7 3.2 copy-start.24
  0.7 3.2 copy-start.21
  6.0 4.5 %copy-start.53 = (bf16[768]{0:T(1024)(128)(2,1)S(1)}, bf16[768]{0:T(1024)(128)(2,1)}, u32[]{:S(2)}) copy-start(bf16[768]{0:T(1024)(128)(2,1)} %param.34) | copy-start | bytes 4612
  6.0 5.9 %copy-start.54 = (bf16[768]{0:T(1024)(128)(2,1)S(1)}, bf16[768]{0:T(1024)(128)(2,1)}, u32[]{:S(2)}) copy-start(bf16[768]{0:T(1024)(128)(2,1)} %param.28) | copy-start | bytes 4612
  6.0 37.7 %collective-permute-start = (bf16[2,4,128,768]{3,2,1,0:T(8,128)(2,1)}, bf16[2,4,128,768]{3,2,1,0:T(8,128)(2,1)}, u32[]{:S(2)}, u32[]{:S(2)}) collective-permute-start(bf16[2,4,128,768]{3,2,1,0:T(8,128)(2,1)} %pad_maximum_fusion.1), channel_id=1, source_target_pairs={{0,1},{1,0},{2,3},{3,2},{4,5},{5,4},{6,7},{7,6},{8,9},{9,8},{10,11... | collective-permute-start | bytes 4718600 | tf_op jit(solution)/shard_map/ppermute | solution.py:394
  10.5 45.3 %copy-start.15 = (bf16[4,128,768]{1,2,0:T(8,128)(2,1)}, bf16[4,128,768]{1,2,0:T(8,128)(2,1)S(1)}, u32[]{:S(2)}) copy-start(bf16[4,128,768]{1,2,0:T(8,128)(2,1)S(1)} %copy.60) | copy-start | bytes 2359300
  13.1 4.5 %copy-start.55 = (bf16[768]{0:T(1024)(128)(2,1)S(1)}, bf16[768]{0:T(1024)(128)(2,1)}, u32[]{:S(2)}) copy-start(bf16[768]{0:T(1024)(128)(2,1)} %param.30) | copy-start | bytes 4612
  17.6 31.1 %copy-start.12 = (bf16[4,128,768]{1,2,0:T(8,128)(2,1)}, bf16[4,128,768]{1,2,0:T(8,128)(2,1)S(1)}, u32[]{:S(2)}) copy-start(bf16[4,128,768]{1,2,0:T(8,128)(2,1)S(1)} %copy.62) | copy-start | bytes 2359300
  48.6 7.2 %copy-start.16 = (bf16[1,4,128,768]{2,3,1,0:T(8,128)(2,1)}, bf16[1,4,128,768]{2,3,1,0:T(8,128)(2,1)S(1)}, u32[]{:S(2)}) copy-start(bf16[1,4,128,768]{2,3,1,0:T(8,128)(2,1)S(1)} %copy.61) | copy-start | bytes 2359300
  52.8 3.2 copy-start.2
  52.8 7.8 %slice-start.4 = ((s8[4718592]{0:T(1024)(128)(4,1)}), s8[4194304]{0:T(1024)(128)(4,1)S(1)}, s32[]{:S(2)}) async-start(s8[4718592]{0:T(1024)(128)(4,1)} %bitcast.157), calls=%async_computation.4 | async-start | bytes 8388608
  56.0 3.2 copy-start.25
  56.0 3.2 copy-start.47
  56.0 4.6 %slice-start.5 = ((s8[4718592]{0:T(1024)(128)(4,1)}), s8[524288]{0:T(1024)(128)(4,1)S(1)}, s32[]{:S(2)}) async-start(s8[4718592]{0:T(1024)(128)(4,1)} %bitcast.157), calls=%async_computation.5 | async-start | bytes 1048576
  59.2 1.4 copy-start.28
  59.2 1.4 copy-start.37
  59.2 1.4 copy-start.49
  60.2 42.3 %copy-start.3 = (f32[4,128,768]{2,1,0:T(8,128)}, f32[4,128,768]{2,1,0:T(8,128)S(1)}, u32[]{:S(2)}) copy-start(f32[4,128,768]{2,1,0:T(8,128)S(1)} %get-tuple-element.66) | copy-start | bytes 4718596
  60.2 98.2 %copy-start.39 = (f32[4,128]{1,0:T(4,128)}, f32[4,128]{1,0:T(4,128)S(1)}, u32[]{:S(2)}) copy-start(f32[4,128]{1,0:T(4,128)S(1)} %broadcast_multiply_fusion.5) | copy-start | bytes 6148
  60.2 19.4 %slice-start.2 = ((s8[4718592]{0:T(1024)(128)(4,1)}), s8[524288]{0:T(1024)(128)(4,1)S(1)}, s32[]{:S(2)}) async-start(s8[4718592]{0:T(1024)(128)(4,1)} %bitcast.155), calls=%async_computation.2 | async-start | bytes 1048576
  60.6 97.8 %copy-start.41 = (f32[4,128]{1,0:T(4,128)}, f32[4,128]{1,0:T(4,128)S(1)}, u32[]{:S(2)}) copy-start(f32[4,128]{1,0:T(4,128)S(1)} %add_rsqrt_fusion.1) | copy-start | bytes 6148
  60.6 19.0 %slice-start.3 = ((s8[4718592]{0:T(1024)(128)(4,1)}), s8[4194304]{0:T(1024)(128)(4,1)S(1)}, s32[]{:S(2)}) async-start(s8[4718592]{0:T(1024)(128)(4,1)} %bitcast.155), calls=%async_computation.3 | async-start | bytes 8388608
  65.1 14.5 %copy-start.50 = (f32[768]{0:T(1024)S(1)}, f32[768]{0:T(1024)}, u32[]{:S(2)}) copy-start(f32[768]{0:T(1024)} %convert_element_type.176) | copy-start | bytes 9220
  79.6 2.9 copy-start.17
  79.6 3.2 copy-start.18
  82.5 1.6 copy-start.46
  86.3 8.9 %copy-start.32 = (bf16[4,128,768]{2,1,0:T(8,128)(2,1)}, bf16[4,128,768]{2,1,0:T(8,128)(2,1)S(1)}, u32[]{:S(2)}) copy-start(bf16[4,128,768]{2,1,0:T(8,128)(2,1)S(1)} %get-tuple-element.44) | copy-start | bytes 2359300
  103.9 3.2 copy-start.36
  103.9 9.4 %slice-start = ((s8[6291456]{0:T(1024)(128)(4,1)}), s8[2097152]{0:T(1024)(128)(4,1)S(1)}, s32[]{:S(2)}) async-start(s8[6291456]{0:T(1024)(128)(4,1)} %bitcast.135), calls=%async_computation | async-start | bytes 4194304
  107.1 6.2 %slice-start.1 = ((s8[6291456]{0:T(1024)(128)(4,1)}), s8[4194304]{0:T(1024)(128)(4,1)S(1)}, s32[]{:S(2)}) async-start(s8[6291456]{0:T(1024)(128)(4,1)} %bitcast.135), calls=%async_computation.1 | async-start | bytes 8388608
  116.1 2.3 copy-start.13
  118.4 1.4 copy-start.31
  119.8 2.1 copy-start.29
  119.8 2.1 copy-start.35
  127.5 13.4 %copy-start.5 = (f32[4,128,768]{2,1,0:T(8,128)}, f32[4,128,768]{2,1,0:T(8,128)S(1)}, u32[]{:S(2)}) copy-start(f32[4,128,768]{2,1,0:T(8,128)S(1)} %copy.87) | copy-start | bytes 4718596
  142.7 3.5 copy-start.26
  142.7 3.5 copy-start.58
  144.0 5.5 %copy-start.56 = (bf16[768,768]{1,0:T(8,128)(2,1)S(1)}, bf16[768,768]{1,0:T(8,128)(2,1)}, u32[]{:S(2)}) copy-start(bf16[768,768]{1,0:T(8,128)(2,1)} %param.22) | copy-start | bytes 3538948
  144.0 36.1 %collective-permute-start.1 = (bf16[2,4,128,768]{3,2,1,0:T(8,128)(2,1)}, bf16[2,4,128,768]{3,2,1,0:T(8,128)(2,1)}, u32[]{:S(2)}, u32[]{:S(2)}) collective-permute-start(bf16[2,4,128,768]{3,2,1,0:T(8,128)(2,1)} %pad_maximum_fusion.2), channel_id=1, source_target_pairs={{0,1},{1,0},{2,3},{3,2},{4,5},{5,4},{6,7},{7,6},{8,9},{9,8},{10,11... | collective-permute-start | bytes 4718600 | tf_op jit(solution)/shard_map/ppermute | solution.py:394
  148.1 3.4 copy-start.33
  151.5 6.9 %copy-start.4 = (f32[4,128,768]{2,1,0:T(8,128)S(1)}, f32[4,128,768]{2,1,0:T(8,128)}, u32[]{:S(2)}) copy-start(f32[4,128,768]{2,1,0:T(8,128)} %copy-done.3) | copy-start | bytes 4718596
  151.5 6.9 %copy-start.59 = (bf16[4,128,3072]{2,1,0:T(8,128)(2,1)S(1)}, bf16[4,128,3072]{2,1,0:T(8,128)(2,1)}, u32[]{:S(2)}) copy-start(bf16[4,128,3072]{2,1,0:T(8,128)(2,1)} %get-tuple-element.76) | copy-start | bytes 9437188
  158.4 23.4 %copy-start.9 = (f32[4,128,768]{2,1,0:T(8,128)S(1)}, f32[4,128,768]{2,1,0:T(8,128)}, u32[]{:S(2)}) copy-start(f32[4,128,768]{2,1,0:T(8,128)} %copy.89) | copy-start | bytes 4718596
  163.4 18.3 %copy-start.6 = (f32[4,128,768]{2,1,0:T(8,128)S(1)}, f32[4,128,768]{2,1,0:T(8,128)}, u32[]{:S(2)}) copy-start(f32[4,128,768]{2,1,0:T(8,128)} %copy-done.5) | copy-start | bytes 4718596
  163.4 18.3 %copy-start.7 = (f32[4,128,768]{2,1,0:T(8,128)S(1)}, f32[4,128,768]{2,1,0:T(8,128)}, u32[]{:S(2)}) copy-start(f32[4,128,768]{2,1,0:T(8,128)} %copy.86) | copy-start | bytes 4718596
  163.4 18.3 %copy-start.8 = (f32[4,128,768]{2,1,0:T(8,128)S(1)}, f32[4,128,768]{2,1,0:T(8,128)}, u32[]{:S(2)}) copy-start(f32[4,128,768]{2,1,0:T(8,128)} %copy.88) | copy-start | bytes 4718596
  182.7 2.3 copy-start.27
  186.9 4.5 %copy-start.52 = (f32[768]{0:T(1024)S(1)}, f32[768]{0:T(1024)}, u32[]{:S(2)}) copy-start(f32[768]{0:T(1024)} %get-tuple-element.27) | copy-start | bytes 9220
  186.9 5.8 %copy-start.51 = (f32[768]{0:T(1024)S(1)}, f32[768]{0:T(1024)}, u32[]{:S(2)}) copy-start(f32[768]{0:T(1024)} %get-tuple-element.32) | copy-start | bytes 9220
  186.9 7.1 %copy-start.48 = (f32[3072]{0:T(1024)S(1)}, f32[3072]{0:T(1024)}, u32[]{:S(2)}) copy-start(f32[3072]{0:T(1024)} %get-tuple-element.75) | copy-start | bytes 36868
  186.9 8.4 %copy-start.45 = (f32[768]{0:T(1024)S(1)}, f32[768]{0:T(1024)}, u32[]{:S(2)}) copy-start(f32[768]{0:T(1024)} %get-tuple-element.43) | copy-start | bytes 9220
  186.9 9.7 %copy-start.44 = (f32[768]{0:T(1024)S(1)}, f32[768]{0:T(1024)}, u32[]{:S(2)}) copy-start(f32[768]{0:T(1024)} %get-tuple-element.29) | copy-start | bytes 9220
  186.9 11.0 %copy-start.43 = (f32[768]{0:T(1024)S(1)}, f32[768]{0:T(1024)}, u32[]{:S(2)}) copy-start(f32[768]{0:T(1024)} %get-tuple-element.34) | copy-start | bytes 9220
  187.0 14.3 %copy-start.23 = (bf16[768,768]{1,0:T(8,128)(2,1)S(1)}, bf16[768,768]{1,0:T(8,128)(2,1)}, u32[]{:S(2)}) copy-start(bf16[768,768]{1,0:T(8,128)(2,1)} %bitcast_convert_fusion.2) | copy-start | bytes 3538948
  341.5 6.3 %copy-start.14 = (bf16[768,3072]{1,0:T(8,128)(2,1)S(1)}, bf16[768,3072]{1,0:T(8,128)(2,1)}, u32[]{:S(2)}) copy-start(bf16[768,3072]{1,0:T(8,128)(2,1)} %get-tuple-element.23) | copy-start | bytes 14155780
  353.5 7.0 %copy-start.11 = (f32[4,128,768]{2,1,0:T(8,128)S(1)}, f32[4,128,768]{2,1,0:T(8,128)}, u32[]{:S(2)}) copy-start(f32[4,128,768]{2,1,0:T(8,128)} %copy-done.10) | copy-start | bytes 4718596
  353.5 7.0 %copy-start.19 = (f32[4,128,768]{2,1,0:T(8,128)S(1)}, f32[4,128,768]{2,1,0:T(8,128)}, u32[]{:S(2)}) copy-start(f32[4,128,768]{2,1,0:T(8,128)} %fusion.47) | copy-start | bytes 4718596
  353.5 7.0 %copy-start.20 = (f32[4,128,768]{2,1,0:T(8,128)S(1)}, f32[4,128,768]{2,1,0:T(8,128)}, u32[]{:S(2)}) copy-start(f32[4,128,768]{2,1,0:T(8,128)} %fusion.50) | copy-start | bytes 4718596
  353.5 7.0 %copy-start.22 = (bf16[768,768]{1,0:T(8,128)(2,1)S(1)}, bf16[768,768]{1,0:T(8,128)(2,1)}, u32[]{:S(2)}) copy-start(bf16[768,768]{1,0:T(8,128)(2,1)} %param.25) | copy-start | bytes 3538948
  353.5 7.0 %copy-start.38 = (f32[768]{0:T(1024)S(1)}, f32[768]{0:T(1024)}, u32[]{:S(2)}) copy-start(f32[768]{0:T(1024)} %convert_element_type.171) | copy-start | bytes 9220
  353.5 7.0 %copy-start.40 = (f32[4,128]{1,0:T(4,128)S(1)}, f32[4,128]{1,0:T(4,128)}, u32[]{:S(2)}) copy-start(f32[4,128]{1,0:T(4,128)} %copy-done.39) | copy-start | bytes 6148
  353.5 7.0 %copy-start.42 = (f32[4,128]{1,0:T(4,128)S(1)}, f32[4,128]{1,0:T(4,128)}, u32[]{:S(2)}) copy-start(f32[4,128]{1,0:T(4,128)} %copy-done.41) | copy-start | bytes 6148
  353.5 9.0 %copy-start.1 = (bf16[768,768]{1,0:T(8,128)(2,1)S(1)}, bf16[768,768]{1,0:T(8,128)(2,1)}, u32[]{:S(2)}) copy-start(bf16[768,768]{1,0:T(8,128)(2,1)} %param.27) | copy-start | bytes 3538948
  (4 other events, 4.4 us)

commit v2 on v1

--- a/solution.py
+++ b/solution.py
@@ -7,7 +7,6 @@
 from jax.experimental.pallas import tpu as pltpu
 from jax.sharding import PartitionSpec as P
 
-HEADS = 12
 MESH = pl.DeviceIdType.MESH
 ROWS = 256
 LANES = 768
@@ -281,31 +280,57 @@
 
 
 def block_of(refs, half, t):
-    outer, inner, attn = refs
+    outer, inner = refs[:2]
     if t < 6:
         return outer.at[pl.ds(pl.multiple_of(half * 1536 + t * ROWS, ROWS), ROWS), :]
     if t < 12:
         i, j = (t - 6) % 3, (t - 6) // 3
         return inner.at[pl.ds(i * ROWS, ROWS), pl.ds(pl.multiple_of((half * 2 + j) * LANES, LANES), LANES)]
-    return attn.at[pl.ds(pl.multiple_of(half * 1536 + (t - 12) * ROWS, ROWS), ROWS), :]
-
-
-def sum_kernel(extra_bits, g_outer, g_inner, g_attn, small_in, s_outer, s_inner, s_attn, small_out,
-               acc, sib, fin, rb, small, small_rb, ssem, rsem, lsem, vsem):
+    return None
+
+
+def attn_block(refs, half, t):
+    ref = refs[2 + 2 * half + (t - 12) // 3]
+    return ref.at[pl.ds((t - 12) % 3 * ROWS, ROWS), :]
+
+
+class Branches:
+    def __init__(self, core, first, second):
+        self.core, self.first, self.second = core, first, second
+
+    def start(self):
+        for core, copy in ((0, self.first), (1, self.second)):
+            @pl.when(self.core == core)
+            def _(copy=copy):
+                copy().start()
+
+    def wait(self):
+        self.first().wait()
+
+
+def sum_kernel(extra_bits, *refs):
+    ins, vectors, refs = refs[:6], refs[6:15], refs[15:]
+    outs, small_out, refs = refs[:6], refs[6], refs[7:]
+    acc, sib, fin, rb, small, small_rb, ssem, rsem, lsem, vsem = refs
     w = Wire(extra_bits)
     count = len(KINDS)
-    ins, outs = (g_outer, g_inner, g_attn), (s_outer, s_inner, s_attn)
+
+    def block_copy(arrays, own, t, buf, outward, sem):
+        def copy(block):
+            return pltpu.make_async_copy(buf, block, sem) if outward else pltpu.make_async_copy(block, buf, sem)
+
+        if t < 12:
+            return copy(block_of(arrays, w.core if own else 1 - w.core, t))
+        low, high = attn_block(arrays, 0, t), attn_block(arrays, 1, t)
+        return Branches(w.core, lambda: copy(low if own else high), lambda: copy(high if own else low))
 
     def load(t, who):
-        half, buf = (w.core, acc) if who == 0 else (1 - w.core, sib)
-        return pltpu.make_async_copy(block_of(ins, half, t), buf.at[pl.ds(t * ROWS, ROWS), :], lsem.at[2 * t + who])
+        buf = (acc, sib)[who].at[pl.ds(t * ROWS, ROWS), :]
+        return block_copy(ins, who == 0, t, buf, False, lsem.at[2 * t + who])
 
     def store(t, who):
-        if who == 0:
-            half, source = w.core, rb.at[pl.ds(tasks.homes[t], ROWS), :]
-        else:
-            half, source = 1 - w.core, fin.at[pl.ds(t * ROWS, ROWS), :]
-        return pltpu.make_async_copy(source, block_of(outs, half, t), lsem.at[2 * t + who])
+        source = rb.at[pl.ds(tasks.homes[t], ROWS), :] if who == 0 else fin.at[pl.ds(t * ROWS, ROWS), :]
+        return block_copy(outs, who == 0, t, source, True, lsem.at[2 * t + who])
 
     for t in range(count):
         load(t, 1).start()
@@ -313,7 +338,10 @@
     w.barrier()
     tasks = Tasks(w, KINDS, acc, sib, fin, rb, ssem, rsem)
 
-    small[0] = small_in[...]
+    for at, ref in enumerate(vectors):
+        for i in range(ref.shape[1] // LANES):
+            small[0, at + i:at + i + 1, :] = ref[:, i * LANES:(i + 1) * LANES]
+    small[0, 12:16, :] = jnp.zeros((4, LANES), jnp.float32)
     hops = ["core", "x", "y"] + list(range(2, 4 + extra_bits))
 
     def small_copy(k):
@@ -348,7 +376,7 @@
         store(t, 1).wait()
 
 
-def sum_gradients(g_outer, g_inner, g_attn, small_in):
+def sum_gradients(matrices, vectors):
     extra_bits = (lax.axis_size("batch") // 16).bit_length() - 1
     rows, sems = plan_sizes(KINDS, extra_bits)
     hops = 5 + extra_bits
@@ -357,14 +385,10 @@
     vmem = pl.BlockSpec(memory_space=pltpu.VMEM)
     return pl.pallas_call(
         functools.partial(sum_kernel, extra_bits),
-        out_shape=(
-            jax.ShapeDtypeStruct(g_outer.shape, jnp.bfloat16),
-            jax.ShapeDtypeStruct(g_inner.shape, jnp.bfloat16),
-            jax.ShapeDtypeStruct(g_attn.shape, jnp.bfloat16),
-            jax.ShapeDtypeStruct(small_in.shape, jnp.float32),
-        ),
-        in_specs=[hbm, hbm, hbm, vmem],
-        out_specs=(hbm, hbm, hbm, vmem),
+        out_shape=tuple(jax.ShapeDtypeStruct(m.shape, jnp.bfloat16) for m in matrices)
+        + (jax.ShapeDtypeStruct((SMALL, LANES), jnp.float32),),
+        in_specs=[hbm] * len(matrices) + [vmem] * len(vectors),
+        out_specs=(hbm,) * len(matrices) + (vmem,),
         scratch_shapes=[
             pltpu.VMEM((count * ROWS, LANES), jnp.bfloat16),
             pltpu.VMEM((count * ROWS, LANES), jnp.bfloat16),
@@ -378,45 +402,139 @@
             pltpu.SemaphoreType.DMA((2, hops)),
         ],
         compiler_params=pltpu.CompilerParams(collective_id=1, has_side_effects=True, vmem_limit_bytes=60 << 20),
-    )(g_outer, g_inner, g_attn, small_in)
+    )(*matrices, *vectors)
+
+
+def nt(a, b):
+    return lax.dot_general(a, b, (((1,), (1,)), ((), ())), preferred_element_type=jnp.float32)
+
+
+def nn(a, b):
+    return lax.dot_general(a, b, (((1,), (0,)), ((), ())), preferred_element_type=jnp.float32)
+
+
+def low_lanes(rows):
+    return lax.broadcasted_iota(jnp.int32, (rows, 128), 1) < 64
+
+
+def attend_pair(q, k, v, bias):
+    low = low_lanes(k.shape[0])
+    zero = jnp.zeros_like(k)
+    vt = v.T
+    parts, sums = [], []
+    for head in range(2):
+        own = jnp.where(low if head == 0 else ~low, k, zero)
+        scores = nt(own, q) + bias
+        top = jnp.max(scores, axis=0, keepdims=True)
+        expo = jnp.exp(scores - top)
+        total = jnp.sum(expo, axis=0, keepdims=True)
+        parts.append(nn(vt[head * 64:head * 64 + 64], expo.astype(jnp.bfloat16)) * (1.0 / total))
+        sums.append(top + jnp.log(total))
+    return jnp.concatenate(parts, axis=0).T.astype(jnp.bfloat16), jnp.concatenate(sums, axis=0)
+
+
+def attend_pair_back(q, k, v, dc, lse, bias):
+    low = low_lanes(k.shape[0])
+    zero = jnp.zeros_like(k)
+    kt = k.T
+    dq, dk, dv = [], [], []
+    for head in range(2):
+        mine = low if head == 0 else ~low
+        probs = jnp.exp(nt(jnp.where(mine, k, zero), q) + (bias - lse[head:head + 1]))
+        d_probs = nt(jnp.where(mine, v, zero), dc)
+        inner = jnp.sum(probs * d_probs, axis=0, keepdims=True)
+        d_scores = (probs * (d_probs - inner)).astype(jnp.bfloat16)
+        dq.append(nn(kt[head * 64:head * 64 + 64], d_scores))
+        dk.append(nn(d_scores, q))
+        dv.append(nn(probs.astype(jnp.bfloat16), dc))
+    d_query = (jnp.concatenate(dq, axis=0) * 0.125).T.astype(jnp.bfloat16)
+    d_key = jnp.where(low, dk[0], dk[1]).astype(jnp.bfloat16)
+    d_value = jnp.where(low, dv[0], dv[1]).astype(jnp.bfloat16)
+    return d_query, d_key, d_value
+
+
+def attend_kernel(q_ref, k_ref, v_ref, bias_ref, ctx_ref, lse_ref):
+    bias = jnp.concatenate([bias_ref[...]] * (q_ref.shape[0] // 128), axis=1)
+    ctx_ref[...], lse_ref[0, 0] = attend_pair(q_ref[...], k_ref[...], v_ref[...], bias)
+
+
+def attend_back_kernel(q_ref, k_ref, v_ref, dc_ref, lse_ref, bias_ref, dq_ref, dk_ref, dv_ref):
+    bias = jnp.concatenate([bias_ref[...]] * (q_ref.shape[0] // 128), axis=1)
+    dq_ref[...], dk_ref[...], dv_ref[...] = attend_pair_back(
+        q_ref[...], k_ref[...], v_ref[...], dc_ref[...], lse_ref[0, 0], bias)
+
+
+def attend(q, k, v, bias, length):
+    rows, width = q.shape
+    seqs, pairs = rows // length, width // 128
+    block = pl.BlockSpec((length, 128), lambda s, p: (s, p))
+    mask = pl.BlockSpec((length, 128), lambda s, p: (s, 0))
+    lse = pl.BlockSpec((1, 1, 2, length), lambda s, p: (s, p, 0, 0))
+    return pl.pallas_call(
+        attend_kernel,
+        grid=(seqs, pairs),
+        out_shape=(jax.ShapeDtypeStruct(q.shape, jnp.bfloat16), jax.ShapeDtypeStruct((seqs, pairs, 2, length), jnp.float32)),
+        in_specs=[block, block, block, mask],
+        out_specs=(block, lse),
+    )(q, k, v, bias)
+
+
+def attend_back(q, k, v, dc, lse, bias, length):
+    rows, width = q.shape
+    seqs, pairs = rows // length, width // 128
+    block = pl.BlockSpec((length, 128), lambda s, p: (s, p))
+    mask = pl.BlockSpec((length, 128), lambda s, p: (s, 0))
+    lse_spec = pl.BlockSpec((1, 1, 2, length), lambda s, p: (s, p, 0, 0))
+    return pl.pallas_call(
+        attend_back_kernel,
+        grid=(seqs, pairs),
+        out_shape=tuple(jax.ShapeDtypeStruct(q.shape, jnp.bfloat16) for _ in range(3)),
+        in_specs=[block, block, block, block, lse_spec, mask],
+        out_specs=(block, block, block),
+    )(q, k, v, dc, lse, bias)
 
 
 epsilon = 1e-05
 
 
-def partner_2(block, axis, distance):
-    count = lax.axis_size(axis)
-    route = []
-    for low in range(count):
-        high = low | 1 << distance
-        if high != low and high < count:
-            route += [(low, high), (high, low)]
-    return lax.ppermute(block, axis, route)
+def to_partner(block):
+    return lax.ppermute(block, "mod", [(0, 1), (1, 0)])
+
+
+def take_side(array, axis, side):
+    half = array.shape[axis] // 2
+    return lax.dynamic_slice_in_dim(array, side * half, half, axis)
+
+
+def gather_sequences(array, side):
+    own = take_side(array, 0, side)
+    other = to_partner(take_side(array, 0, 1 - side))
+    both = jnp.where(side == 0, jnp.concatenate((own, other), axis=1), jnp.concatenate((other, own), axis=1))
+    return both.reshape(-1, array.shape[2])
+
+
+def return_rows(array, side):
+    own = take_side(array, 1, side)
+    other = to_partner(take_side(array, 1, 1 - side))
+    return jnp.where(side == 0, jnp.concatenate((own, other)), jnp.concatenate((other, own)))
 
 
 def linear(rows, weight_matrix):
+    return lax.dot_general(rows, weight_matrix, (((1,), (0,)), ((), ())), preferred_element_type=jnp.float32)
+
+
+def back_linear(gradient_rows, weight_matrix):
+    return lax.dot_general(gradient_rows, weight_matrix, (((1,), (1,)), ((), ())), preferred_element_type=jnp.float32)
+
+
+def weight_grad(layer_inputs, gradient_rows):
     return lax.dot_general(
-        rows,
-        weight_matrix,
-        (((rows.ndim - 1,), (0,)), ((), ())),
-        preferred_element_type=jnp.float32,
-    )
-
-
-def back_linear(gradient_row_block, weight_matrix):
-    return jnp.einsum(
-        "nhr,gr->nhg", gradient_row_block, weight_matrix, preferred_element_type=jnp.float32
-    )
-
-
-def weight_grad(layer_inputs, gradient_row_block):
-    return jnp.einsum(
-        "try,tro->yo", layer_inputs, gradient_row_block, preferred_element_type=jnp.float32
-    )
+        layer_inputs, gradient_rows, (((0,), (0,)), ((), ())), preferred_element_type=jnp.float32
+    ).astype(jnp.bfloat16)
 
 
 def row_total(values):
-    return jnp.sum(values.astype(jnp.float32), axis=(0, 1))
+    return jnp.sum(values.astype(jnp.float32), axis=0, keepdims=True)
 
 
 def layer_norm(rows):
@@ -425,11 +543,11 @@
     return (centre * factor, factor)
 
 
-def norm_back(gradient_row_block, normed, factor):
+def norm_back(gradient_rows, normed, factor):
     return factor * (
-        gradient_row_block
-        - jnp.mean(gradient_row_block, axis=-1, keepdims=True)
-        - normed * jnp.mean(gradient_row_block * normed, axis=-1, keepdims=True)
+        gradient_rows
+        - jnp.mean(gradient_rows, axis=-1, keepdims=True)
+        - normed * jnp.mean(gradient_rows * normed, axis=-1, keepdims=True)
     )
 
 
@@ -455,65 +573,35 @@
     cotangent,
 ):
     seq_count, half_len, width = hidden_in.shape
-    head_size = width // HEADS
-    factor_qk = 1.0 / jnp.sqrt(jnp.float32(head_size))
-    text_half = lax.axis_index("mod") == 0
-    rows_in = hidden_in.astype(jnp.float32)
-    query = linear(hidden_in, w_query) + b_query.astype(jnp.float32)
-    query_b = query.astype(jnp.bfloat16)
-    key_b = linear(hidden_in, w_key).astype(jnp.bfloat16)
-    value_b = (linear(hidden_in, w_value) + b_value.astype(jnp.float32)).astype(jnp.bfloat16)
-    partner = partner_2(jnp.stack((key_b, value_b)), "mod", 0)
-    all_keys = jnp.where(
-        text_half,
-        jnp.concatenate((key_b, partner[0]), axis=1),
-        jnp.concatenate((partner[0], key_b), axis=1),
-    )
-    all_values = jnp.where(
-        text_half,
-        jnp.concatenate((value_b, partner[1]), axis=1),
-        jnp.concatenate((partner[1], value_b), axis=1),
-    )
-    slot_ok = lax.broadcasted_iota(jnp.int32, (seq_count, half_len), 1) < region_count[:, None]
-    valid = jnp.concatenate((text_mask == 1, slot_ok), axis=1)[:, None, None, :]
-    query_h = query_b.reshape(seq_count, half_len, HEADS, head_size)
-    key_h = all_keys.reshape(seq_count, 2 * half_len, HEADS, head_size)
-    value_h = all_values.reshape(seq_count, 2 * half_len, HEADS, head_size)
-
-    def masked_scores():
-        scores = (
-            jnp.einsum("sqhe,skhe->shqk", query_h, key_h, preferred_element_type=jnp.float32)
-            * factor_qk
-        )
-        return jnp.where(valid, scores, jnp.float32(-1000000000.0))
-
-    masked = masked_scores()
-    highest = jnp.max(masked, axis=-1, keepdims=True)
-    expo = jnp.exp(masked - highest)
-    totals = jnp.sum(expo, axis=-1, keepdims=True)
-    log_total = highest + jnp.log(totals)
-    probs_b = (expo / totals).astype(jnp.bfloat16)
-    context_b = (
-        jnp.einsum("shqk,skhe->sqhe", probs_b, value_h, preferred_element_type=jnp.float32)
-        .reshape(seq_count, half_len, width)
-        .astype(jnp.bfloat16)
-    )
-    branch = linear(context_b, w_attn_out) + b_attn_out.astype(jnp.float32)
-    normed_one, factor_one = layer_norm(rows_in + branch)
-    middle = normed_one * gain_attn.astype(jnp.float32) + shift_attn.astype(jnp.float32)
+    length = 2 * half_len
+    side = lax.axis_index("mod")
+    f32 = jnp.float32
+    rows_b = gather_sequences(hidden_in, side)
+    upstream = gather_sequences(cotangent, side).astype(f32)
+    mask = take_side(text_mask, 0, side) == 1
+    regions = take_side(region_count, 0, side)
+    slot_ok = lax.broadcasted_iota(jnp.int32, mask.shape, 1) < regions[:, None]
+    bias = jnp.where(jnp.concatenate((mask, slot_ok), axis=1), f32(0.0), f32(-1000000000.0)).reshape(-1, 1)
+    bias = jnp.broadcast_to(bias, (bias.shape[0], 128))
+
+    query_b = ((linear(rows_b, w_query) + b_query.astype(f32)).astype(jnp.bfloat16) * jnp.bfloat16(0.125))
+    key_b = linear(rows_b, w_key).astype(jnp.bfloat16)
+    value_b = (linear(rows_b, w_value) + b_value.astype(f32)).astype(jnp.bfloat16)
+    context_b, lse = attend(query_b, key_b, value_b, bias, length)
+    branch = linear(context_b, w_attn_out) + b_attn_out.astype(f32)
+    normed_one, factor_one = layer_norm(rows_b.astype(f32) + branch)
+    middle = normed_one * gain_attn.astype(f32) + shift_attn.astype(f32)
     middle_b = middle.astype(jnp.bfloat16)
-    pre_act = linear(middle_b, w_inner) + b_inner.astype(jnp.float32)
+    pre_act = linear(middle_b, w_inner) + b_inner.astype(f32)
     activ, gelu_back = jax.vjp(lambda values: jax.nn.gelu(values, approximate=False), pre_act)
     activ_b = activ.astype(jnp.bfloat16)
-    ffn_out = linear(activ_b, w_outer) + b_outer.astype(jnp.float32)
+    ffn_out = linear(activ_b, w_outer) + b_outer.astype(f32)
     normed_two, factor_two = layer_norm(middle + ffn_out)
-    layer_out = (normed_two * gain_ffn.astype(jnp.float32) + shift_ffn.astype(jnp.float32)).astype(
-        jnp.bfloat16
-    )
-    upstream = cotangent.astype(jnp.float32)
-    grad_gain_ffn = jnp.sum(upstream * normed_two, axis=(0, 1))
-    grad_shift_ffn = jnp.sum(upstream, axis=(0, 1))
-    d_res_two = norm_back(upstream * gain_ffn.astype(jnp.float32), normed_two, factor_two)
+    layer_out = (normed_two * gain_ffn.astype(f32) + shift_ffn.astype(f32)).astype(jnp.bfloat16)
+    layer_out = return_rows(layer_out.reshape(seq_count // 2, length, width), side)
+    grad_gain_ffn = row_total(upstream * normed_two)
+    grad_shift_ffn = row_total(upstream)
+    d_res_two = norm_back(upstream * gain_ffn.astype(f32), normed_two, factor_two)
     d_ffn_b = d_res_two.astype(jnp.bfloat16)
     grad_b_outer = row_total(d_ffn_b)
     grad_w_outer = weight_grad(activ_b, d_ffn_b)
@@ -522,90 +610,56 @@
     grad_b_inner = row_total(d_pre_b)
     grad_w_inner = weight_grad(middle_b, d_pre_b)
     d_middle = d_res_two + back_linear(d_pre_b, w_inner)
-    grad_gain_attn = jnp.sum(d_middle * normed_one, axis=(0, 1))
-    grad_shift_attn = jnp.sum(d_middle, axis=(0, 1))
-    d_res_one = norm_back(d_middle * gain_attn.astype(jnp.float32), normed_one, factor_one)
+    grad_gain_attn = row_total(d_middle * normed_one)
+    grad_shift_attn = row_total(d_middle)
+    d_res_one = norm_back(d_middle * gain_attn.astype(f32), normed_one, factor_one)
     d_branch_b = d_res_one.astype(jnp.bfloat16)
-    attention_output_bias_gradient = row_total(d_branch_b)
+    grad_b_attn_out = row_total(d_branch_b)
     grad_w_attn_out = weight_grad(context_b, d_branch_b)
     d_context_b = back_linear(d_branch_b, w_attn_out).astype(jnp.bfloat16)
-    d_context_h = d_context_b.reshape(seq_count, half_len, HEADS, head_size)
-    probs_again = jnp.exp(masked_scores() - log_total)
-    probs_low = probs_again.astype(jnp.bfloat16)
-    d_probs = jnp.einsum(
-        "sqhe,skhe->shqk", d_context_h, value_h, preferred_element_type=jnp.float32
-    )
-    d_scores_b = (
-        probs_again * (d_probs - jnp.sum(probs_again * d_probs, axis=-1, keepdims=True))
-    ).astype(jnp.bfloat16)
-    d_query_b = (
-        (
-            jnp.einsum("shqk,skhe->sqhe", d_scores_b, key_h, preferred_element_type=jnp.float32)
-            * factor_qk
-        )
-        .reshape(seq_count, half_len, width)
-        .astype(jnp.bfloat16)
-    )
-    d_keys_all = (
-        jnp.einsum("shqk,sqhe->skhe", d_scores_b, query_h, preferred_element_type=jnp.float32)
-        * factor_qk
-    ).reshape(seq_count, 2 * half_len, width)
-    d_values_all = jnp.einsum(
-        "shqk,sqhe->skhe", probs_low, d_context_h, preferred_element_type=jnp.float32
-    ).reshape(seq_count, 2 * half_len, width)
-    lower_keys, upper_keys = (d_keys_all[:, :half_len], d_keys_all[:, half_len:])
-    lower_values, upper_values = (d_values_all[:, :half_len], d_values_all[:, half_len:])
-    own_keys = jnp.where(text_half, lower_keys, upper_keys)
-    own_values = jnp.where(text_half, lower_values, upper_values)
-    other_keys = jnp.where(text_half, upper_keys, lower_keys)
-    other_values = jnp.where(text_half, upper_values, lower_values)
-    returned = partner_2(
-        jnp.stack((other_keys, other_values)).astype(jnp.bfloat16), "mod", 0
-    ).astype(jnp.float32)
-    d_key_b = (own_keys + returned[0]).astype(jnp.bfloat16)
-    d_value_b = (own_values + returned[1]).astype(jnp.bfloat16)
+    d_query_b, d_key_b, d_value_b = attend_back(query_b, key_b, value_b, d_context_b, lse, bias, length)
     grad_b_query = row_total(d_query_b)
     grad_b_value = row_total(d_value_b)
-    grad_w_query = weight_grad(hidden_in, d_query_b)
-    key_weight_gradient = weight_grad(hidden_in, d_key_b)
-    grad_w_value = weight_grad(hidden_in, d_value_b)
     input_grad = (
         d_res_one
         + back_linear(d_query_b, w_query)
         + back_linear(d_key_b, w_key)
         + back_linear(d_value_b, w_value)
     ).astype(jnp.bfloat16)
-    g_outer = grad_w_outer.astype(jnp.bfloat16)
-    g_inner = grad_w_inner.astype(jnp.bfloat16)
-    g_attn = jnp.concatenate(
-        [g.astype(jnp.bfloat16) for g in (grad_w_query, key_weight_gradient, grad_w_value, grad_w_attn_out)]
+    input_grad = return_rows(input_grad.reshape(seq_count // 2, length, width), side)
+    sums = sum_gradients(
+        (
+            grad_w_outer,
+            grad_w_inner,
+            weight_grad(rows_b, d_query_b),
+            weight_grad(rows_b, d_key_b),
+            weight_grad(rows_b, d_value_b),
+            grad_w_attn_out,
+        ),
+        (
+            grad_b_query, grad_b_value, grad_b_attn_out, grad_gain_attn, grad_shift_attn, grad_b_outer,
+            grad_gain_ffn, grad_shift_ffn, grad_b_inner,
+        ),
     )
-    small_in = jnp.concatenate(
-        [
-            grad_b_query, grad_b_value, attention_output_bias_gradient, grad_gain_attn, grad_shift_attn,
-            grad_b_inner, grad_b_outer, grad_gain_ffn, grad_shift_ffn, jnp.zeros((4 * width,), jnp.float32),
-        ]
-    ).reshape(SMALL, width)
-    s_outer, s_inner, s_attn, s_small = sum_gradients(g_outer, g_inner, g_attn, small_in)
-    wide = s_attn.astype(jnp.float32).reshape(4, width, width)
+    s_outer, s_inner, s_query, s_key, s_value, s_attn_out, small = sums
     return (
         layer_out,
         input_grad,
-        wide[0],
-        s_small[0],
-        wide[1],
-        wide[2],
-        s_small[1],
-        wide[3],
-        s_small[2],
-        s_small[3],
-        s_small[4],
-        s_inner.astype(jnp.float32),
-        s_small[5:9].reshape(-1),
-        s_outer.astype(jnp.float32),
-        s_small[9],
-        s_small[10],
-        s_small[11],
+        s_query.astype(f32),
+        small[0],
+        s_key.astype(f32),
+        s_value.astype(f32),
+        small[1],
+        s_attn_out.astype(f32),
+        small[2],
+        small[3],
+        small[4],
+        s_inner.astype(f32),
+        small[8:12].reshape(-1),
+        s_outer.astype(f32),
+        small[5],
+        small[6],
+        small[7],
     )
 
 

time: 369 us -> 297 us (0.80)
  local copies, waits for them, and re-layouts: 52.3 us -> 13.9 us
  waiting for transfers between devices: 36.8 us -> 6.86 us
  Pallas kernels: 133 us -> 162 us
  other arithmetic: 57.5 us -> 34.4 us
  matrix products: 76.4 us -> 69 us
    ppermute x2 -> x4, waiting for transfers between devices: 36.8 us -> 6.86 us  [to_partner(): return lax.ppermute(block, 'mod', [(0, 1), (1, 0)])]
    pallas_call x1 -> x3, Pallas kernels: 133 us -> 162 us  [the longest x1 136 us: sum_gradients(): pl.pallas_call(functools.partial(sum_kernel, extra_bits), out_shape=tuple...]
    unnamed x145 -> x84, local copies, waits for them, and re-layouts: 25.6 us -> 3.21 us
    slice x8 -> x2, local copies, waits for them, and re-layouts: 19.5 us -> 1.4 us  [the longest x1 0.74 us: on_device(): small[8:12].reshape(-1)]
    convert_element_type x14 -> x15, other arithmetic: 37.8 us -> 26.8 us  [the longest x1 5.05 us: on_device(): s_inner.astype(f32)]
    dot_general x24 -> x18, matrix products: 76.4 us -> 69 us  [the longest x6 31.6 us: linear(): lax.dot_general(rows, weight_matrix, (((1,), (0,)), ((), ())), preferred_...]
    broadcast_in_dim x0 -> x9, local copies, waits for them, and re-layouts: none -> 5.48 us  [the longest x8 4.64 us: row_total(): return jnp.sum(values.astype(jnp.float32), axis=0, keepdims=True)]
    concatenate x2 -> x0, other arithmetic: 5.44 us -> none  [the longest x1 4.87 us: on_device(): jnp.concatenate([g.astype(jnp.bfloat16) for g in (grad_w_query, key_weigh...]
  transfers between devices with their start and end apart: 2 -> 4, of which waited for: 2 -> 2; matrix products, arithmetic and copies ran while one was open for 9% -> 13% of each run, Pallas kernels for 0% -> 47%
where the time goes in v2:
time: 297 us; the launch traced here: 293 us
  Pallas kernels  162 us (55%)
  matrix products  69 us (23%)
  other arithmetic  34.4 us (12%)
  local copies, waits for them, and re-layouts  13.9 us (5%)
  waiting for transfers between devices  6.86 us (2%)
  starting transfers between devices  5.13 us (2%)
    pallas_call x1, Pallas kernels, sum_gradients(): pl.pallas_call(functools.partial(sum_kernel, extra_bits), out_shape=tuple...  136 us
    dot_general x6, matrix products, linear(): lax.dot_general(rows, weight_matrix, (((1,), (0,)), ((), ())), preferred_...  31.6 us
    dot_general x6, matrix products, back_linear(): lax.dot_general(gradient_rows, weight_matrix, (((1,), (1,)), ((), ())), p...  19.6 us
    dot_general x6, matrix products, weight_grad(): lax.dot_general(layer_inputs, gradient_rows, (((0,), (0,)), ((), ())), pr...  17.9 us
    pallas_call x1, Pallas kernels, attend_back(): pl.pallas_call(attend_back_kernel, grid=(seqs, pairs), out_shape=tuple((j...  13.1 us
    pallas_call x1, Pallas kernels, attend(): pl.pallas_call(attend_kernel, grid=(seqs, pairs), out_shape=(jax.ShapeDty...  12.5 us
    ppermute x4, waiting for transfers between devices, to_partner(): return lax.ppermute(block, 'mod', [(0, 1), (1, 0)])  6.86 us
  transfers between devices with their start and end apart: 4, of which 2 were waited for; matrix products, arithmetic and copies ran while one was open for 13% of the time, Pallas kernels for 47%

profile of v2, /device:TPU:0, one launch (start us, length us, event | category | flops | bytes accessed | tf_op | source)
XLA Modules:
  0.0 292.6 jit_solution(18382689307803932017)
XLA Ops:
  0.7 2.0 constant_dynamic-slice_fusion.2
  2.8 3.0 %collective-permute-start.2 = (bf16[2,128,768]{2,1,0:T(8,128)(2,1)}, bf16[2,128,768]{2,1,0:T(8,128)(2,1)S(1)}, u32[]{:S(2)}, u32[]{:S(2)}) collective-permute-start(bf16[2,128,768]{2,1,0:T(8,128)(2,1)} %get-tuple-element.66), channel_id=1, source_target_pairs={{0,1},{1,0},{2,3},{3,2},{4,5},{5,4},{6,7},{7,6},{8,9},{9,8},{10,11... | collective-permute-start | bytes 1179656 | tf_op jit(solution)/shard_map/ppermute | solution.py:501
  6.1 1.3 convert_element_type.134
  7.4 0.7 convert_element_type.139
  8.0 1.3 convert_element_type.127
  9.3 1.3 convert_element_type.130
  10.6 1.3 convert_element_type.132
  11.9 1.3 convert_element_type.138
  13.1 1.3 convert_element_type.140
  14.4 1.3 convert_element_type.136
  15.9 0.4 convert_reduce_fusion.1
  16.3 0.6 copy.37
  16.9 6.7 %collective-permute-done = bf16[2,128,768]{2,1,0:T(8,128)(2,1)} collective-permute-done((bf16[2,128,768]{2,1,0:T(8,128)(2,1)S(1)}, bf16[2,128,768]{2,1,0:T(8,128)(2,1)}, u32[]{:S(2)}, u32[]{:S(2)}) %collective-permute-start) | collective-permute-done | bytes 393248 | tf_op jit(solution)/shard_map/ppermute | solution.py:501
  23.6 1.3 maximum_select_fusion
  25.0 1.7 convolution_convert_fusion.7.k_ref
  26.6 1.7 add_convert_fusion.3.v_ref
  28.3 1.7 fusion.14.q_ref
  30.0 0.8 broadcast_in_dim.30.bias_ref
  30.8 12.5 %shard_map.314 = (bf16[512,768]{1,0:T(8,128)(2,1)}, f32[2,6,2,256]{3,2,1,0:T(2,128)}) custom-call(bf16[512,768]{1,0:T(8,128)(2,1)} %fusion.14.q_ref, bf16[512,768]{1,0:T(8,128)(2,1)} %convolution_convert_fusion.7.k_ref, bf16[512,768]{1,0:T(8,128)(2,1)} %add_convert_fusion.3.v_ref, f32[512,128]{1,0:T(8,128)} %broadcast_in_dim.30.bias_ref), custom_call_target="tpu_custom_call" | custom-call | tf_op jit(solution)/shard_map/pallas_call | solution.py:473
  43.4 2.0 fusion.29
  45.7 0.4 copy-done.17
  46.1 19.4 %multiply_convert_fusion = (bf16[512,3072]{1,0:T(8,128)(2,1)S(1)}, f32[512,3072]{1,0:T(8,128)}, f32[512,3072]{1,0:T(8,128)}) fusion(f32[3072]{0:T(1024)S(1)} %copy-done.17, bf16[768,3072]{1,0:T(8,128)(2,1)} %param.31, f32[512,768]{1,0:T(8,128)S(1)} %get-tuple-element.73, f32[768]{0:T(1024)S(1)} %copy-done.21, f32[768]{0:T(1024)S(1)} %convert_element_type.133, ...), kind=kOutput, calls=%fused_computation.4 | convolution fusion | flops 2521694208 | bytes 22042624 | tf_op jit(solution)/shard_map/dot_general | solution.py:523
  65.5 5.1 %fusion.30 = (f32[512]{0:T(512)S(1)}, f32[512,768]{1,0:T(8,128)S(1)}) fusion(f32[768]{0:T(1024)S(1)} %copy-done.22, bf16[512,3072]{1,0:T(8,128)(2,1)S(1)} %get-tuple-element.61, bf16[3072,768]{1,0:T(8,128)(2,1)} %param.33, f32[768]{0:T(1024)S(1)} %copy-done.21, f32[768]{0:T(1024)S(1)} %convert_element_type.133, f32[512]{0:T(512)S(1)} %add_rsqrt_fusion.1, ...), kind=kOutput, calls=%fused_computation.99 | convolution fusion | flops 2418671104 | bytes 11025408 | tf_op jit(solution)/shard_map/dot_general | solution.py:523
  71.0 0.7 fusion.12
  71.8 1.5 convert_reduce_fusion.2
  73.3 4.3 %convolution_convert_fusion.1.refs_0_ = bf16[3072,768]{1,0:T(8,128)(2,1)} fusion(bf16[512,3072]{1,0:T(8,128)(2,1)S(1)} %get-tuple-element.61, f32[512,768]{1,0:T(8,128)S(1)} %get-tuple-element.58), kind=kOutput, calls=%fused_computation.19 | convolution fusion | flops 2418671616 | bytes 9437184 | tf_op jit(solution)/shard_map/dot_general | solution.py:531
  77.6 9.5 %convert_reduce_fusion = (f32[3072]{0:T(1024)}, bf16[512,3072]{1,0:T(8,128)(2,1)}) fusion(f32[512,3072]{1,0:T(8,128)} %get-tuple-element.62, bf16[3072,768]{1,0:T(8,128)(2,1)S(1)} %bitcast.71, f32[512,768]{1,0:T(8,128)S(1)} %get-tuple-element.58, f32[512,3072]{1,0:T(8,128)} %get-tuple-element.74, f32[3072]{0:T(1024)S(1)} %copy-done.17), kind=kOutput, calls=%fused_computation.2 | convolution fusion | flops 2443047936 | bytes 22044672 | tf_op jit(solution)/shard_map/dot_general | solution.py:527
  87.2 5.8 %multiply_reduce_fusion = (f32[768]{0:T(1024)}, f32[512]{0:T(512)S(1)}, f32[512]{0:T(512)S(1)}, f32[768]{0:T(1024)}, f32[512,768]{1,0:T(8,128)S(1)}) fusion(f32[512,768]{1,0:T(8,128)S(1)} %get-tuple-element.73, f32[512]{0:T(512)S(1)} %add_rsqrt_fusion.1, f32[512]{0:T(512)S(1)} %broadcast_multiply_fusion.4, f32[768]{0:T(1024)S(1)} %convert_element_type.133, ...), kind=kOutput, calls=%fused_computation.32 | convolution fusion | flops 2419848704 | bytes 12600320 | tf_op jit(solution)/shard_map/dot_general | solution.py:527
  93.0 4.8 %convolution_convert_fusion.refs_1_ = bf16[768,3072]{1,0:T(8,128)(2,1)} fusion(bf16[512,3072]{1,0:T(8,128)(2,1)S(1)} %copy-done.34, f32[512,768]{1,0:T(8,128)S(1)} %get-tuple-element.73, f32[768]{0:T(1024)S(1)} %copy-done.21, f32[768]{0:T(1024)S(1)} %convert_element_type.133, f32[512]{0:T(512)S(1)} %add_rsqrt_fusion.1, f32[512]{0:T(512)S(1)} %broadcast_multiply_fusion.4), kind=kOutput, calls=%fused_computation.18 | convolution fusion | flops 2420244480 | bytes 9447424 | tf_op jit(solution)/shard_map/dot_general | solution.py:531
  97.8 0.5 convert_reduce_fusion.3
  98.3 0.6 copy-done.9
  98.9 1.8 convolution_convert_fusion.2.refs_5_
  100.7 1.7 convolution_convert_fusion.6.dc_ref
  102.4 13.1 %shard_map.315 = (bf16[512,768]{1,0:T(8,128)(2,1)}, bf16[512,768]{1,0:T(8,128)(2,1)}, bf16[512,768]{1,0:T(8,128)(2,1)}) custom-call(bf16[512,768]{1,0:T(8,128)(2,1)} %fusion.14.q_ref, bf16[512,768]{1,0:T(8,128)(2,1)} %convolution_convert_fusion.7.k_ref, bf16[512,768]{1,0:T(8,128)(2,1)} %add_convert_fusion.3.v_ref, ...), custom_call_target="tpu_custom_call" | custom-call | tf_op jit(solution)/shard_map/pallas_call | solution.py:488
  115.6 3.3 %convolution_convert_fusion.4.refs_3_ = bf16[768,768]{1,0:T(8,128)(2,1)} fusion(bf16[512,768]{1,0:T(8,128)(2,1)} %bitcast.64, bf16[512,768]{1,0:T(8,128)(2,1)} %get-tuple-element.32), kind=kOutput, calls=%fused_computation.49 | convolution fusion | flops 604569600 | bytes 2752512 | tf_op jit(solution)/shard_map/dot_general | solution.py:531
  118.9 0.8 fusion.32
  120.3 1.8 convolution_convert_fusion.5.refs_2_
  122.1 0.8 fusion.31
  123.0 0.6 broadcast_in_dim.70.refs_13_
  123.5 0.6 broadcast_in_dim.69.refs_12_
  124.1 0.6 broadcast_in_dim.68.refs_11_
  124.7 0.9 constant_dynamic-slice_fusion.5
  125.6 1.7 collective-permute-start.1
  127.4 0.6 broadcast_in_dim.34.refs_9_
  128.0 0.6 broadcast_in_dim.33.refs_8_
  128.5 0.6 broadcast_in_dim.35.refs_10_
  129.1 0.6 broadcast_in_dim.31.refs_6_
  129.7 1.8 convolution_convert_fusion.3.refs_4_
  131.5 0.9 add_convert_fusion.1
  132.5 0.4 collective-permute-start.3
  133.0 0.6 broadcast_in_dim.32.refs_7_
  133.6 136.4 %shard_map.316 = (bf16[3072,768]{1,0:T(8,128)(2,1)}, bf16[768,3072]{1,0:T(8,128)(2,1)}, bf16[768,768]{1,0:T(8,128)(2,1)}, bf16[768,768]{1,0:T(8,128)(2,1)}, bf16...) custom-call(bf16[3072,768]{1,0:T(8,128)(2,1)} %convolution_convert_fusion.1.refs_0_, ...), custom_call_target="tpu_custom_call" | custom-call | tf_op jit(solution)/shard_map/pallas_call | solution.py:386
  270.0 0.7 slice.32
  270.8 0.6 reshape.126
  271.4 2.9 %convert_element_type.161 = f32[768,768]{1,0:T(8,128)} convert(bf16[768,768]{1,0:T(8,128)(2,1)} %get-tuple-element.34) | non-fusion elementwise | flops 589824 | bytes 3538944 | tf_op jit(solution)/shard_map/convert_element_type | solution.py:648
  274.3 1.6 convert_element_type.162
  276.0 1.6 convert_element_type.163
  277.6 1.6 convert_element_type.164
  279.2 1.0 copy-done.1
  280.1 5.0 %convert_element_type.165 = f32[768,3072]{1,0:T(8,128)} convert(bf16[768,3072]{1,0:T(8,128)(2,1)S(1)} %copy-done.1) | non-fusion elementwise | flops 2359296 | bytes 14155776 | tf_op jit(solution)/shard_map/convert_element_type | solution.py:657
  285.2 4.5 %convert_element_type.166 = f32[3072,768]{1,0:T(8,128)} convert(bf16[3072,768]{1,0:T(8,128)(2,1)S(1)} %bitcast.57) | non-fusion elementwise | flops 2359296 | bytes 14155776 | tf_op jit(solution)/shard_map/convert_element_type | solution.py:659
  289.7 0.7 slice_reduce_fusion
  290.3 1.0 maximum_select_fusion.1
  291.4 1.0 maximum_select_fusion.3
  (105 shorter events, 2.2 us)
Async XLA Ops:
  0.7 42.7 %copy-start = (bf16[768,768]{1,0:T(8,128)(2,1)S(1)}, bf16[768,768]{1,0:T(8,128)(2,1)}, u32[]{:S(2)}) copy-start(bf16[768,768]{1,0:T(8,128)(2,1)} %param.27) | copy-start | bytes 3538948
  0.7 5.1 %copy-start.13 = (bf16[4,128,768]{2,1,0:T(8,128)(2,1)S(1)}, bf16[4,128,768]{2,1,0:T(8,128)(2,1)}, u32[]{:S(2)}) copy-start(bf16[4,128,768]{2,1,0:T(8,128)(2,1)} %param.19) | copy-start | bytes 2359300
  0.7 5.2 %copy-start.33 = (s32[4]{0:T(128)S(1)}, s32[4]{0:T(128)}, u32[]{:S(2)}) copy-start(s32[4]{0:T(128)} %param.21) | copy-start | bytes 52
  0.7 5.3 %copy-start.27 = (s32[4,128]{1,0:T(4,128)S(1)}, s32[4,128]{1,0:T(4,128)}, u32[]{:S(2)}) copy-start(s32[4,128]{1,0:T(4,128)} %param.20) | copy-start | bytes 6148
  0.7 5.4 %copy-start.26 = (bf16[768]{0:T(1024)(128)(2,1)S(1)}, bf16[768]{0:T(1024)(128)(2,1)}, u32[]{:S(2)}) copy-start(bf16[768]{0:T(1024)(128)(2,1)} %param.29) | copy-start | bytes 4612
  2.8 13.1 %collective-permute-start.2 = (bf16[2,128,768]{2,1,0:T(8,128)(2,1)}, bf16[2,128,768]{2,1,0:T(8,128)(2,1)S(1)}, u32[]{:S(2)}, u32[]{:S(2)}) collective-permute-start(bf16[2,128,768]{2,1,0:T(8,128)(2,1)} %get-tuple-element.66), channel_id=1, source_target_pairs={{0,1},{1,0},{2,3},{3,2},{4,5},{5,4},{6,7},{7,6},{8,9},{9,8},{10,11... | collective-permute-start | bytes 1179656 | tf_op jit(solution)/shard_map/ppermute | solution.py:501
  5.8 17.8 %collective-permute-start = (bf16[2,128,768]{2,1,0:T(8,128)(2,1)S(1)}, bf16[2,128,768]{2,1,0:T(8,128)(2,1)}, u32[]{:S(2)}, u32[]{:S(2)}) collective-permute-start(bf16[2,128,768]{2,1,0:T(8,128)(2,1)S(1)} %get-tuple-element.71), channel_id=1, source_target_pairs={{0,1},{1,0},{2,3},{3,2},{4,5},{5,4},{6,7},{7,6},{8,9},{9,8},{10,11... | collective-permute-start | bytes 1179656 | tf_op jit(solution)/shard_map/ppermute | solution.py:501
  15.7 9.2 %copy-start.28 = (bf16[768,768]{1,0:T(8,128)(2,1)S(1)}, bf16[768,768]{1,0:T(8,128)(2,1)}, u32[]{:S(2)}) copy-start(bf16[768,768]{1,0:T(8,128)(2,1)} %param.24) | copy-start | bytes 3538948
  24.9 18.4 %copy-start.10 = (bf16[2,256,768]{2,1,0:T(8,128)(2,1)}, bf16[2,256,768]{2,1,0:T(8,128)(2,1)S(1)}, u32[]{:S(2)}) copy-start(bf16[2,256,768]{2,1,0:T(8,128)(2,1)S(1)} %maximum_select_fusion) | copy-start | bytes 2359300
  24.9 1.7 copy-start.4
  24.9 1.7 copy-start.25
  26.6 1.7 copy-start.24
  26.6 1.7 copy-start.30
  30.0 13.4 %copy-start.23 = (f32[768]{0:T(1024)S(1)}, f32[768]{0:T(1024)}, u32[]{:S(2)}) copy-start(f32[768]{0:T(1024)} %convert_element_type.132) | copy-start | bytes 9220
  45.4 0.7 copy-start.17
  45.4 0.7 copy-start.21
  46.1 19.4 %copy-start.22 = (f32[768]{0:T(1024)S(1)}, f32[768]{0:T(1024)}, u32[]{:S(2)}) copy-start(f32[768]{0:T(1024)} %convert_element_type.138) | copy-start | bytes 9220
  70.9 0.8 copy-start.16
  71.0 0.8 copy-start.18
  71.7 5.9 %slice-start.2 = ((s8[4718592]{0:T(1024)(128)(4,1)}), s8[4194304]{0:T(1024)(128)(4,1)S(1)}, s32[]{:S(2)}) async-start(s8[4718592]{0:T(1024)(128)(4,1)} %bitcast.70), calls=%async_computation.2 | async-start | bytes 8388608
  73.3 4.3 %slice-start.3 = ((s8[4718592]{0:T(1024)(128)(4,1)}), s8[524288]{0:T(1024)(128)(4,1)S(1)}, s32[]{:S(2)}) async-start(s8[4718592]{0:T(1024)(128)(4,1)} %bitcast.70), calls=%async_computation.3 | async-start | bytes 1048576
  73.3 13.9 %slice-start.4 = ((s8[4718592]{0:T(1024)(128)(4,1)}), s8[4194304]{0:T(1024)(128)(4,1)S(1)}, s32[]{:S(2)}) async-start(s8[4718592]{0:T(1024)(128)(4,1)} %bitcast.72), calls=%async_computation.4 | async-start | bytes 8388608
  77.6 9.6 %slice-start.5 = ((s8[4718592]{0:T(1024)(128)(4,1)}), s8[524288]{0:T(1024)(128)(4,1)S(1)}, s32[]{:S(2)}) async-start(s8[4718592]{0:T(1024)(128)(4,1)} %bitcast.72), calls=%async_computation.5 | async-start | bytes 1048576
  87.2 5.8 %copy-start.34 = (bf16[512,3072]{1,0:T(8,128)(2,1)S(1)}, bf16[512,3072]{1,0:T(8,128)(2,1)}, u32[]{:S(2)}) copy-start(bf16[512,3072]{1,0:T(8,128)(2,1)} %get-tuple-element.79) | copy-start | bytes 9437188
  97.8 1.1 copy-start.9
  115.5 3.4 %copy-start.29 = (bf16[768,768]{1,0:T(8,128)(2,1)S(1)}, bf16[768,768]{1,0:T(8,128)(2,1)}, u32[]{:S(2)}) copy-start(bf16[768,768]{1,0:T(8,128)(2,1)} %param.24) | copy-start | bytes 3538948
  115.5 3.3 %copy-start.32 = (bf16[512,768]{1,0:T(8,128)(2,1)S(1)}, bf16[512,768]{1,0:T(8,128)(2,1)}, u32[]{:S(2)}) copy-start(bf16[512,768]{1,0:T(8,128)(2,1)} %get-tuple-element.32) | copy-start | bytes 2359300
  118.9 1.1 copy-start.12
  118.9 1.4 copy-start.11
  120.3 1.8 copy-start.31
  122.1 2.0 copy-start.15
  122.9 4.4 %copy-start.20 = (f32[768]{0:T(1024)S(1)}, f32[768]{0:T(1024)}, u32[]{:S(2)}) copy-start(f32[768]{0:T(1024)} %get-tuple-element.41) | copy-start | bytes 9220
  122.9 5.6 %copy-start.19 = (f32[768]{0:T(1024)S(1)}, f32[768]{0:T(1024)}, u32[]{:S(2)}) copy-start(f32[768]{0:T(1024)} %get-tuple-element.46) | copy-start | bytes 9220
  122.9 6.7 %copy-start.2 = (bf16[512,768]{1,0:T(8,128)(2,1)S(1)}, bf16[512,768]{1,0:T(8,128)(2,1)}, u32[]{:S(2)}) copy-start(bf16[512,768]{1,0:T(8,128)(2,1)} %get-tuple-element.33) | copy-start | bytes 2359300
  125.6 164.7 %collective-permute-start.1 = (bf16[2,128,768]{2,1,0:T(8,128)(2,1)}, bf16[2,128,768]{2,1,0:T(8,128)(2,1)S(1)}, u32[]{:S(2)}, u32[]{:S(2)}) collective-permute-start(bf16[2,128,768]{2,1,0:T(8,128)(2,1)} %get-tuple-element.69), channel_id=1, source_target_pairs={{0,1},{1,0},{2,3},{3,2},{4,5},{5,4},{6,7},{7,6},{8,9},{9,8},{10,11... | collective-permute-start | bytes 1179656 | tf_op jit(solution)/shard_map/ppermute | solution.py:501
  129.7 1.8 copy-start.5
  132.5 158.9 %collective-permute-start.3 = (bf16[2,128,768]{2,1,0:T(8,128)(2,1)S(1)}, bf16[2,128,768]{2,1,0:T(8,128)(2,1)S(1)}, u32[]{:S(2)}, u32[]{:S(2)}) collective-permute-start(bf16[2,128,768]{2,1,0:T(8,128)(2,1)S(1)} %get-tuple-element.65), channel_id=1, source_target_pairs={{0,1},{1,0},{2,3},{3,2},{4,5},{5,4},{6,7},{7,6},{8,9},{9,8},{10,11... | collective-permute-start | bytes 1179656 | tf_op jit(solution)/shard_map/ppermute | solution.py:501
  271.4 2.9 %copy-start.8 = (bf16[768,768]{1,0:T(8,128)(2,1)S(1)}, bf16[768,768]{1,0:T(8,128)(2,1)}, u32[]{:S(2)}) copy-start(bf16[768,768]{1,0:T(8,128)(2,1)} %get-tuple-element.36) | copy-start | bytes 3538948
  274.3 1.7 copy-start.7
  274.3 3.3 %copy-start.6 = (bf16[768,768]{1,0:T(8,128)(2,1)S(1)}, bf16[768,768]{1,0:T(8,128)(2,1)}, u32[]{:S(2)}) copy-start(bf16[768,768]{1,0:T(8,128)(2,1)} %get-tuple-element.38) | copy-start | bytes 3538948
  276.0 4.1 %copy-start.1 = (bf16[768,3072]{1,0:T(8,128)(2,1)S(1)}, bf16[768,3072]{1,0:T(8,128)(2,1)}, u32[]{:S(2)}) copy-start(bf16[768,3072]{1,0:T(8,128)(2,1)} %get-tuple-element.39) | copy-start | bytes 14155780
  277.6 7.6 %slice-start = ((s8[4718592]{0:T(1024)(128)(4,1)}), s8[4194304]{0:T(1024)(128)(4,1)S(1)}, s32[]{:S(2)}) async-start(s8[4718592]{0:T(1024)(128)(4,1)} %bitcast.56), calls=%async_computation | async-start | bytes 8388608
  280.1 5.1 %slice-start.1 = ((s8[4718592]{0:T(1024)(128)(4,1)}), s8[524288]{0:T(1024)(128)(4,1)S(1)}, s32[]{:S(2)}) async-start(s8[4718592]{0:T(1024)(128)(4,1)} %bitcast.56), calls=%async_computation.1 | async-start | bytes 1048576
  285.2 4.5 %copy-start.14 = (f32[16,768]{1,0:T(8,128)S(1)}, f32[16,768]{1,0:T(8,128)}, u32[]{:S(2)}) copy-start(f32[16,768]{1,0:T(8,128)} %get-tuple-element.35) | copy-start | bytes 147460
  285.2 5.2 %copy-start.3 = (bf16[2,128,768]{2,1,0:T(8,128)(2,1)S(1)}, bf16[2,128,768]{2,1,0:T(8,128)(2,1)}, u32[]{:S(2)}) copy-start(bf16[2,128,768]{2,1,0:T(8,128)(2,1)} %get-tuple-element.68) | copy-start | bytes 1179652

commit v3 on v2

--- a/solution.py
+++ b/solution.py
@@ -96,8 +96,8 @@
 
 
 class Tasks:
-    def __init__(self, wire, kinds, acc, sib, fin, rb, ssem, rsem):
-        self.w, self.acc, self.sib, self.fin, self.rb = wire, acc, sib, fin, rb
+    def __init__(self, wire, kinds, part, rb, ssem, rsem, block):
+        self.w, self.acc, self.rb, self.block = wire, part, rb, block
         self.ssem, self.rsem = ssem, rsem
         self.rb_at = 0
         self.sem_at = 0
@@ -122,7 +122,8 @@
     def build(self, t, kind):
         w = self.w
         steps = []
-        home = t * ROWS
+        home = (w.core * len(KINDS) + t) * ROWS
+        away = ((1 - w.core) * len(KINDS) + t) * ROWS
         at0 = self.space(ROWS)
 
         def done(at, n):
@@ -232,7 +233,7 @@
                 )
 
         exchange(
-            lambda: self.sib.at[pl.ds(home, ROWS), :],
+            lambda: self.rows(away, ROWS),
             lambda: self.rb.at[pl.ds(at0, ROWS), :],
             w.peer("core"),
             lambda: add_rows(self.acc, home, self.rb, at0, ROWS),
@@ -257,12 +258,16 @@
             gather(d2, b3, n3)
             gather(d1, b2, n2)
             line_gather(home, n1)
-        exchange(
-            lambda: self.rb.at[pl.ds(at0, ROWS), :],
-            lambda: self.fin.at[pl.ds(home, ROWS), :],
-            w.peer("core"),
-            lambda: None,
-        )
+        k = self.sem_at
+        self.sem_at += 1
+
+        def last(block):
+            return pltpu.make_async_remote_copy(
+                src_ref=self.rb.at[pl.ds(at0, ROWS), :], dst_ref=block, send_sem=self.ssem.at[k], recv_sem=self.rsem.at[k],
+                device_id=w.peer("core"), device_id_type=MESH)
+
+        final = by_core(w.core, lambda half: last(self.block(half, t)), t)
+        steps.append((lambda: final.start(), lambda: final.wait()))
         self.homes.append(at0)
         return steps
 
@@ -275,73 +280,258 @@
 
 
 KINDS = "ABCABDABCABDABCABD"
-START = tuple(t // 3 for t in range(18))
+START = tuple((0, 1, 2, 4, 8, 9)[t // 3] for t in range(18))
 SMALL = 16
+SMALL_START = 10
+LAG = 1
 
 
 def block_of(refs, half, t):
-    outer, inner = refs[:2]
     if t < 6:
-        return outer.at[pl.ds(pl.multiple_of(half * 1536 + t * ROWS, ROWS), ROWS), :]
+        return refs[0].at[pl.ds(pl.multiple_of(half * 1536 + t * ROWS, ROWS), ROWS), :]
     if t < 12:
         i, j = (t - 6) % 3, (t - 6) // 3
-        return inner.at[pl.ds(i * ROWS, ROWS), pl.ds(pl.multiple_of((half * 2 + j) * LANES, LANES), LANES)]
-    return None
-
-
-def attn_block(refs, half, t):
-    ref = refs[2 + 2 * half + (t - 12) // 3]
-    return ref.at[pl.ds((t - 12) % 3 * ROWS, ROWS), :]
+        return refs[1].at[pl.ds(i * ROWS, ROWS), pl.ds(pl.multiple_of((half * 2 + j) * LANES, LANES), LANES)]
+    return refs[2 + 2 * half + (t - 12) // 3].at[pl.ds((t - 12) % 3 * ROWS, ROWS), :]
 
 
 class Branches:
-    def __init__(self, core, first, second):
-        self.core, self.first, self.second = core, first, second
+    def __init__(self, core, make):
+        self.core, self.make = core, make
 
     def start(self):
-        for core, copy in ((0, self.first), (1, self.second)):
+        for core in range(2):
             @pl.when(self.core == core)
-            def _(copy=copy):
-                copy().start()
+            def _(core=core):
+                self.make(core).start()
 
     def wait(self):
-        self.first().wait()
-
-
-def sum_kernel(extra_bits, *refs):
-    ins, vectors, refs = refs[:6], refs[6:15], refs[15:]
-    outs, small_out, refs = refs[:6], refs[6], refs[7:]
-    acc, sib, fin, rb, small, small_rb, ssem, rsem, lsem, vsem = refs
+        self.make(0).wait()
+
+
+class Plain:
+    def __init__(self, make):
+        self.make = make
+
+    def start(self):
+        self.make().start()
+
+    def wait(self):
+        self.make().wait()
+
+
+def by_core(core, make, t):
+    return Plain(lambda: make(core)) if t < 12 else Branches(core, make)
+
+
+def tn(a, b):
+    return lax.dot_general(a, b, (((0,), (0,)), ((), ())), preferred_element_type=jnp.float32)
+
+
+FULL = ("q", "k", "v", "ctx", "x", "mid", "dffn", "dmid", "normed", "wq", "wk", "wv", "wo")
+
+
+def back_kernel(extra_bits, *refs):
+    g_outer, w_outer, w_inner, slope, *refs = refs
+    full_in, refs = dict(zip(FULL, refs)), refs[len(FULL):]
+    factor, gain, lse, bias_ref, sum_outer, sum_gain, sum_shift, *refs = refs
+    outs, small_out, grad_out, refs = refs[:6], refs[6], refs[7], refs[8:]
+    v, refs = dict(zip(FULL, refs)), refs[len(FULL):]
+    wou, win, gp, dp, dc, db, dq, dk, dv, ig, part, rb, small, small_rb, ssem, rsem, lsem, vsem, fsem, tsem, osem, isem = refs
     w = Wire(extra_bits)
     count = len(KINDS)
-
-    def block_copy(arrays, own, t, buf, outward, sem):
-        def copy(block):
-            return pltpu.make_async_copy(buf, block, sem) if outward else pltpu.make_async_copy(block, buf, sem)
-
-        if t < 12:
-            return copy(block_of(arrays, w.core if own else 1 - w.core, t))
-        low, high = attn_block(arrays, 0, t), attn_block(arrays, 1, t)
-        return Branches(w.core, lambda: copy(low if own else high), lambda: copy(high if own else low))
-
-    def load(t, who):
-        buf = (acc, sib)[who].at[pl.ds(t * ROWS, ROWS), :]
-        return block_copy(ins, who == 0, t, buf, False, lsem.at[2 * t + who])
-
-    def store(t, who):
-        source = rb.at[pl.ds(tasks.homes[t], ROWS), :] if who == 0 else fin.at[pl.ds(t * ROWS, ROWS), :]
-        return block_copy(outs, who == 0, t, source, True, lsem.at[2 * t + who])
-
-    for t in range(count):
-        load(t, 1).start()
-        load(t, 0).start()
+    f32 = jnp.float32
+    rows = dp.shape[0]
+    length = bias_ref.shape[0] // lse.shape[0]
+    order = (0, 2, 1, 3)
+
+    def load(half, t):
+        to = part.at[pl.ds((half * count + t) * ROWS, ROWS), :]
+        return pltpu.make_async_copy(g_outer.at[pl.ds(half * 1536 + t * ROWS, ROWS), :], to, lsem.at[half, t])
+
+    def fetch(name):
+        return pltpu.make_async_copy(full_in[name], v[name], fsem.at[FULL.index(name)])
+
+    def tile(which, n):
+        at, slot = order[n] * LANES, n % 2
+        source, to = (
+            (w_outer.at[pl.ds(at, LANES), :], wou),
+            (w_inner.at[:, pl.ds(at, LANES)], win),
+            (slope.at[:, pl.ds(at, LANES)], gp),
+        )[which]
+        return pltpu.make_async_copy(source, to.at[slot], tsem.at[which, n])
+
+    for t in range(6):
+        load(0, t).start()
+        load(1, t).start()
+        if t == 0:
+            fetch("dffn").start()
+            tile(0, 0).start()
+            tile(2, 0).start()
+            fetch("mid").start()
+            tile(1, 0).start()
+            fetch("dmid").start()
+    for which in range(3):
+        tile(which, 1).start()
+    for name in ("normed", "wo", "ctx", "k", "q", "v", "x", "wq", "wk", "wv"):
+        fetch(name).start()
     w.barrier()
-    tasks = Tasks(w, KINDS, acc, sib, fin, rb, ssem, rsem)
-
-    for at, ref in enumerate(vectors):
-        for i in range(ref.shape[1] // LANES):
-            small[0, at + i:at + i + 1, :] = ref[:, i * LANES:(i + 1) * LANES]
-    small[0, 12:16, :] = jnp.zeros((4, LANES), jnp.float32)
+    tasks = Tasks(w, KINDS, part, rb, ssem, rsem, lambda half, t: block_of(outs, half, t))
+
+    def store(t):
+        def make(half):
+            return pltpu.make_async_copy(rb.at[pl.ds(tasks.homes[t], ROWS), :], block_of(outs, half, t), osem.at[t])
+
+        return by_core(w.core, make, t)
+
+    def grad_blocks(left, right, half, t):
+        def body(i, carry):
+            columns = pl.ds(pl.multiple_of(i * ROWS, ROWS), ROWS)
+            to = pl.ds(pl.multiple_of((half * count + t + i) * ROWS, ROWS), ROWS)
+            part[to, :] = tn(left[:, columns], right[...]).astype(jnp.bfloat16)
+            return carry
+
+        lax.fori_loop(0, LANES // ROWS, body, 0)
+
+    def by_rows(step, body, carry=0):
+        def wrapped(r, carry):
+            return body(pl.ds(pl.multiple_of(r * step, step), step), carry)
+
+        return lax.fori_loop(0, rows // step, wrapped, carry)
+
+    none = jnp.zeros((1, LANES), f32)
+
+    def d_pre(n):
+        tile(0, n).wait()
+        tile(2, n).wait()
+        if n == 0:
+            fetch("dffn").wait()
+
+        def body(at, total):
+            d = (nt(v["dffn"][at, :], wou[n % 2]) * gp[n % 2, at, :].astype(f32)).astype(jnp.bfloat16)
+            dp[at, :] = d
+            return total + jnp.sum(d.astype(f32), axis=0, keepdims=True)
+
+        small[0, 8 + order[n]:9 + order[n], :] = by_rows(128, body, none)
+        if n + 2 < 4:
+            tile(0, n + 2).start()
+            tile(2, n + 2).start()
+
+    def inner_blocks(n):
+        if n == 0:
+            fetch("mid").wait()
+        grad_blocks(v["mid"], dp, order[n] // 2, 6 + 3 * (order[n] % 2))
+
+    def d_mid(n):
+        tile(1, n).wait()
+        if n == 0:
+            fetch("dmid").wait()
+
+        def body(at, carry):
+            v["dmid"][at, :] += nt(dp[at, :], win[n % 2])
+            return carry
+
+        by_rows(128, body)
+        if n + 2 < 4:
+            tile(1, n + 2).start()
+
+    def norm_step():
+        fetch("normed").wait()
+
+        def body(at, sums):
+            d, normed = v["dmid"][at, :], v["normed"][at, :]
+            e = d * gain[...]
+            res = factor[at, :] * (
+                e - jnp.mean(e, axis=-1, keepdims=True) - normed * jnp.mean(e * normed, axis=-1, keepdims=True)
+            )
+            low = res.astype(jnp.bfloat16)
+            v["dmid"][at, :] = res
+            db[at, :] = low
+            return (
+                sums[0] + jnp.sum(low.astype(f32), axis=0, keepdims=True),
+                sums[1] + jnp.sum(d * normed, axis=0, keepdims=True),
+                sums[2] + jnp.sum(d, axis=0, keepdims=True),
+            )
+
+        sums = by_rows(64, body, (none, none, none))
+        for i in range(3):
+            small[0, 2 + i:3 + i, :] = sums[i]
+
+    def d_context():
+        fetch("wo").wait()
+
+        def body(i, carry):
+            at = pl.ds(pl.multiple_of(i * 256, 256), 256)
+            dc[:, at] = nt(db[...], v["wo"][at, :]).astype(jnp.bfloat16)
+            return carry
+
+        lax.fori_loop(0, LANES // 256, body, 0)
+
+    def out_blocks():
+        fetch("ctx").wait()
+        grad_blocks(v["ctx"], db, 1, 15)
+
+    def attention(seq, first, pairs):
+        if seq == 0 and first == 0:
+            for name in ("q", "k", "v"):
+                fetch(name).wait()
+        at = pl.ds(seq * length, length)
+        bias = jnp.concatenate([bias_ref[at, :]] * (length // 128), axis=1)
+
+        def body(p, carry):
+            c = pl.ds(pl.multiple_of(p * 128, 128), 128)
+            dq[at, c], dk[at, c], dv[at, c] = attend_pair_back(
+                v["q"][at, c], v["k"][at, c], v["v"][at, c], dc[at, c], lse[seq, p], bias)
+            return carry
+
+        lax.fori_loop(first, first + pairs, body, 0)
+
+    def total_rows(ref, row):
+        def body(at, total):
+            return total + jnp.sum(ref[at, :].astype(f32), axis=0, keepdims=True)
+
+        small[0, row:row + 1, :] = by_rows(128, body, none)
+
+    def value_blocks():
+        grad_blocks(v["x"], dv, 1, 12)
+        total_rows(dv, 1)
+
+    def query_blocks():
+        fetch("x").wait()
+        grad_blocks(v["x"], dq, 0, 12)
+        total_rows(dq, 0)
+
+    def key_blocks():
+        grad_blocks(v["x"], dk, 0, 15)
+
+    def grad_copy(seq, away):
+        source = ig.at[2 * seq + (1 - w.m if away else w.m)]
+        to = grad_out.at[w.m * lse.shape[0] + seq]
+        if not away:
+            return pltpu.make_async_copy(source, to, isem.at[2, seq])
+        return pltpu.make_async_remote_copy(
+            src_ref=source, dst_ref=to, send_sem=isem.at[0, seq], recv_sem=isem.at[1, seq],
+            device_id=w.peer("x"), device_id_type=MESH)
+
+    def input_rows(seq):
+        if seq == 0:
+            for name in ("wq", "wk", "wv"):
+                fetch(name).wait()
+
+        def body(i, carry):
+            at = pl.ds(pl.multiple_of(i * 128, 128), 128)
+            total = v["dmid"][at, :] + nt(dq[at, :], v["wq"][...])
+            total = total + nt(dk[at, :], v["wk"][...]) + nt(dv[at, :], v["wv"][...])
+            ig[i] = total.astype(jnp.bfloat16)
+            return carry
+
+        lax.fori_loop(2 * seq, 2 * seq + 2, body, 0)
+        grad_copy(seq, True).start()
+        grad_copy(seq, False).start()
+
+    small[0, 12:16, :] = jnp.zeros((4, LANES), f32)
+    for row, ref in ((5, sum_outer), (6, sum_gain), (7, sum_shift)):
+        small[0, row:row + 1, :] = ref[...]
     hops = ["core", "x", "y"] + list(range(2, 4 + extra_bits))
 
     def small_copy(k):
@@ -356,53 +546,83 @@
         if k < len(hops):
             small_copy(k).start()
 
-    ops = [(START[t] + p, t, p) for t in range(count) for p in range(len(tasks.steps[t]) + 1)]
-    ops += [(k + 1, count, k) for k in range(len(hops) + 1)]
-    for _, t, p in sorted(ops):
+    seqs, pairs = lse.shape[:2]
+    work = [[(d_pre, n), (inner_blocks, n), (d_mid, n)] for n in range(4)]
+    work.append([(norm_step,), (d_context,), (out_blocks,)])
+    attn = [(attention, seq, first, 2) for seq in range(seqs) for first in range(0, pairs, 2)]
+    half = len(attn) // 2
+    work += [attn[:half], attn[half:], [(query_blocks,), (value_blocks,), (key_blocks,)]]
+    work.append([(input_rows, seq) for seq in range(seqs)])
+
+    def comm(t, p):
         if t == count:
             small_op(p)
-            continue
-        if p == 0:
-            load(t, 1).wait()
-        if p == 1:
-            load(t, 0).wait()
+            return
+        if p == 0 and t < 6:
+            load(0, t).wait()
+            load(1, t).wait()
         tasks.op(t, p)
-        if p == len(tasks.steps[t]):
-            store(t, 0).start()
-            store(t, 1).start()
+        if p == len(tasks.steps[t]) - 1:
+            store(t).start()
+
+    ops = [(START[t] + p, t, p) for t in range(count) for p in range(len(tasks.steps[t]) + 1)]
+    ops += [(SMALL_START + k, count, k) for k in range(len(hops) + 1)]
+    for slot in range(max(op[0] for op in ops) + 1):
+        now = sorted(op for op in ops if op[0] == slot)
+        jobs = work[slot] if slot < len(work) else []
+        marks = [(i * len(now)) // max(len(jobs), 1) + LAG for i in range(len(jobs))]
+        for i, (_, t, p) in enumerate(now):
+            for job, mark in zip(jobs, marks):
+                if min(mark, len(now) - 1) == i:
+                    job[0](*job[1:])
+            comm(t, p)
     small_out[...] = small[len(hops)]
     for t in range(count):
-        store(t, 0).wait()
-        store(t, 1).wait()
-
-
-def sum_gradients(matrices, vectors):
+        store(t).wait()
+    for seq in range(seqs):
+        grad_copy(seq, False).wait()
+        grad_copy(seq, True).wait()
+
+
+def backward(g_outer, w_outer, w_inner, slope, full, blocks, shape):
     extra_bits = (lax.axis_size("batch") // 16).bit_length() - 1
-    rows, sems = plan_sizes(KINDS, extra_bits)
+    space, sems = plan_sizes(KINDS, extra_bits)
     hops = 5 + extra_bits
     count = len(KINDS)
+    low, f32 = jnp.bfloat16, jnp.float32
     hbm = pl.BlockSpec(memory_space=pl.ANY)
     vmem = pl.BlockSpec(memory_space=pltpu.VMEM)
+    rows, width = full[0].shape
+    grads = [g_outer.shape, w_inner.shape] + [(width, width)] * 4
+    flat = pltpu.VMEM((rows, width), low)
     return pl.pallas_call(
-        functools.partial(sum_kernel, extra_bits),
-        out_shape=tuple(jax.ShapeDtypeStruct(m.shape, jnp.bfloat16) for m in matrices)
-        + (jax.ShapeDtypeStruct((SMALL, LANES), jnp.float32),),
-        in_specs=[hbm] * len(matrices) + [vmem] * len(vectors),
-        out_specs=(hbm,) * len(matrices) + (vmem,),
-        scratch_shapes=[
-            pltpu.VMEM((count * ROWS, LANES), jnp.bfloat16),
-            pltpu.VMEM((count * ROWS, LANES), jnp.bfloat16),
-            pltpu.VMEM((count * ROWS, LANES), jnp.bfloat16),
-            pltpu.VMEM((rows, LANES), jnp.bfloat16),
-            pltpu.VMEM((hops + 1, SMALL, LANES), jnp.float32),
-            pltpu.VMEM((hops, SMALL, LANES), jnp.float32),
+        functools.partial(back_kernel, extra_bits),
+        out_shape=tuple(jax.ShapeDtypeStruct(g, low) for g in grads)
+        + (jax.ShapeDtypeStruct((SMALL, LANES), f32), jax.ShapeDtypeStruct(shape, low)),
+        in_specs=[hbm] * (4 + len(full)) + [vmem] * len(blocks),
+        out_specs=(hbm,) * len(grads) + (vmem, hbm),
+        scratch_shapes=[pltpu.VMEM(m.shape, m.dtype) for m in full]
+        + [
+            pltpu.VMEM((2, LANES, LANES), low),
+            pltpu.VMEM((2, LANES, LANES), low),
+            pltpu.VMEM((2, rows, LANES), low),
+            flat, flat, flat, flat, flat, flat,
+            pltpu.VMEM((rows // 128, 128, width), low),
+            pltpu.VMEM((2 * count * ROWS, LANES), low),
+            pltpu.VMEM((space, LANES), low),
+            pltpu.VMEM((hops + 1, SMALL, LANES), f32),
+            pltpu.VMEM((hops, SMALL, LANES), f32),
             pltpu.SemaphoreType.DMA((sems,)),
             pltpu.SemaphoreType.DMA((sems,)),
-            pltpu.SemaphoreType.DMA((2 * count,)),
+            pltpu.SemaphoreType.DMA((2, 6)),
             pltpu.SemaphoreType.DMA((2, hops)),
+            pltpu.SemaphoreType.DMA((len(full),)),
+            pltpu.SemaphoreType.DMA((3, 4)),
+            pltpu.SemaphoreType.DMA((count,)),
+            pltpu.SemaphoreType.DMA((3, shape[0] // 2)),
         ],
-        compiler_params=pltpu.CompilerParams(collective_id=1, has_side_effects=True, vmem_limit_bytes=60 << 20),
-    )(*matrices, *vectors)
+        compiler_params=pltpu.CompilerParams(collective_id=1, has_side_effects=True, vmem_limit_bytes=62 << 20),
+    )(g_outer, w_outer, w_inner, slope, *full, *blocks)
 
 
 def nt(a, b):
@@ -458,12 +678,6 @@
     ctx_ref[...], lse_ref[0, 0] = attend_pair(q_ref[...], k_ref[...], v_ref[...], bias)
 
 
-def attend_back_kernel(q_ref, k_ref, v_ref, dc_ref, lse_ref, bias_ref, dq_ref, dk_ref, dv_ref):
-    bias = jnp.concatenate([bias_ref[...]] * (q_ref.shape[0] // 128), axis=1)
-    dq_ref[...], dk_ref[...], dv_ref[...] = attend_pair_back(
-        q_ref[...], k_ref[...], v_ref[...], dc_ref[...], lse_ref[0, 0], bias)
-
-
 def attend(q, k, v, bias, length):
     rows, width = q.shape
     seqs, pairs = rows // length, width // 128
@@ -477,21 +691,6 @@
         in_specs=[block, block, block, mask],
         out_specs=(block, lse),
     )(q, k, v, bias)
-
-
-def attend_back(q, k, v, dc, lse, bias, length):
-    rows, width = q.shape
-    seqs, pairs = rows // length, width // 128
-    block = pl.BlockSpec((length, 128), lambda s, p: (s, p))
-    mask = pl.BlockSpec((length, 128), lambda s, p: (s, 0))
-    lse_spec = pl.BlockSpec((1, 1, 2, length), lambda s, p: (s, p, 0, 0))
-    return pl.pallas_call(
-        attend_back_kernel,
-        grid=(seqs, pairs),
-        out_shape=tuple(jax.ShapeDtypeStruct(q.shape, jnp.bfloat16) for _ in range(3)),
-        in_specs=[block, block, block, block, lse_spec, mask],
-        out_specs=(block, block, block),
-    )(q, k, v, dc, lse, bias)
 
 
 epsilon = 1e-05
@@ -593,8 +792,9 @@
     middle = normed_one * gain_attn.astype(f32) + shift_attn.astype(f32)
     middle_b = middle.astype(jnp.bfloat16)
     pre_act = linear(middle_b, w_inner) + b_inner.astype(f32)
-    activ, gelu_back = jax.vjp(lambda values: jax.nn.gelu(values, approximate=False), pre_act)
-    activ_b = activ.astype(jnp.bfloat16)
+    below = 0.5 * (1.0 + lax.erf(pre_act * f32(0.7071067811865476)))
+    slope_b = (below + pre_act * (jnp.exp(-0.5 * pre_act * pre_act) * f32(0.3989422804014327))).astype(jnp.bfloat16)
+    activ_b = (pre_act * below).astype(jnp.bfloat16)
     ffn_out = linear(activ_b, w_outer) + b_outer.astype(f32)
     normed_two, factor_two = layer_norm(middle + ffn_out)
     layer_out = (normed_two * gain_ffn.astype(f32) + shift_ffn.astype(f32)).astype(jnp.bfloat16)
@@ -605,43 +805,15 @@
     d_ffn_b = d_res_two.astype(jnp.bfloat16)
     grad_b_outer = row_total(d_ffn_b)
     grad_w_outer = weight_grad(activ_b, d_ffn_b)
-    d_activ = back_linear(d_ffn_b, w_outer)
-    d_pre_b = gelu_back(d_activ)[0].astype(jnp.bfloat16)
-    grad_b_inner = row_total(d_pre_b)
-    grad_w_inner = weight_grad(middle_b, d_pre_b)
-    d_middle = d_res_two + back_linear(d_pre_b, w_inner)
-    grad_gain_attn = row_total(d_middle * normed_one)
-    grad_shift_attn = row_total(d_middle)
-    d_res_one = norm_back(d_middle * gain_attn.astype(f32), normed_one, factor_one)
-    d_branch_b = d_res_one.astype(jnp.bfloat16)
-    grad_b_attn_out = row_total(d_branch_b)
-    grad_w_attn_out = weight_grad(context_b, d_branch_b)
-    d_context_b = back_linear(d_branch_b, w_attn_out).astype(jnp.bfloat16)
-    d_query_b, d_key_b, d_value_b = attend_back(query_b, key_b, value_b, d_context_b, lse, bias, length)
-    grad_b_query = row_total(d_query_b)
-    grad_b_value = row_total(d_value_b)
-    input_grad = (
-        d_res_one
-        + back_linear(d_query_b, w_query)
-        + back_linear(d_key_b, w_key)
-        + back_linear(d_value_b, w_value)
-    ).astype(jnp.bfloat16)
-    input_grad = return_rows(input_grad.reshape(seq_count // 2, length, width), side)
-    sums = sum_gradients(
+    s_outer, s_inner, s_query, s_key, s_value, s_attn_out, small, input_grad = backward(
+        grad_w_outer, w_outer, w_inner, slope_b,
         (
-            grad_w_outer,
-            grad_w_inner,
-            weight_grad(rows_b, d_query_b),
-            weight_grad(rows_b, d_key_b),
-            weight_grad(rows_b, d_value_b),
-            grad_w_attn_out,
+            query_b, key_b, value_b, context_b, rows_b, middle_b, d_ffn_b, d_res_two, normed_one,
+            w_query, w_key, w_value, w_attn_out,
         ),
-        (
-            grad_b_query, grad_b_value, grad_b_attn_out, grad_gain_attn, grad_shift_attn, grad_b_outer,
-            grad_gain_ffn, grad_shift_ffn, grad_b_inner,
-        ),
+        (factor_one, gain_attn.astype(f32).reshape(1, -1), lse, bias, grad_b_outer, grad_gain_ffn, grad_shift_ffn),
+        hidden_in.shape,
     )
-    s_outer, s_inner, s_query, s_key, s_value, s_attn_out, small = sums
     return (
         layer_out,
         input_grad,

time: 297 us -> 230 us (0.77); the launches traced: 293 us -> 229 us
  matrix products: 69 us -> 22.6 us
  waiting for transfers between devices: 6.86 us -> 0.37 us
  Pallas kernels: 162 us -> 157 us
  local copies, waits for them, and re-layouts: 13.9 us -> 9.98 us
    dot_general x6 -> x0, matrix products: 19.6 us -> none  [back_linear(): lax.dot_general(gradient_rows, weight_matrix, (((1,), (1,)), ((), ())), p...]
    dot_general x6 -> x1, matrix products: 17.9 us -> 4.31 us  [weight_grad(): lax.dot_general(layer_inputs, gradient_rows, (((0,), (0,)), ((), ())), pr...]
    dot_general x6, matrix products: 31.6 us -> 18.3 us  [linear(): lax.dot_general(rows, weight_matrix, (((1,), (0,)), ((), ())), preferred_...]
    ppermute x4 -> x3, waiting for transfers between devices: 6.86 us -> 0.37 us  [to_partner(): return lax.ppermute(block, 'mod', [(0, 1), (1, 0)])]
    pallas_call x2 -> x1, Pallas kernels: 150 us -> 145 us  [backward(): pl.pallas_call(functools.partial(back_kernel, extra_bits), out_shape=tupl...]
  transfers between devices with their start and end apart: 4 -> 3, of which waited for: 2 -> 1; matrix products, arithmetic and copies ran while one was open for 13% -> 25% of each run, Pallas kernels for 47% -> 69%
where the time goes in v3:
time: 230 us; the launch traced here: 229 us
  Pallas kernels  157 us (68%)
  other arithmetic  32.5 us (14%)
  matrix products  22.6 us (10%)
  local copies, waits for them, and re-layouts  9.98 us (4%)
  starting transfers between devices  5.13 us (2%)
    pallas_call x1, Pallas kernels, backward(): pl.pallas_call(functools.partial(back_kernel, extra_bits), out_shape=tupl...  145 us
    dot_general x6, matrix products, linear(): lax.dot_general(rows, weight_matrix, (((1,), (0,)), ((), ())), preferred_...  18.3 us
    pallas_call x1, Pallas kernels, attend(): pl.pallas_call(attend_kernel, grid=(seqs, pairs), out_shape=(jax.ShapeDty...  12 us
    convert_element_type x1, other arithmetic, on_device(): s_inner.astype(f32)  7.52 us
    ppermute x3, starting transfers between devices, to_partner(): return lax.ppermute(block, 'mod', [(0, 1), (1, 0)])  5.13 us
  transfers between devices with their start and end apart: 3, of which 1 were waited for; matrix products, arithmetic and copies ran while one was open for 25% of the time, Pallas kernels for 69%

profile of v3, /device:TPU:0, one launch (start us, length us, event | category | flops | bytes accessed | tf_op | source)
XLA Modules:
  0.0 228.7 jit_solution(10858542812364589146)
XLA Ops:
  0.7 0.0 copy-start.14
  0.7 2.0 constant_dynamic-slice_fusion.6
  2.7 3.0 %collective-permute-start = (bf16[2,128,768]{2,1,0:T(8,128)(2,1)}, bf16[2,128,768]{2,1,0:T(8,128)(2,1)}, u32[]{:S(2)}, u32[]{:S(2)}) collective-permute-start(bf16[2,128,768]{2,1,0:T(8,128)(2,1)} %get-tuple-element.62), channel_id=1, source_target_pairs={{0,1},{1,0},{2,3},{3,2},{4,5},{5,4},{6,7},{7,6},{8,9},{9,8},{10,11... | collective-permute-start | bytes 1179656 | tf_op jit(solution)/shard_map/ppermute | solution.py:700
  5.7 0.1 constant_dynamic-slice_fusion
  5.7 0.1 collective-permute-start.2
  5.8 0.6 broadcast_in_dim.21.refs_18_
  6.4 0.6 convert_element_type.94
  7.0 0.6 convert_element_type.91
  7.6 0.7 dynamic_slice.27
  8.3 0.8 fusion.15
  9.1 0.6 copy.37
  9.7 1.3 convert_element_type.96
  10.9 0.7 convert_element_type.98
  11.6 1.3 convert_element_type.100
  12.9 1.3 convert_element_type.102
  14.2 0.7 convert_element_type.103
  14.9 0.7 convert_element_type.104
  15.6 0.4 collective-permute-done
  15.9 1.3 maximum_select_fusion
  17.3 0.0 copy-start.7
  17.3 0.0 copy-start.21
  17.3 1.7 convolution_convert_fusion.1.k_ref.refs_5_
  19.0 1.7 add_convert_fusion.1.v_ref.refs_6_
  20.7 1.7 fusion.13.q_ref.refs_4_
  22.3 0.8 broadcast_in_dim.20.bias_ref.refs_20_
  23.2 12.0 %shard_map.314 = (bf16[512,768]{1,0:T(8,128)(2,1)}, f32[2,6,2,256]{3,2,1,0:T(2,128)}) custom-call(bf16[512,768]{1,0:T(8,128)(2,1)} %fusion.13.q_ref.refs_4_, bf16[512,768]{1,0:T(8,128)(2,1)} %convolution_convert_fusion.1.k_ref.refs_5_, bf16[512,768]{1,0:T(8,128)(2,1)} %add_convert_fusion.1.v_ref.refs_6_, f32[512,128]{1,0:T(8,128)} %broadcast_in_dim.20.bias_ref.refs_20_), custom_call_target="tpu_custom_call" | custom-call | tf_op jit(solution)/shard_map/pallas_call | solution.py:687
  35.2 2.0 fusion.17
  37.2 0.0 copy-start.16
  37.2 0.3 multiply_reduce_fusion.1
  37.6 0.0 slice-start
  37.6 0.3 fusion.12
  37.9 0.0 copy-start
  37.9 0.0 copy-done.16
  37.9 0.0 slice-start.1
  38.0 0.0 copy-start.19
  38.0 8.6 %fusion.4 = (bf16[512,3072]{1,0:T(8,128)(2,1)}, bf16[512,3072]{1,0:T(8,128)(2,1)S(1)}) fusion(f32[3072]{0:T(1024)S(1)} %copy-done.16, bf16[512,768]{1,0:T(8,128)(2,1)S(1)} %get-tuple-element.52.refs_9_, bf16[768,3072]{1,0:T(8,128)(2,1)} %refs_2_.1), kind=kOutput, calls=%fused_computation.5 | convolution fusion | flops 2434793472 | bytes 11808768 | tf_op jit(solution)/shard_map/dot_general | solution.py:722
  46.6 2.7 %fusion.18 = (f32[512]{0:T(512)S(1)}, f32[512,768]{1,0:T(8,128)S(1)}) fusion(f32[768]{0:T(1024)S(1)} %copy-done.19, bf16[512,3072]{1,0:T(8,128)(2,1)S(1)} %get-tuple-element.55, bf16[3072,768]{1,0:T(8,128)(2,1)S(1)} %bitcast.40, f32[768]{0:T(1024)S(1)} %convert_element_type.98, f32[512,768]{1,0:T(8,128)S(1)} %get-tuple-element.53.refs_12_, ...), kind=kOutput, calls=%fused_computation.63 | convolution fusion | flops 2417884672 | bytes 11021312 | tf_op jit(solution)/shard_map/dot_general | solution.py:722
  49.3 0.3 multiply_reduce_fusion
  49.6 0.0 collective-permute-done.2
  49.6 0.7 fusion.11
  50.4 0.4 convert_reduce_fusion
  50.8 1.8 convert_reduce_fusion.1
  52.7 0.1 constant_dynamic-slice_fusion.3
  52.7 2.1 collective-permute-start.1
  54.8 4.3 %convolution_convert_fusion.refs_0_ = bf16[3072,768]{1,0:T(8,128)(2,1)} fusion(bf16[512,3072]{1,0:T(8,128)(2,1)S(1)} %get-tuple-element.55, bf16[512,768]{1,0:T(8,128)(2,1)S(1)} %get-tuple-element.50.refs_10_), kind=kOutput, calls=%fused_computation.8 | convolution fusion | flops 2418278400 | bytes 8650752 | tf_op jit(solution)/shard_map/dot_general | solution.py:730
  59.1 0.6 broadcast_in_dim.22.refs_21_
  59.7 0.6 broadcast_in_dim.23.refs_22_
  60.3 0.9 copy.36.refs_17_
  61.2 0.6 broadcast_in_dim.24.refs_23_
  61.8 145.1 %shard_map.315 = (bf16[3072,768]{1,0:T(8,128)(2,1)}, bf16[768,3072]{1,0:T(8,128)(2,1)}, bf16[768,768]{1,0:T(8,128)(2,1)}, bf16[768,768]{1,0:T(8,128)(2,1)}, bf16...) custom-call(bf16[3072,768]{1,0:T(8,128)(2,1)} %convolution_convert_fusion.ref, ...), custom_call_target="tpu_custom_call" | custom-call | tf_op jit(solution)/shard_map/pallas_call | solution.py:598
  206.9 7.5 %convert_element_type.117 = f32[768,3072]{1,0:T(8,128)} convert(bf16[768,3072]{1,0:T(8,128)(2,1)} %get-tuple-element.35) | non-fusion elementwise | flops 2359296 | bytes 14155776 | tf_op jit(solution)/shard_map/convert_element_type | solution.py:829
  214.4 4.5 %convert_element_type.118 = f32[3072,768]{1,0:T(8,128)} convert(bf16[3072,768]{1,0:T(8,128)(2,1)S(1)} %copy-done.1) | non-fusion elementwise | flops 2359296 | bytes 14155776 | tf_op jit(solution)/shard_map/convert_element_type | solution.py:831
  218.9 1.6 convert_element_type.113
  220.5 0.1 copy-done.11
  220.6 1.6 convert_element_type.114
  222.2 0.1 copy-done.10
  222.3 1.6 convert_element_type.115
  223.8 0.1 copy-done.9
  223.9 1.6 convert_element_type.116
  225.5 0.6 reshape.128
  226.1 0.7 slice_reduce_fusion
  226.8 0.0 collective-permute-done.1
  226.8 1.0 maximum_select_fusion.1
  227.8 0.9 copy.40
  (53 shorter events, 0.1 us)
Async XLA Ops:
  0.7 5.0 %copy-start.14 = (bf16[4,128,768]{2,1,0:T(8,128)(2,1)S(1)}, bf16[4,128,768]{2,1,0:T(8,128)(2,1)}, u32[]{:S(2)}) copy-start(bf16[4,128,768]{2,1,0:T(8,128)(2,1)} %param.37) | copy-start | bytes 2359300
  0.7 5.1 %copy-start.18 = (bf16[768]{0:T(1024)(128)(2,1)S(1)}, bf16[768]{0:T(1024)(128)(2,1)}, u32[]{:S(2)}) copy-start(bf16[768]{0:T(1024)(128)(2,1)} %param.29) | copy-start | bytes 4612
  0.7 5.7 %copy-start.23 = (bf16[768]{0:T(1024)(128)(2,1)S(1)}, bf16[768]{0:T(1024)(128)(2,1)}, u32[]{:S(2)}) copy-start(bf16[768]{0:T(1024)(128)(2,1)} %param.26) | copy-start | bytes 4612
  0.7 6.3 %copy-start.24 = (bf16[768]{0:T(1024)(128)(2,1)S(1)}, bf16[768]{0:T(1024)(128)(2,1)}, u32[]{:S(2)}) copy-start(bf16[768]{0:T(1024)(128)(2,1)} %param.23) | copy-start | bytes 4612
  2.7 14.6 %copy-start.6 = (bf16[768,768]{1,0:T(8,128)(2,1)S(1)}, bf16[768,768]{1,0:T(8,128)(2,1)}, u32[]{:S(2)}) copy-start(bf16[768,768]{1,0:T(8,128)(2,1)} %refs_14_.1) | copy-start | bytes 3538948
  2.7 13.2 %collective-permute-start = (bf16[2,128,768]{2,1,0:T(8,128)(2,1)}, bf16[2,128,768]{2,1,0:T(8,128)(2,1)}, u32[]{:S(2)}, u32[]{:S(2)}) collective-permute-start(bf16[2,128,768]{2,1,0:T(8,128)(2,1)} %get-tuple-element.62), channel_id=1, source_target_pairs={{0,1},{1,0},{2,3},{3,2},{4,5},{5,4},{6,7},{7,6},{8,9},{9,8},{10,11... | collective-permute-start | bytes 1179656 | tf_op jit(solution)/shard_map/ppermute | solution.py:700
  5.7 43.9 %collective-permute-start.2 = (bf16[2,128,768]{2,1,0:T(8,128)(2,1)S(1)}, bf16[2,128,768]{2,1,0:T(8,128)(2,1)S(1)}, u32[]{:S(2)}, u32[]{:S(2)}) collective-permute-start(bf16[2,128,768]{2,1,0:T(8,128)(2,1)S(1)} %get-tuple-element.57), channel_id=1, source_target_pairs={{0,1},{1,0},{2,3},{3,2},{4,5},{5,4},{6,7},{7,6},{8,9},{9,8},{10,11... | collective-permute-start | bytes 1179656 | tf_op jit(solution)/shard_map/ppermute | solution.py:700
  17.3 17.9 %copy-start.3 = (bf16[2,256,768]{2,1,0:T(8,128)(2,1)}, bf16[2,256,768]{2,1,0:T(8,128)(2,1)S(1)}, u32[]{:S(2)}) copy-start(bf16[2,256,768]{2,1,0:T(8,128)(2,1)S(1)} %maximum_select_fusion) | copy-start | bytes 2359300
  17.3 1.7 copy-start.7
  17.3 1.7 copy-start.21
  19.0 1.7 copy-start.5
  19.0 1.7 copy-start.20
  20.7 1.7 copy-start.17
  22.3 12.8 %copy-start.8 = (bf16[768,768]{1,0:T(8,128)(2,1)S(1)}, bf16[768,768]{1,0:T(8,128)(2,1)}, u32[]{:S(2)}) copy-start(bf16[768,768]{1,0:T(8,128)(2,1)} %refs_16_.1) | copy-start | bytes 3538948
  22.3 12.9 %copy-start.22 = (f32[768]{0:T(1024)S(1)}, f32[768]{0:T(1024)}, u32[]{:S(2)}) copy-start(f32[768]{0:T(1024)} %convert_element_type.96) | copy-start | bytes 9220
  37.2 0.7 copy-start.16
  37.6 9.0 %slice-start = ((s8[4718592]{0:T(1024)(128)(4,1)}), s8[4194304]{0:T(1024)(128)(4,1)S(1)}, s32[]{:S(2)}) async-start(s8[4718592]{0:T(1024)(128)(4,1)} %bitcast.39), calls=%async_computation | async-start | bytes 8388608
  37.9 8.6 %copy-start.4 = (bf16[512,768]{1,0:T(8,128)(2,1)}, bf16[512,768]{1,0:T(8,128)(2,1)S(1)}, u32[]{:S(2)}) copy-start(bf16[512,768]{1,0:T(8,128)(2,1)S(1)} %get-tuple-element.52.refs_9_) | copy-start | bytes 2359300
  37.9 8.6 %copy-start = (f32[512,768]{1,0:T(8,128)}, f32[512,768]{1,0:T(8,128)S(1)}, u32[]{:S(2)}) copy-start(f32[512,768]{1,0:T(8,128)S(1)} %get-tuple-element.53.refs_12_) | copy-start | bytes 4718596
  37.9 8.6 %slice-start.1 = ((s8[4718592]{0:T(1024)(128)(4,1)}), s8[524288]{0:T(1024)(128)(4,1)S(1)}, s32[]{:S(2)}) async-start(s8[4718592]{0:T(1024)(128)(4,1)} %bitcast.39), calls=%async_computation.1 | async-start | bytes 1048576
  38.0 8.6 %copy-start.19 = (f32[768]{0:T(1024)S(1)}, f32[768]{0:T(1024)}, u32[]{:S(2)}) copy-start(f32[768]{0:T(1024)} %convert_element_type.102) | copy-start | bytes 9220
  52.7 6.5 %copy-start.2 = (bf16[512,768]{1,0:T(8,128)(2,1)}, bf16[512,768]{1,0:T(8,128)(2,1)S(1)}, u32[]{:S(2)}) copy-start(bf16[512,768]{1,0:T(8,128)(2,1)S(1)} %get-tuple-element.50.refs_10_) | copy-start | bytes 2359300
  52.7 174.0 %collective-permute-start.1 = (bf16[2,128,768]{2,1,0:T(8,128)(2,1)S(1)}, bf16[2,128,768]{2,1,0:T(8,128)(2,1)S(1)}, u32[]{:S(2)}, u32[]{:S(2)}) collective-permute-start(bf16[2,128,768]{2,1,0:T(8,128)(2,1)S(1)} %get-tuple-element.60), channel_id=1, source_target_pairs={{0,1},{1,0},{2,3},{3,2},{4,5},{5,4},{6,7},{7,6},{8,9},{9,8},{10,11... | collective-permute-start | bytes 1179656 | tf_op jit(solution)/shard_map/ppermute | solution.py:700
  206.9 7.5 %copy-start.1 = (bf16[3072,768]{1,0:T(8,128)(2,1)S(1)}, bf16[3072,768]{1,0:T(8,128)(2,1)}, u32[]{:S(2)}) copy-start(bf16[3072,768]{1,0:T(8,128)(2,1)} %get-tuple-element.36) | copy-start | bytes 14155780
  214.4 4.5 %copy-start.12 = (bf16[768,768]{1,0:T(8,128)(2,1)S(1)}, bf16[768,768]{1,0:T(8,128)(2,1)}, u32[]{:S(2)}) copy-start(bf16[768,768]{1,0:T(8,128)(2,1)} %get-tuple-element.30) | copy-start | bytes 3538948
  218.9 1.7 copy-start.11
  220.6 1.7 copy-start.10
  222.3 1.7 copy-start.9
  223.9 1.6 copy-start.15
  225.5 2.3 %copy-start.13 = (bf16[4,128,768]{2,1,0:T(8,128)(2,1)S(1)}, bf16[4,128,768]{2,1,0:T(8,128)(2,1)}, u32[]{:S(2)}) copy-start(bf16[4,128,768]{2,1,0:T(8,128)(2,1)} %get-tuple-element.87) | copy-start | bytes 2359300

commit v4 on v3

--- a/solution.py
+++ b/solution.py
@@ -280,9 +280,9 @@
 
 
 KINDS = "ABCABDABCABDABCABD"
-START = tuple((0, 1, 2, 4, 8, 9)[t // 3] for t in range(18))
+START = tuple((0, 1, 2, 3, 6, 6)[t // 3] for t in range(18))
 SMALL = 16
-SMALL_START = 10
+SMALL_START = 8
 LAG = 1
 
 
@@ -385,13 +385,8 @@
         return by_core(w.core, make, t)
 
     def grad_blocks(left, right, half, t):
-        def body(i, carry):
-            columns = pl.ds(pl.multiple_of(i * ROWS, ROWS), ROWS)
-            to = pl.ds(pl.multiple_of((half * count + t + i) * ROWS, ROWS), ROWS)
-            part[to, :] = tn(left[:, columns], right[...]).astype(jnp.bfloat16)
-            return carry
-
-        lax.fori_loop(0, LANES // ROWS, body, 0)
+        to = pl.ds((half * count + t) * ROWS, left.shape[1])
+        part[to, :] = tn(left[...], right[...]).astype(jnp.bfloat16)
 
     def by_rows(step, body, carry=0):
         def wrapped(r, carry):
@@ -407,12 +402,9 @@
         if n == 0:
             fetch("dffn").wait()
 
-        def body(at, total):
-            d = (nt(v["dffn"][at, :], wou[n % 2]) * gp[n % 2, at, :].astype(f32)).astype(jnp.bfloat16)
-            dp[at, :] = d
-            return total + jnp.sum(d.astype(f32), axis=0, keepdims=True)
-
-        small[0, 8 + order[n]:9 + order[n], :] = by_rows(128, body, none)
+        d = (nt(v["dffn"][...], wou[n % 2]) * gp[n % 2].astype(f32)).astype(jnp.bfloat16)
+        dp[...] = d
+        small[0, 8 + order[n]:9 + order[n], :] = jnp.sum(d.astype(f32), axis=0, keepdims=True)
         if n + 2 < 4:
             tile(0, n + 2).start()
             tile(2, n + 2).start()
@@ -427,11 +419,7 @@
         if n == 0:
             fetch("dmid").wait()
 
-        def body(at, carry):
-            v["dmid"][at, :] += nt(dp[at, :], win[n % 2])
-            return carry
-
-        by_rows(128, body)
+        v["dmid"][...] += nt(dp[...], win[n % 2])
         if n + 2 < 4:
             tile(1, n + 2).start()
 
@@ -453,19 +441,14 @@
                 sums[2] + jnp.sum(d, axis=0, keepdims=True),
             )
 
-        sums = by_rows(64, body, (none, none, none))
+        sums = by_rows(128, body, (none, none, none))
         for i in range(3):
             small[0, 2 + i:3 + i, :] = sums[i]
 
     def d_context():
         fetch("wo").wait()
 
-        def body(i, carry):
-            at = pl.ds(pl.multiple_of(i * 256, 256), 256)
-            dc[:, at] = nt(db[...], v["wo"][at, :]).astype(jnp.bfloat16)
-            return carry
-
-        lax.fori_loop(0, LANES // 256, body, 0)
+        dc[...] = nt(db[...], v["wo"][...]).astype(jnp.bfloat16)
 
     def out_blocks():
         fetch("ctx").wait()
@@ -478,13 +461,12 @@
         at = pl.ds(seq * length, length)
         bias = jnp.concatenate([bias_ref[at, :]] * (length // 128), axis=1)
 
-        def body(p, carry):
-            c = pl.ds(pl.multiple_of(p * 128, 128), 128)
-            dq[at, c], dk[at, c], dv[at, c] = attend_pair_back(
-                v["q"][at, c], v["k"][at, c], v["v"][at, c], dc[at, c], lse[seq, p], bias)
-            return carry
-
-        lax.fori_loop(first, first + pairs, body, 0)
+        columns = [pl.ds(p * 128, 128) for p in range(first, first + pairs)]
+        found = attend_back(
+            [(v["q"][at, c], v["k"][at, c], v["v"][at, c], dc[at, c], lse[seq, first + i]) for i, c in enumerate(columns)],
+            bias)
+        for c, (d_query, d_key, d_value) in zip(columns, found):
+            dq[at, c], dk[at, c], dv[at, c] = d_query, d_key, d_value
 
     def total_rows(ref, row):
         def body(at, total):
@@ -518,14 +500,11 @@
             for name in ("wq", "wk", "wv"):
                 fetch(name).wait()
 
-        def body(i, carry):
-            at = pl.ds(pl.multiple_of(i * 128, 128), 128)
-            total = v["dmid"][at, :] + nt(dq[at, :], v["wq"][...])
-            total = total + nt(dk[at, :], v["wk"][...]) + nt(dv[at, :], v["wv"][...])
-            ig[i] = total.astype(jnp.bfloat16)
-            return carry
-
-        lax.fori_loop(2 * seq, 2 * seq + 2, body, 0)
+        at = pl.ds(seq * length, length)
+        total = v["dmid"][at, :] + nt(dq[at, :], v["wq"][...])
+        total = total + nt(dk[at, :], v["wk"][...]) + nt(dv[at, :], v["wv"][...])
+        for i in range(length // 128):
+            ig[2 * seq + i] = total[i * 128:i * 128 + 128].astype(jnp.bfloat16)
         grad_copy(seq, True).start()
         grad_copy(seq, False).start()
 
@@ -547,11 +526,10 @@
             small_copy(k).start()
 
     seqs, pairs = lse.shape[:2]
-    work = [[(d_pre, n), (inner_blocks, n), (d_mid, n)] for n in range(4)]
-    work.append([(norm_step,), (d_context,), (out_blocks,)])
-    attn = [(attention, seq, first, 2) for seq in range(seqs) for first in range(0, pairs, 2)]
-    half = len(attn) // 2
-    work += [attn[:half], attn[half:], [(query_blocks,), (value_blocks,), (key_blocks,)]]
+    ffn = [job for n in range(4) for job in ((d_pre, n), (inner_blocks, n), (d_mid, n))]
+    attn = [(attention, seq, first, 3) for seq in range(seqs) for first in range(0, pairs, 3)]
+    work = [ffn[:3], ffn[3:7], ffn[7:], [(norm_step,), (d_context,), (out_blocks,)] + attn[:1]]
+    work += [attn[1:], [(query_blocks,), (value_blocks,), (key_blocks,)]]
     work.append([(input_rows, seq) for seq in range(seqs)])
 
     def comm(t, p):
@@ -637,59 +615,81 @@
     return lax.broadcasted_iota(jnp.int32, (rows, 128), 1) < 64
 
 
-def attend_pair(q, k, v, bias):
-    low = low_lanes(k.shape[0])
-    zero = jnp.zeros_like(k)
-    vt = v.T
-    parts, sums = [], []
-    for head in range(2):
-        own = jnp.where(low if head == 0 else ~low, k, zero)
-        scores = nt(own, q) + bias
-        top = jnp.max(scores, axis=0, keepdims=True)
-        expo = jnp.exp(scores - top)
-        total = jnp.sum(expo, axis=0, keepdims=True)
-        parts.append(nn(vt[head * 64:head * 64 + 64], expo.astype(jnp.bfloat16)) * (1.0 / total))
-        sums.append(top + jnp.log(total))
-    return jnp.concatenate(parts, axis=0).T.astype(jnp.bfloat16), jnp.concatenate(sums, axis=0)
-
-
-def attend_pair_back(q, k, v, dc, lse, bias):
-    low = low_lanes(k.shape[0])
-    zero = jnp.zeros_like(k)
-    kt = k.T
-    dq, dk, dv = [], [], []
-    for head in range(2):
-        mine = low if head == 0 else ~low
-        probs = jnp.exp(nt(jnp.where(mine, k, zero), q) + (bias - lse[head:head + 1]))
-        d_probs = nt(jnp.where(mine, v, zero), dc)
-        inner = jnp.sum(probs * d_probs, axis=0, keepdims=True)
-        d_scores = (probs * (d_probs - inner)).astype(jnp.bfloat16)
-        dq.append(nn(kt[head * 64:head * 64 + 64], d_scores))
-        dk.append(nn(d_scores, q))
-        dv.append(nn(probs.astype(jnp.bfloat16), dc))
-    d_query = (jnp.concatenate(dq, axis=0) * 0.125).T.astype(jnp.bfloat16)
-    d_key = jnp.where(low, dk[0], dk[1]).astype(jnp.bfloat16)
-    d_value = jnp.where(low, dv[0], dv[1]).astype(jnp.bfloat16)
-    return d_query, d_key, d_value
-
-
-def attend_kernel(q_ref, k_ref, v_ref, bias_ref, ctx_ref, lse_ref):
-    bias = jnp.concatenate([bias_ref[...]] * (q_ref.shape[0] // 128), axis=1)
-    ctx_ref[...], lse_ref[0, 0] = attend_pair(q_ref[...], k_ref[...], v_ref[...], bias)
-
-
-def attend(q, k, v, bias, length):
+def heads_of(pairs):
+    return [(i, head) for i in range(len(pairs)) for head in range(2)]
+
+
+def own_lanes(block, head):
+    low = low_lanes(block.shape[0])
+    return jnp.where(low if head == 0 else ~low, block, jnp.zeros_like(block))
+
+
+def attend(pairs, bias):
+    heads = heads_of(pairs)
+    scores = [nt(own_lanes(pairs[i][1], head), pairs[i][0]) + bias for i, head in heads]
+    tops = [jnp.max(s, axis=0, keepdims=True) for s in scores]
+    expo = [jnp.exp(s - top) for s, top in zip(scores, tops)]
+    totals = [jnp.sum(e, axis=0, keepdims=True) for e in expo]
+    vt = [pair[2].T for pair in pairs]
+    context = [
+        nn(vt[i][head * 64:head * 64 + 64], e.astype(jnp.bfloat16)) * (1.0 / total)
+        for e, total, (i, head) in zip(expo, totals, heads)
+    ]
+    logs = [top + jnp.log(total) for top, total in zip(tops, totals)]
+    return [
+        (jnp.concatenate(context[2 * i:2 * i + 2], axis=0).T.astype(jnp.bfloat16), jnp.concatenate(logs[2 * i:2 * i + 2], axis=0))
+        for i in range(len(pairs))
+    ]
+
+
+def attend_back(pairs, bias):
+    heads = heads_of(pairs)
+    kt = [pair[1].T for pair in pairs]
+    scores = [nt(own_lanes(pairs[i][1], head), pairs[i][0]) for i, head in heads]
+    d_probs = [nt(own_lanes(pairs[i][2], head), pairs[i][3]) for i, head in heads]
+    probs = [jnp.exp(s + (bias - pairs[i][4][head:head + 1])) for s, (i, head) in zip(scores, heads)]
+    inner = [jnp.sum(p * d, axis=0, keepdims=True) for p, d in zip(probs, d_probs)]
+    d_scores = [(p * (d - one)).astype(jnp.bfloat16) for p, d, one in zip(probs, d_probs, inner)]
+    probs_low = [p.astype(jnp.bfloat16) for p in probs]
+    dq = [nn(kt[i][head * 64:head * 64 + 64], d) for d, (i, head) in zip(d_scores, heads)]
+    dk = [nn(d, pairs[i][0]) for d, (i, head) in zip(d_scores, heads)]
+    dv = [nn(p, pairs[i][3]) for p, (i, head) in zip(probs_low, heads)]
+    low = low_lanes(pairs[0][0].shape[0])
+    return [
+        (
+            (jnp.concatenate(dq[2 * i:2 * i + 2], axis=0) * 0.125).T.astype(jnp.bfloat16),
+            jnp.where(low, dk[2 * i], dk[2 * i + 1]).astype(jnp.bfloat16),
+            jnp.where(low, dv[2 * i], dv[2 * i + 1]).astype(jnp.bfloat16),
+        )
+        for i in range(len(pairs))
+    ]
+
+
+def forward_kernel(q_ref, k_ref, v_ref, bias_ref, ctx_ref, lse_ref):
+    length, width = q_ref.shape
+    bias = jnp.concatenate([bias_ref[...]] * (length // 128), axis=1)
+
+    def body(step, carry):
+        columns = [pl.ds(pl.multiple_of((step * 3 + i) * 128, 128), 128) for i in range(3)]
+        found = attend([(q_ref[:, c], k_ref[:, c], v_ref[:, c]) for c in columns], bias)
+        for i, (context, logs) in enumerate(found):
+            ctx_ref[:, columns[i]] = context
+            lse_ref[0, step * 3 + i] = logs
+        return carry
+
+    lax.fori_loop(0, width // 384, body, 0)
+
+
+def attention_forward(q, k, v, bias, length):
     rows, width = q.shape
     seqs, pairs = rows // length, width // 128
-    block = pl.BlockSpec((length, 128), lambda s, p: (s, p))
-    mask = pl.BlockSpec((length, 128), lambda s, p: (s, 0))
-    lse = pl.BlockSpec((1, 1, 2, length), lambda s, p: (s, p, 0, 0))
+    block = pl.BlockSpec((length, width), lambda s: (s, 0))
     return pl.pallas_call(
-        attend_kernel,
-        grid=(seqs, pairs),
+        forward_kernel,
+        grid=(seqs,),
         out_shape=(jax.ShapeDtypeStruct(q.shape, jnp.bfloat16), jax.ShapeDtypeStruct((seqs, pairs, 2, length), jnp.float32)),
-        in_specs=[block, block, block, mask],
-        out_specs=(block, lse),
+        in_specs=[block, block, block, pl.BlockSpec((length, 128), lambda s: (s, 0))],
+        out_specs=(block, pl.BlockSpec((1, pairs, 2, length), lambda s: (s, 0, 0, 0))),
     )(q, k, v, bias)
 
 
@@ -786,7 +786,7 @@
     query_b = ((linear(rows_b, w_query) + b_query.astype(f32)).astype(jnp.bfloat16) * jnp.bfloat16(0.125))
     key_b = linear(rows_b, w_key).astype(jnp.bfloat16)
     value_b = (linear(rows_b, w_value) + b_value.astype(f32)).astype(jnp.bfloat16)
-    context_b, lse = attend(query_b, key_b, value_b, bias, length)
+    context_b, lse = attention_forward(query_b, key_b, value_b, bias, length)
     branch = linear(context_b, w_attn_out) + b_attn_out.astype(f32)
     normed_one, factor_one = layer_norm(rows_b.astype(f32) + branch)
     middle = normed_one * gain_attn.astype(f32) + shift_attn.astype(f32)

time: 230 us -> 214 us (0.930); the launches traced: 229 us -> 210 us
  Pallas kernels: 157 us -> 138 us
    pallas_call x1, Pallas kernels: 145 us -> 133 us  [backward(): pl.pallas_call(functools.partial(back_kernel, extra_bits), out_shape=tupl...]
    pallas_call x1, Pallas kernels: 12 us -> 5.82 us  [attention_forward(): pl.pallas_call(forward_kernel, grid=(seqs,), out_shape=(jax.ShapeDtypeStr...]
  transfers between devices with their start and end apart: 3 -> 3, of which waited for: 1 -> 1; matrix products, arithmetic and copies ran while one was open for 25% -> 27% of each run, Pallas kernels for 69% -> 66%
where the time goes in v4:
time: 214 us; the launch traced here: 210 us
  Pallas kernels  138 us (64%)
  other arithmetic  32.5 us (15%)
  matrix products  22.6 us (11%)
  local copies, waits for them, and re-layouts  9.98 us (5%)
  starting transfers between devices  5.14 us (2%)
    pallas_call x1, Pallas kernels, backward(): pl.pallas_call(functools.partial(back_kernel, extra_bits), out_shape=tupl...  133 us
    dot_general x6, matrix products, linear(): lax.dot_general(rows, weight_matrix, (((1,), (0,)), ((), ())), preferred_...  18.3 us
    convert_element_type x1, other arithmetic, on_device(): s_inner.astype(f32)  7.52 us
    pallas_call x1, Pallas kernels, attention_forward(): pl.pallas_call(forward_kernel, grid=(seqs,), out_shape=(jax.ShapeDtypeStr...  5.82 us
    ppermute x3, starting transfers between devices, to_partner(): return lax.ppermute(block, 'mod', [(0, 1), (1, 0)])  5.14 us
    convert_element_type x1, other arithmetic, on_device(): s_outer.astype(f32)  4.48 us
    dot_general x1, matrix products, weight_grad(): lax.dot_general(layer_inputs, gradient_rows, (((0,), (0,)), ((), ())), pr...  4.31 us
  transfers between devices with their start and end apart: 3, of which 1 were waited for; matrix products, arithmetic and copies ran while one was open for 27% of the time, Pallas kernels for 66%

profile of v4, /device:TPU:0, one launch (start us, length us, event | category | flops | bytes accessed | tf_op | source)
XLA Modules:
  0.0 210.2 jit_solution(14438346059338978852)
XLA Ops:
  0.7 2.0 constant_dynamic-slice_fusion.6
  2.7 3.0 %collective-permute-start = (bf16[2,128,768]{2,1,0:T(8,128)(2,1)}, bf16[2,128,768]{2,1,0:T(8,128)(2,1)}, u32[]{:S(2)}, u32[]{:S(2)}) collective-permute-start(bf16[2,128,768]{2,1,0:T(8,128)(2,1)} %get-tuple-element.62), channel_id=1, source_target_pairs={{0,1},{1,0},{2,3},{3,2},{4,5},{5,4},{6,7},{7,6},{8,9},{9,8},{10,11... | collective-permute-start | bytes 1179656 | tf_op jit(solution)/shard_map/ppermute | solution.py:700
  5.7 0.1 constant_dynamic-slice_fusion
  5.7 0.1 collective-permute-start.2
  5.8 0.6 broadcast_in_dim.21.refs_18_
  6.4 0.6 convert_element_type.94
  7.0 0.6 convert_element_type.91
  7.6 0.7 dynamic_slice.27
  8.3 0.8 fusion.15
  9.1 0.6 copy.37
  9.7 1.3 convert_element_type.96
  10.9 0.7 convert_element_type.98
  11.6 1.3 convert_element_type.100
  12.9 1.3 convert_element_type.102
  14.2 0.7 convert_element_type.103
  14.9 0.7 convert_element_type.104
  15.6 0.4 collective-permute-done
  15.9 1.3 maximum_select_fusion
  17.3 0.0 copy-start.7
  17.3 0.0 copy-start.21
  17.3 1.7 convolution_convert_fusion.1.k_ref.refs_5_
  19.0 1.7 add_convert_fusion.1.v_ref.refs_6_
  20.7 1.7 fusion.13.q_ref.refs_4_
  22.3 0.8 broadcast_in_dim.20.bias_ref.refs_20_
  23.2 5.8 %shard_map.314 = (bf16[512,768]{1,0:T(8,128)(2,1)}, f32[2,6,2,256]{3,2,1,0:T(2,128)}) custom-call(bf16[512,768]{1,0:T(8,128)(2,1)} %fusion.13.q_ref.refs_4_, bf16[512,768]{1,0:T(8,128)(2,1)} %convolution_convert_fusion.1.k_ref.refs_5_, bf16[512,768]{1,0:T(8,128)(2,1)} %add_convert_fusion.1.v_ref.refs_6_, f32[512,128]{1,0:T(8,128)} %broadcast_in_dim.20.bias_ref.refs_20_), custom_call_target="tpu_custom_call" | custom-call | tf_op jit(solution)/shard_map/pallas_call | solution.py:687
  29.0 2.0 fusion.17
  31.1 0.0 copy-start.16
  31.1 0.3 multiply_reduce_fusion.1
  31.4 0.0 slice-start
  31.4 0.3 fusion.12
  31.7 0.0 copy-start.4
  31.8 0.0 copy-start
  31.8 0.0 copy-done.16
  31.8 0.0 slice-start.1
  31.8 0.0 copy-start.19
  31.8 8.6 %fusion.4 = (bf16[512,3072]{1,0:T(8,128)(2,1)}, bf16[512,3072]{1,0:T(8,128)(2,1)S(1)}) fusion(f32[3072]{0:T(1024)S(1)} %copy-done.16, bf16[512,768]{1,0:T(8,128)(2,1)S(1)} %get-tuple-element.52.refs_9_, bf16[768,3072]{1,0:T(8,128)(2,1)} %refs_2_.1), kind=kOutput, calls=%fused_computation.5 | convolution fusion | flops 2434793472 | bytes 11808768 | tf_op jit(solution)/shard_map/dot_general | solution.py:722
  40.4 2.7 %fusion.18 = (f32[512]{0:T(512)S(1)}, f32[512,768]{1,0:T(8,128)S(1)}) fusion(f32[768]{0:T(1024)S(1)} %copy-done.19, bf16[512,3072]{1,0:T(8,128)(2,1)S(1)} %get-tuple-element.55, bf16[3072,768]{1,0:T(8,128)(2,1)S(1)} %bitcast.40, f32[768]{0:T(1024)S(1)} %convert_element_type.98, f32[512,768]{1,0:T(8,128)S(1)} %get-tuple-element.53.refs_12_, ...), kind=kOutput, calls=%fused_computation.63 | convolution fusion | flops 2417884672 | bytes 11021312 | tf_op jit(solution)/shard_map/dot_general | solution.py:722
  43.1 0.3 multiply_reduce_fusion
  43.5 0.0 collective-permute-done.2
  43.5 0.7 fusion.11
  44.2 0.4 convert_reduce_fusion
  44.7 1.8 convert_reduce_fusion.1
  46.5 0.1 constant_dynamic-slice_fusion.3
  46.6 2.1 collective-permute-start.1
  48.7 4.3 %convolution_convert_fusion.refs_0_ = bf16[3072,768]{1,0:T(8,128)(2,1)} fusion(bf16[512,3072]{1,0:T(8,128)(2,1)S(1)} %get-tuple-element.55, bf16[512,768]{1,0:T(8,128)(2,1)S(1)} %get-tuple-element.50.refs_10_), kind=kOutput, calls=%fused_computation.8 | convolution fusion | flops 2418278400 | bytes 8650752 | tf_op jit(solution)/shard_map/dot_general | solution.py:730
  53.0 0.6 broadcast_in_dim.22.refs_21_
  53.6 0.6 broadcast_in_dim.23.refs_22_
  54.1 0.9 copy.36.refs_17_
  55.0 0.6 broadcast_in_dim.24.refs_23_
  55.6 132.7 %shard_map.315 = (bf16[3072,768]{1,0:T(8,128)(2,1)}, bf16[768,3072]{1,0:T(8,128)(2,1)}, bf16[768,768]{1,0:T(8,128)(2,1)}, bf16[768,768]{1,0:T(8,128)(2,1)}, bf16...) custom-call(bf16[3072,768]{1,0:T(8,128)(2,1)} %convolution_convert_fusion.ref, ...), custom_call_target="tpu_custom_call" | custom-call | tf_op jit(solution)/shard_map/pallas_call | solution.py:576
  188.3 7.5 %convert_element_type.117 = f32[768,3072]{1,0:T(8,128)} convert(bf16[768,3072]{1,0:T(8,128)(2,1)} %get-tuple-element.35) | non-fusion elementwise | flops 2359296 | bytes 14155776 | tf_op jit(solution)/shard_map/convert_element_type | solution.py:829
  195.8 4.5 %convert_element_type.118 = f32[3072,768]{1,0:T(8,128)} convert(bf16[3072,768]{1,0:T(8,128)(2,1)S(1)} %copy-done.1) | non-fusion elementwise | flops 2359296 | bytes 14155776 | tf_op jit(solution)/shard_map/convert_element_type | solution.py:831
  200.3 1.6 convert_element_type.113
  201.8 0.1 copy-done.11
  201.9 1.6 convert_element_type.114
  203.5 0.1 copy-done.10
  203.6 1.6 convert_element_type.115
  205.2 0.1 copy-done.9
  205.3 1.6 convert_element_type.116
  206.9 0.6 reshape.128
  207.5 0.7 slice_reduce_fusion
  208.1 0.0 collective-permute-done.1
  208.2 1.0 maximum_select_fusion.1
  209.2 0.9 copy.40
  (53 shorter events, 0.1 us)
Async XLA Ops:
  0.7 5.0 %copy-start.14 = (bf16[4,128,768]{2,1,0:T(8,128)(2,1)S(1)}, bf16[4,128,768]{2,1,0:T(8,128)(2,1)}, u32[]{:S(2)}) copy-start(bf16[4,128,768]{2,1,0:T(8,128)(2,1)} %param.37) | copy-start | bytes 2359300
  0.7 5.1 %copy-start.18 = (bf16[768]{0:T(1024)(128)(2,1)S(1)}, bf16[768]{0:T(1024)(128)(2,1)}, u32[]{:S(2)}) copy-start(bf16[768]{0:T(1024)(128)(2,1)} %param.29) | copy-start | bytes 4612
  0.7 5.7 %copy-start.23 = (bf16[768]{0:T(1024)(128)(2,1)S(1)}, bf16[768]{0:T(1024)(128)(2,1)}, u32[]{:S(2)}) copy-start(bf16[768]{0:T(1024)(128)(2,1)} %param.26) | copy-start | bytes 4612
  0.7 6.3 %copy-start.24 = (bf16[768]{0:T(1024)(128)(2,1)S(1)}, bf16[768]{0:T(1024)(128)(2,1)}, u32[]{:S(2)}) copy-start(bf16[768]{0:T(1024)(128)(2,1)} %param.23) | copy-start | bytes 4612
  2.7 14.6 %copy-start.6 = (bf16[768,768]{1,0:T(8,128)(2,1)S(1)}, bf16[768,768]{1,0:T(8,128)(2,1)}, u32[]{:S(2)}) copy-start(bf16[768,768]{1,0:T(8,128)(2,1)} %refs_14_.1) | copy-start | bytes 3538948
  2.7 13.2 %collective-permute-start = (bf16[2,128,768]{2,1,0:T(8,128)(2,1)}, bf16[2,128,768]{2,1,0:T(8,128)(2,1)}, u32[]{:S(2)}, u32[]{:S(2)}) collective-permute-start(bf16[2,128,768]{2,1,0:T(8,128)(2,1)} %get-tuple-element.62), channel_id=1, source_target_pairs={{0,1},{1,0},{2,3},{3,2},{4,5},{5,4},{6,7},{7,6},{8,9},{9,8},{10,11... | collective-permute-start | bytes 1179656 | tf_op jit(solution)/shard_map/ppermute | solution.py:700
  5.7 37.7 %collective-permute-start.2 = (bf16[2,128,768]{2,1,0:T(8,128)(2,1)S(1)}, bf16[2,128,768]{2,1,0:T(8,128)(2,1)S(1)}, u32[]{:S(2)}, u32[]{:S(2)}) collective-permute-start(bf16[2,128,768]{2,1,0:T(8,128)(2,1)S(1)} %get-tuple-element.57), channel_id=1, source_target_pairs={{0,1},{1,0},{2,3},{3,2},{4,5},{5,4},{6,7},{7,6},{8,9},{9,8},{10,11... | collective-permute-start | bytes 1179656 | tf_op jit(solution)/shard_map/ppermute | solution.py:700
  17.3 11.7 %copy-start.3 = (bf16[2,256,768]{2,1,0:T(8,128)(2,1)}, bf16[2,256,768]{2,1,0:T(8,128)(2,1)S(1)}, u32[]{:S(2)}) copy-start(bf16[2,256,768]{2,1,0:T(8,128)(2,1)S(1)} %maximum_select_fusion) | copy-start | bytes 2359300
  17.3 1.7 copy-start.7
  17.3 1.7 copy-start.21
  19.0 1.7 copy-start.5
  19.0 1.7 copy-start.20
  20.7 1.7 copy-start.17
  22.3 6.7 %copy-start.8 = (bf16[768,768]{1,0:T(8,128)(2,1)S(1)}, bf16[768,768]{1,0:T(8,128)(2,1)}, u32[]{:S(2)}) copy-start(bf16[768,768]{1,0:T(8,128)(2,1)} %refs_16_.1) | copy-start | bytes 3538948
  22.3 6.7 %copy-start.22 = (f32[768]{0:T(1024)S(1)}, f32[768]{0:T(1024)}, u32[]{:S(2)}) copy-start(f32[768]{0:T(1024)} %convert_element_type.96) | copy-start | bytes 9220
  31.1 0.7 copy-start.16
  31.4 9.0 %slice-start = ((s8[4718592]{0:T(1024)(128)(4,1)}), s8[4194304]{0:T(1024)(128)(4,1)S(1)}, s32[]{:S(2)}) async-start(s8[4718592]{0:T(1024)(128)(4,1)} %bitcast.39), calls=%async_computation | async-start | bytes 8388608
  31.7 8.6 %copy-start.4 = (bf16[512,768]{1,0:T(8,128)(2,1)}, bf16[512,768]{1,0:T(8,128)(2,1)S(1)}, u32[]{:S(2)}) copy-start(bf16[512,768]{1,0:T(8,128)(2,1)S(1)} %get-tuple-element.52.refs_9_) | copy-start | bytes 2359300
  31.8 8.6 %copy-start = (f32[512,768]{1,0:T(8,128)}, f32[512,768]{1,0:T(8,128)S(1)}, u32[]{:S(2)}) copy-start(f32[512,768]{1,0:T(8,128)S(1)} %get-tuple-element.53.refs_12_) | copy-start | bytes 4718596
  31.8 8.6 %slice-start.1 = ((s8[4718592]{0:T(1024)(128)(4,1)}), s8[524288]{0:T(1024)(128)(4,1)S(1)}, s32[]{:S(2)}) async-start(s8[4718592]{0:T(1024)(128)(4,1)} %bitcast.39), calls=%async_computation.1 | async-start | bytes 1048576
  31.8 8.6 %copy-start.19 = (f32[768]{0:T(1024)S(1)}, f32[768]{0:T(1024)}, u32[]{:S(2)}) copy-start(f32[768]{0:T(1024)} %convert_element_type.102) | copy-start | bytes 9220
  46.5 6.5 %copy-start.2 = (bf16[512,768]{1,0:T(8,128)(2,1)}, bf16[512,768]{1,0:T(8,128)(2,1)S(1)}, u32[]{:S(2)}) copy-start(bf16[512,768]{1,0:T(8,128)(2,1)S(1)} %get-tuple-element.50.refs_10_) | copy-start | bytes 2359300
  46.6 161.6 %collective-permute-start.1 = (bf16[2,128,768]{2,1,0:T(8,128)(2,1)S(1)}, bf16[2,128,768]{2,1,0:T(8,128)(2,1)S(1)}, u32[]{:S(2)}, u32[]{:S(2)}) collective-permute-start(bf16[2,128,768]{2,1,0:T(8,128)(2,1)S(1)} %get-tuple-element.60), channel_id=1, source_target_pairs={{0,1},{1,0},{2,3},{3,2},{4,5},{5,4},{6,7},{7,6},{8,9},{9,8},{10,11... | collective-permute-start | bytes 1179656 | tf_op jit(solution)/shard_map/ppermute | solution.py:700
  188.3 7.5 %copy-start.1 = (bf16[3072,768]{1,0:T(8,128)(2,1)S(1)}, bf16[3072,768]{1,0:T(8,128)(2,1)}, u32[]{:S(2)}) copy-start(bf16[3072,768]{1,0:T(8,128)(2,1)} %get-tuple-element.36) | copy-start | bytes 14155780
  195.8 4.5 %copy-start.12 = (bf16[768,768]{1,0:T(8,128)(2,1)S(1)}, bf16[768,768]{1,0:T(8,128)(2,1)}, u32[]{:S(2)}) copy-start(bf16[768,768]{1,0:T(8,128)(2,1)} %get-tuple-element.30) | copy-start | bytes 3538948
  200.3 1.7 copy-start.11
  201.9 1.7 copy-start.10
  203.6 1.7 copy-start.9
  205.3 1.6 copy-start.15
  206.9 2.3 %copy-start.13 = (bf16[4,128,768]{2,1,0:T(8,128)(2,1)S(1)}, bf16[4,128,768]{2,1,0:T(8,128)(2,1)}, u32[]{:S(2)}) copy-start(bf16[4,128,768]{2,1,0:T(8,128)(2,1)} %get-tuple-element.87) | copy-start | bytes 2359300

commit v5 on v4

--- a/solution.py
+++ b/solution.py
@@ -80,7 +80,7 @@
 
 
 def add_rows(acc, at, rb, rb_at, n):
-    step = min(n, 64)
+    step = 64 if n > 64 else min(n, 32)
 
     def body(i, carry):
         d = pl.multiple_of(at + i * step, 16)
@@ -280,10 +280,17 @@
 
 
 KINDS = "ABCABDABCABDABCABD"
-START = tuple((0, 1, 2, 3, 6, 6)[t // 3] for t in range(18))
+ORDER = (
+    1, 4, 0, 3, 2, -1, 5, -1, 1, 0, 3, 2, 5, -1, 4, -1, -1, 2, 7, -1, 0, 6, 1, 8, 5, -1, 7, 6, 2, -1, 3, 8, 4, -1, 0, 1,
+    -1, 5, 2, -1, 0, 9, 6, 11, 10, 7, 1, 8, -1, 4, 9, 0, 2, 5, 3, 11, 1, -1, 10, -1, 5, 0, 6, 4, 3, -1, 8, 5, 9, 6, 0, 7,
+    4, 2, 1, -1, 10, 2, 5, 3, 8, 6, 0, 4, 1, 11, -1, 10, 7, 1, 5, 0, 9, 2, 6, 8, -1, -1, 1, 9, 10, 12, 13, 8, 7, 14, 11, 0,
+    3, 4, -1, 1, 8, 2, 15, 5, 17, 13, 7, 14, 9, 6, 3, 16, 11, 12, 17, 10, 8, 15, 2, 16, -1, 14, 17, 3, 13, 4, 1, 6, 5, 0, 12, 7,
+    2, 9, 10, 11, 3, 4, 15, 16, 14, 13, 6, 8, 0, 17, 5, 11, 12, 7, 4, 3, 13, 9, 1, 14, 12, 10, 16, 15, 8, 16, 11, 6, 17, 5, 15, 13,
+    12, 3, 9, 7, 10, 16, 15, 13, 14, 11, 17, 2, 9, 12, 10, 16, 13, 14, 8, 15, 4, 6, 7, 3, 17, 12, 9, 11, 14, 16, 8, 13, 17, 4, 10, 12,
+    12, 15, 13, 11, 15, 16, 7, 9, 14, 17, 11, 16, 6, 15, 9, 10, 14, 13, 12, 17, 16, 15, 10, 14, 14, 17, 13, 12, 17, 15, 16, 13, 11, 12, 14, 17,
+    7, 15, 16,
+)
 SMALL = 16
-SMALL_START = 8
-LAG = 1
 
 
 def block_of(refs, half, t):
@@ -402,9 +409,12 @@
         if n == 0:
             fetch("dffn").wait()
 
-        d = (nt(v["dffn"][...], wou[n % 2]) * gp[n % 2].astype(f32)).astype(jnp.bfloat16)
-        dp[...] = d
-        small[0, 8 + order[n]:9 + order[n], :] = jnp.sum(d.astype(f32), axis=0, keepdims=True)
+        def body(at, total):
+            d = (nt(v["dffn"][at, :], wou[n % 2]) * gp[n % 2, at, :].astype(f32)).astype(jnp.bfloat16)
+            dp[at, :] = d
+            return total + jnp.sum(d.astype(f32), axis=0, keepdims=True)
+
+        small[0, 8 + order[n]:9 + order[n], :] = by_rows(256, body, none)
         if n + 2 < 4:
             tile(0, n + 2).start()
             tile(2, n + 2).start()
@@ -419,7 +429,11 @@
         if n == 0:
             fetch("dmid").wait()
 
-        v["dmid"][...] += nt(dp[...], win[n % 2])
+        def body(at, carry):
+            v["dmid"][at, :] += nt(dp[at, :], win[n % 2])
+            return carry
+
+        by_rows(256, body)
         if n + 2 < 4:
             tile(1, n + 2).start()
 
@@ -454,19 +468,24 @@
         fetch("ctx").wait()
         grad_blocks(v["ctx"], db, 1, 15)
 
-    def attention(seq, first, pairs):
-        if seq == 0 and first == 0:
+    def attention(seq, count):
+        if seq == 0:
             for name in ("q", "k", "v"):
                 fetch(name).wait()
         at = pl.ds(seq * length, length)
         bias = jnp.concatenate([bias_ref[at, :]] * (length // 128), axis=1)
 
-        columns = [pl.ds(p * 128, 128) for p in range(first, first + pairs)]
-        found = attend_back(
-            [(v["q"][at, c], v["k"][at, c], v["v"][at, c], dc[at, c], lse[seq, first + i]) for i, c in enumerate(columns)],
-            bias)
-        for c, (d_query, d_key, d_value) in zip(columns, found):
-            dq[at, c], dk[at, c], dv[at, c] = d_query, d_key, d_value
+        def body(step, carry):
+            first = step * count
+            columns = [pl.ds(pl.multiple_of((first + i) * 128, 128), 128) for i in range(count)]
+            found = attend_back(
+                [(v["q"][at, c], v["k"][at, c], v["v"][at, c], dc[at, c], lse[seq, first + i]) for i, c in enumerate(columns)],
+                bias)
+            for c, (d_query, d_key, d_value) in zip(columns, found):
+                dq[at, c], dk[at, c], dv[at, c] = d_query, d_key, d_value
+            return carry
+
+        lax.fori_loop(0, lse.shape[1] // count, body, 0)
 
     def total_rows(ref, row):
         def body(at, total):
@@ -495,18 +514,22 @@
             src_ref=source, dst_ref=to, send_sem=isem.at[0, seq], recv_sem=isem.at[1, seq],
             device_id=w.peer("x"), device_id_type=MESH)
 
-    def input_rows(seq):
-        if seq == 0:
-            for name in ("wq", "wk", "wv"):
-                fetch(name).wait()
-
-        at = pl.ds(seq * length, length)
-        total = v["dmid"][at, :] + nt(dq[at, :], v["wq"][...])
-        total = total + nt(dk[at, :], v["wk"][...]) + nt(dv[at, :], v["wv"][...])
-        for i in range(length // 128):
-            ig[2 * seq + i] = total[i * 128:i * 128 + 128].astype(jnp.bfloat16)
-        grad_copy(seq, True).start()
-        grad_copy(seq, False).start()
+    def input_rows():
+        for name in ("wq", "wk", "wv"):
+            fetch(name).wait()
+
+        def body(seq, carry):
+            at = pl.ds(pl.multiple_of(seq * length, length), length)
+            total = v["dmid"][at, :] + nt(dq[at, :], v["wq"][...])
+            total = total + nt(dk[at, :], v["wk"][...]) + nt(dv[at, :], v["wv"][...])
+            for i in range(length // 128):
+                ig[2 * seq + i] = total[i * 128:i * 128 + 128].astype(jnp.bfloat16)
+            return carry
+
+        lax.fori_loop(0, lse.shape[0], body, 0)
+        for seq in range(lse.shape[0]):
+            grad_copy(seq, True).start()
+            grad_copy(seq, False).start()
 
     small[0, 12:16, :] = jnp.zeros((4, LANES), f32)
     for row, ref in ((5, sum_outer), (6, sum_gain), (7, sum_shift)):
@@ -525,12 +548,10 @@
         if k < len(hops):
             small_copy(k).start()
 
-    seqs, pairs = lse.shape[:2]
-    ffn = [job for n in range(4) for job in ((d_pre, n), (inner_blocks, n), (d_mid, n))]
-    attn = [(attention, seq, first, 3) for seq in range(seqs) for first in range(0, pairs, 3)]
-    work = [ffn[:3], ffn[3:7], ffn[7:], [(norm_step,), (d_context,), (out_blocks,)] + attn[:1]]
-    work += [attn[1:], [(query_blocks,), (value_blocks,), (key_blocks,)]]
-    work.append([(input_rows, seq) for seq in range(seqs)])
+    seqs = lse.shape[0]
+    work = [job for n in range(4) for job in ((d_pre, n), (inner_blocks, n), (d_mid, n))]
+    work += [(norm_step,), (d_context,), (out_blocks,)] + [(attention, seq, 3) for seq in range(seqs)]
+    work += [(query_blocks,), (value_blocks,), (key_blocks,), (input_rows,)]
 
     def comm(t, p):
         if t == count:
@@ -543,17 +564,24 @@
         if p == len(tasks.steps[t]) - 1:
             store(t).start()
 
-    ops = [(START[t] + p, t, p) for t in range(count) for p in range(len(tasks.steps[t]) + 1)]
-    ops += [(SMALL_START + k, count, k) for k in range(len(hops) + 1)]
-    for slot in range(max(op[0] for op in ops) + 1):
-        now = sorted(op for op in ops if op[0] == slot)
-        jobs = work[slot] if slot < len(work) else []
-        marks = [(i * len(now)) // max(len(jobs), 1) + LAG for i in range(len(jobs))]
-        for i, (_, t, p) in enumerate(now):
-            for job, mark in zip(jobs, marks):
-                if min(mark, len(now) - 1) == i:
-                    job[0](*job[1:])
-            comm(t, p)
+    at, vectors, since = [0] * count, 0, 0
+    for t in ORDER:
+        if t < 0:
+            job = work.pop(0)
+            job[0](*job[1:])
+            continue
+        comm(t, at[t])
+        at[t] += 1
+        since += 1
+        if len(work) < 2 and since >= 6 and vectors <= len(hops):
+            comm(count, vectors)
+            vectors, since = vectors + 1, 0
+    for k in range(vectors, len(hops) + 1):
+        comm(count, k)
+    for _ in range(extra_bits):
+        for t in range(count):
+            comm(t, at[t])
+            at[t] += 1
     small_out[...] = small[len(hops)]
     for t in range(count):
         store(t).wait()
@@ -693,6 +721,23 @@
     )(q, k, v, bias)
 
 
+def widen_kernel(*refs):
+    for source, to in zip(refs[:len(refs) // 2], refs[len(refs) // 2:]):
+        to[...] = source[...].astype(jnp.float32)
+
+
+def to_float32(arrays):
+    steps = 12
+    blocks = [pl.BlockSpec((a.shape[0] // steps, a.shape[1]), lambda i: (i, 0)) for a in arrays]
+    return pl.pallas_call(
+        widen_kernel,
+        grid=(steps,),
+        out_shape=tuple(jax.ShapeDtypeStruct(a.shape, jnp.float32) for a in arrays),
+        in_specs=blocks,
+        out_specs=tuple(blocks),
+    )(*arrays)
+
+
 epsilon = 1e-05
 
 
@@ -814,21 +859,24 @@
         (factor_one, gain_attn.astype(f32).reshape(1, -1), lse, bias, grad_b_outer, grad_gain_ffn, grad_shift_ffn),
         hidden_in.shape,
     )
+    s_outer, s_inner, s_query, s_key, s_value, s_attn_out = to_float32(
+        (s_outer, s_inner, s_query, s_key, s_value, s_attn_out)
+    )
     return (
         layer_out,
         input_grad,
-        s_query.astype(f32),
+        s_query,
         small[0],
-        s_key.astype(f32),
-        s_value.astype(f32),
+        s_key,
+        s_value,
         small[1],
-        s_attn_out.astype(f32),
+        s_attn_out,
         small[2],
         small[3],
         small[4],
-        s_inner.astype(f32),
+        s_inner,
         small[8:12].reshape(-1),
-        s_outer.astype(f32),
+        s_outer,
         small[5],
         small[6],
         small[7],

time: 214 us -> 214 us (level); the launches traced: 210 us -> 213 us
  other arithmetic: 32.5 us -> 14.8 us
  Pallas kernels: 138 us -> 152 us
  waiting for transfers between devices: 0.37 us -> 6.33 us
    convert_element_type x6 -> x0, other arithmetic: 18.3 us -> none  [the longest x1 7.52 us: on_device(): s_inner.astype(f32)]
    pallas_call x0 -> x1, Pallas kernels: none -> 15.7 us  [to_float32(): pl.pallas_call(widen_kernel, grid=(steps,), out_shape=tuple((jax.ShapeDty...]
    ppermute x3, waiting for transfers between devices: 0.37 us -> 6.33 us  [to_partner(): return lax.ppermute(block, 'mod', [(0, 1), (1, 0)])]
  transfers between devices with their start and end apart: 3 -> 3, of which waited for: 1 -> 1; matrix products, arithmetic and copies ran while one was open for 27% -> 10% of each run, Pallas kernels for 66% -> 69%
where the time goes in v5:
time: 214 us; the launch traced here: 213 us
  Pallas kernels  152 us (71%)
  matrix products  22.6 us (11%)
  other arithmetic  14.8 us (7%)
  local copies, waits for them, and re-layouts  11.4 us (5%)
  waiting for transfers between devices  6.33 us (3%)
  starting transfers between devices  4.86 us (2%)
    pallas_call x1, Pallas kernels, backward(): pl.pallas_call(functools.partial(back_kernel, extra_bits), out_shape=tupl...  131 us
    dot_general x6, matrix products, linear(): lax.dot_general(rows, weight_matrix, (((1,), (0,)), ((), ())), preferred_...  18.3 us
    pallas_call x1, Pallas kernels, to_float32(): pl.pallas_call(widen_kernel, grid=(steps,), out_shape=tuple((jax.ShapeDty...  15.7 us
    ppermute x3, waiting for transfers between devices, to_partner(): return lax.ppermute(block, 'mod', [(0, 1), (1, 0)])  6.33 us
    pallas_call x1, Pallas kernels, attention_forward(): pl.pallas_call(forward_kernel, grid=(seqs,), out_shape=(jax.ShapeDtypeStr...  5.66 us
    ppermute x3, starting transfers between devices, to_partner(): return lax.ppermute(block, 'mod', [(0, 1), (1, 0)])  4.86 us
    dot_general x1, matrix products, weight_grad(): lax.dot_general(layer_inputs, gradient_rows, (((0,), (0,)), ((), ())), pr...  4.31 us
  transfers between devices with their start and end apart: 3, of which 1 were waited for; matrix products, arithmetic and copies ran while one was open for 10% of the time, Pallas kernels for 69%

profile of v5, /device:TPU:0, one launch (start us, length us, event | category | flops | bytes accessed | tf_op | source)
XLA Modules:
  0.0 213.3 jit_solution(16809595393968998037)
XLA Ops:
  0.7 0.0 copy-start.9
  0.7 2.0 constant_dynamic-slice_fusion
  2.7 3.0 %collective-permute-start.2 = (bf16[2,128,768]{2,1,0:T(8,128)(2,1)}, bf16[2,128,768]{2,1,0:T(8,128)(2,1)S(1)}, u32[]{:S(2)}, u32[]{:S(2)}) collective-permute-start(bf16[2,128,768]{2,1,0:T(8,128)(2,1)} %get-tuple-element.69), channel_id=1, source_target_pairs={{0,1},{1,0},{2,3},{3,2},{4,5},{5,4},{6,7},{7,6},{8,9},{9,8},{10,11... | collective-permute-start | bytes 1179656 | tf_op jit(solution)/shard_map/ppermute | solution.py:745
  5.7 0.1 constant_dynamic-slice_fusion.6
  5.7 0.0 copy-start.5
  5.7 0.1 collective-permute-start
  5.8 0.6 broadcast_in_dim.21.refs_18_
  6.4 0.7 dynamic_slice.27
  7.1 0.8 fusion.15
  7.9 0.6 copy.37
  8.5 0.0 copy-done.21
  8.5 0.6 convert_element_type.80
  9.1 1.3 convert_element_type.73
  10.4 1.3 convert_element_type.76
  11.6 1.3 convert_element_type.78
  12.9 1.3 convert_element_type.84
  14.2 0.7 convert_element_type.86
  14.9 1.3 convert_element_type.82
  16.2 0.0 collective-permute-done.2
  16.2 0.4 convert_reduce_fusion
  16.6 0.6 copy.38
  17.2 6.3 %collective-permute-done = bf16[2,128,768]{2,1,0:T(8,128)(2,1)} collective-permute-done((bf16[2,128,768]{2,1,0:T(8,128)(2,1)S(1)}, bf16[2,128,768]{2,1,0:T(8,128)(2,1)}, u32[]{:S(2)}, u32[]{:S(2)}) %collective-permute-start) | collective-permute-done | bytes 393248 | tf_op jit(solution)/shard_map/ppermute | solution.py:745
  23.5 1.3 maximum_select_fusion
  24.8 0.0 copy-start.2
  24.8 0.0 copy-done.5
  24.8 0.0 copy-start.6
  24.9 0.0 copy-start.19
  24.9 1.7 convolution_convert_fusion.1.k_ref.refs_5_
  26.5 1.7 add_convert_fusion.1.v_ref.refs_6_
  28.2 0.0 copy-done.18
  28.2 1.7 fusion.13.q_ref.refs_4_
  29.9 0.8 broadcast_in_dim.20.bias_ref.refs_20_
  30.7 5.7 %shard_map.314 = (bf16[512,768]{1,0:T(8,128)(2,1)}, f32[2,6,2,256]{3,2,1,0:T(2,128)}) custom-call(bf16[512,768]{1,0:T(8,128)(2,1)} %fusion.13.q_ref.refs_4_, bf16[512,768]{1,0:T(8,128)(2,1)} %convolution_convert_fusion.1.k_ref.refs_5_, bf16[512,768]{1,0:T(8,128)(2,1)} %add_convert_fusion.1.v_ref.refs_6_, f32[512,128]{1,0:T(8,128)} %broadcast_in_dim.20.bias_ref.refs_20_), custom_call_target="tpu_custom_call" | custom-call | tf_op jit(solution)/shard_map/pallas_call | solution.py:715
  36.4 2.0 fusion.17
  38.4 0.0 copy-start.12
  38.5 0.3 multiply_reduce_fusion.1
  38.8 0.3 copy-done.11
  39.1 0.3 fusion.12
  39.5 0.0 copy-start
  39.5 0.0 copy-done.12
  39.5 0.0 slice-start.1
  39.5 0.0 copy-start.16
  39.5 8.5 %fusion.4 = (bf16[512,3072]{1,0:T(8,128)(2,1)}, bf16[512,3072]{1,0:T(8,128)(2,1)S(1)}) fusion(f32[3072]{0:T(1024)S(1)} %copy-done.12, bf16[512,768]{1,0:T(8,128)(2,1)S(1)} %get-tuple-element.64.refs_9_, bf16[768,3072]{1,0:T(8,128)(2,1)} %refs_2_.1), kind=kOutput, calls=%fused_computation.5 | convolution fusion | flops 2434793472 | bytes 11808768 | tf_op jit(solution)/shard_map/dot_general | solution.py:767
  48.1 0.0 slice-done
  48.1 2.7 %fusion.18 = (f32[512]{0:T(512)S(1)}, f32[512,768]{1,0:T(8,128)S(1)}) fusion(f32[768]{0:T(1024)S(1)} %copy-done.16, bf16[512,3072]{1,0:T(8,128)(2,1)S(1)} %get-tuple-element.67, bf16[3072,768]{1,0:T(8,128)(2,1)S(1)} %bitcast.40, f32[768]{0:T(1024)S(1)} %copy-done.11, f32[512,768]{1,0:T(8,128)S(1)} %get-tuple-element.65.refs_12_, ...), kind=kOutput, calls=%fused_computation.63 | convolution fusion | flops 2417884672 | bytes 11021312 | tf_op jit(solution)/shard_map/dot_general | solution.py:767
  50.8 0.3 multiply_reduce_fusion
  51.2 0.0 copy-start.13
  51.2 0.7 fusion.11
  51.9 1.9 convert_reduce_fusion.1
  53.8 0.1 constant_dynamic-slice_fusion.3
  53.8 1.8 collective-permute-start.1
  55.7 4.3 %convolution_convert_fusion.refs_0_ = bf16[3072,768]{1,0:T(8,128)(2,1)} fusion(bf16[512,3072]{1,0:T(8,128)(2,1)S(1)} %get-tuple-element.67, bf16[512,768]{1,0:T(8,128)(2,1)S(1)} %get-tuple-element.62.refs_10_), kind=kOutput, calls=%fused_computation.8 | convolution fusion | flops 2418278400 | bytes 8650752 | tf_op jit(solution)/shard_map/dot_general | solution.py:775
  60.0 0.6 broadcast_in_dim.24.refs_23_
  60.6 0.9 copy.36.refs_17_
  61.4 0.6 broadcast_in_dim.23.refs_22_
  62.0 0.6 broadcast_in_dim.22.refs_21_
  62.6 131.0 %shard_map.315 = (bf16[3072,768]{1,0:T(8,128)(2,1)}, bf16[768,3072]{1,0:T(8,128)(2,1)}, bf16[768,768]{1,0:T(8,128)(2,1)}, bf16[768,768]{1,0:T(8,128)(2,1)}, bf16...) custom-call(bf16[3072,768]{1,0:T(8,128)(2,1)} %convolution_convert_fusion.ref, ...), custom_call_target="tpu_custom_call" | custom-call | tf_op jit(solution)/shard_map/pallas_call | solution.py:604
  193.6 0.7 slice.32
  194.4 0.6 reshape.128
  195.0 15.7 %shard_map.316 = (f32[3072,768]{1,0:T(8,128)}, f32[768,3072]{1,0:T(8,128)}, f32[768,768]{1,0:T(8,128)}, f32[768,768]{1,0:T(8,128)}, f32[768,768]{1,0:T(8,128)}, /*index=5*/f32[768,768]{1,0:T(8,128)}) custom-call(bf16[3072,768]{1,0:T(8,128)(2,1)} %get-tuple-element.36.refs_0_, bf16[768,3072]{1,0:T(8,128)(2,1)} %get-tuple-element.37.refs_1_, ...), custom_call_target="tpu_custom_call" | custom-call | tf_op jit(solution)/shard_map/pallas_call | solution.py:732
  210.7 0.7 slice_reduce_fusion
  211.4 0.0 collective-permute-done.1
  211.4 1.0 maximum_select_fusion.1
  212.4 0.9 copy.40
  (42 shorter events, 0.1 us)
Async XLA Ops:
  0.7 5.0 %copy-start.9 = (bf16[4,128,768]{2,1,0:T(8,128)(2,1)S(1)}, bf16[4,128,768]{2,1,0:T(8,128)(2,1)}, u32[]{:S(2)}) copy-start(bf16[4,128,768]{2,1,0:T(8,128)(2,1)} %param.19) | copy-start | bytes 2359300
  0.7 5.1 %copy-start.15 = (bf16[768]{0:T(1024)(128)(2,1)S(1)}, bf16[768]{0:T(1024)(128)(2,1)}, u32[]{:S(2)}) copy-start(bf16[768]{0:T(1024)(128)(2,1)} %param.29) | copy-start | bytes 4612
  0.7 7.8 %copy-start.20 = (bf16[768]{0:T(1024)(128)(2,1)S(1)}, bf16[768]{0:T(1024)(128)(2,1)}, u32[]{:S(2)}) copy-start(bf16[768]{0:T(1024)(128)(2,1)} %param.35) | copy-start | bytes 4612
  0.7 7.8 %copy-start.21 = (bf16[768]{0:T(1024)(128)(2,1)S(1)}, bf16[768]{0:T(1024)(128)(2,1)}, u32[]{:S(2)}) copy-start(bf16[768]{0:T(1024)(128)(2,1)} %param.30) | copy-start | bytes 4612
  2.7 13.5 %collective-permute-start.2 = (bf16[2,128,768]{2,1,0:T(8,128)(2,1)}, bf16[2,128,768]{2,1,0:T(8,128)(2,1)S(1)}, u32[]{:S(2)}, u32[]{:S(2)}) collective-permute-start(bf16[2,128,768]{2,1,0:T(8,128)(2,1)} %get-tuple-element.69), channel_id=1, source_target_pairs={{0,1},{1,0},{2,3},{3,2},{4,5},{5,4},{6,7},{7,6},{8,9},{9,8},{10,11... | collective-permute-start | bytes 1179656 | tf_op jit(solution)/shard_map/ppermute | solution.py:745
  5.7 19.1 %copy-start.5 = (bf16[768,768]{1,0:T(8,128)(2,1)S(1)}, bf16[768,768]{1,0:T(8,128)(2,1)}, u32[]{:S(2)}) copy-start(bf16[768,768]{1,0:T(8,128)(2,1)} %refs_14_.1) | copy-start | bytes 3538948
  5.7 17.8 %collective-permute-start = (bf16[2,128,768]{2,1,0:T(8,128)(2,1)S(1)}, bf16[2,128,768]{2,1,0:T(8,128)(2,1)}, u32[]{:S(2)}, u32[]{:S(2)}) collective-permute-start(bf16[2,128,768]{2,1,0:T(8,128)(2,1)S(1)} %get-tuple-element.74), channel_id=1, source_target_pairs={{0,1},{1,0},{2,3},{3,2},{4,5},{5,4},{6,7},{7,6},{8,9},{9,8},{10,11... | collective-permute-start | bytes 1179656 | tf_op jit(solution)/shard_map/ppermute | solution.py:745
  24.8 11.6 %copy-start.2 = (bf16[2,256,768]{2,1,0:T(8,128)(2,1)}, bf16[2,256,768]{2,1,0:T(8,128)(2,1)S(1)}, u32[]{:S(2)}) copy-start(bf16[2,256,768]{2,1,0:T(8,128)(2,1)S(1)} %maximum_select_fusion) | copy-start | bytes 2359300
  24.8 1.7 copy-start.6
  24.9 1.7 copy-start.19
  26.5 1.7 copy-start.4
  26.5 1.7 copy-start.18
  28.2 1.7 copy-start.14
  29.9 6.5 %copy-start.7 = (bf16[768,768]{1,0:T(8,128)(2,1)S(1)}, bf16[768,768]{1,0:T(8,128)(2,1)}, u32[]{:S(2)}) copy-start(bf16[768,768]{1,0:T(8,128)(2,1)} %refs_16_.1) | copy-start | bytes 3538948
  29.9 6.5 %copy-start.17 = (f32[768]{0:T(1024)S(1)}, f32[768]{0:T(1024)}, u32[]{:S(2)}) copy-start(f32[768]{0:T(1024)} %convert_element_type.78) | copy-start | bytes 9220
  38.4 0.7 copy-start.11
  38.4 1.0 copy-start.12
  39.1 9.0 %slice-start = ((s8[4718592]{0:T(1024)(128)(4,1)}), s8[4194304]{0:T(1024)(128)(4,1)S(1)}, s32[]{:S(2)}) async-start(s8[4718592]{0:T(1024)(128)(4,1)} %bitcast.39), calls=%async_computation | async-start | bytes 8388608
  39.5 8.6 %copy-start.3 = (bf16[512,768]{1,0:T(8,128)(2,1)}, bf16[512,768]{1,0:T(8,128)(2,1)S(1)}, u32[]{:S(2)}) copy-start(bf16[512,768]{1,0:T(8,128)(2,1)S(1)} %get-tuple-element.64.refs_9_) | copy-start | bytes 2359300
  39.5 8.6 %copy-start = (f32[512,768]{1,0:T(8,128)}, f32[512,768]{1,0:T(8,128)S(1)}, u32[]{:S(2)}) copy-start(f32[512,768]{1,0:T(8,128)S(1)} %get-tuple-element.65.refs_12_) | copy-start | bytes 4718596
  39.5 8.6 %slice-start.1 = ((s8[4718592]{0:T(1024)(128)(4,1)}), s8[524288]{0:T(1024)(128)(4,1)S(1)}, s32[]{:S(2)}) async-start(s8[4718592]{0:T(1024)(128)(4,1)} %bitcast.39), calls=%async_computation.1 | async-start | bytes 1048576
  39.5 8.6 %copy-start.16 = (f32[768]{0:T(1024)S(1)}, f32[768]{0:T(1024)}, u32[]{:S(2)}) copy-start(f32[768]{0:T(1024)} %convert_element_type.84) | copy-start | bytes 9220
  51.2 0.8 copy-start.13
  53.8 6.2 %copy-start.1 = (bf16[512,768]{1,0:T(8,128)(2,1)}, bf16[512,768]{1,0:T(8,128)(2,1)S(1)}, u32[]{:S(2)}) copy-start(bf16[512,768]{1,0:T(8,128)(2,1)S(1)} %get-tuple-element.62.refs_10_) | copy-start | bytes 2359300
  53.8 157.5 %collective-permute-start.1 = (bf16[2,128,768]{2,1,0:T(8,128)(2,1)S(1)}, bf16[2,128,768]{2,1,0:T(8,128)(2,1)S(1)}, u32[]{:S(2)}, u32[]{:S(2)}) collective-permute-start(bf16[2,128,768]{2,1,0:T(8,128)(2,1)S(1)} %get-tuple-element.72), channel_id=1, source_target_pairs={{0,1},{1,0},{2,3},{3,2},{4,5},{5,4},{6,7},{7,6},{8,9},{9,8},{10,11... | collective-permute-start | bytes 1179656 | tf_op jit(solution)/shard_map/ppermute | solution.py:745
  195.0 15.7 %copy-start.10 = (f32[16,768]{1,0:T(8,128)S(1)}, f32[16,768]{1,0:T(8,128)}, u32[]{:S(2)}) copy-start(f32[16,768]{1,0:T(8,128)} %get-tuple-element.43) | copy-start | bytes 147460
  210.7 1.7 copy-start.8

commit v6 on v5

--- a/solution.py
+++ b/solution.py
@@ -750,9 +750,9 @@
     return lax.dynamic_slice_in_dim(array, side * half, half, axis)
 
 
-def gather_sequences(array, side):
+def gather_sequences(array, side, away):
     own = take_side(array, 0, side)
-    other = to_partner(take_side(array, 0, 1 - side))
+    other = to_partner(away)
     both = jnp.where(side == 0, jnp.concatenate((own, other), axis=1), jnp.concatenate((other, own), axis=1))
     return both.reshape(-1, array.shape[2])
 
@@ -820,8 +820,9 @@
     length = 2 * half_len
     side = lax.axis_index("mod")
     f32 = jnp.float32
-    rows_b = gather_sequences(hidden_in, side)
-    upstream = gather_sequences(cotangent, side).astype(f32)
+    rows_b = gather_sequences(hidden_in, side, take_side(hidden_in, 0, 1 - side))
+    rows_b, away = lax.optimization_barrier((rows_b, take_side(cotangent, 0, 1 - side)))
+    upstream = gather_sequences(cotangent, side, away).astype(f32)
     mask = take_side(text_mask, 0, side) == 1
     regions = take_side(region_count, 0, side)
     slot_ok = lax.broadcasted_iota(jnp.int32, mask.shape, 1) < regions[:, None]

time: 214 us -> 207 us (0.967)
  other arithmetic: 14.8 us -> 8.64 us
  local copies, waits for them, and re-layouts: 11.4 us -> 8.49 us
  transfers between devices with their start and end apart: 3 -> 3, of which waited for: 1 -> 1; matrix products, arithmetic and copies ran while one was open for 10% -> 16% of each run, Pallas kernels for 69% -> 75%
where the time goes in v6:
time: 207 us; the launch traced here: 206 us
  Pallas kernels  154 us (74%)
  matrix products  22.9 us (11%)
  other arithmetic  8.64 us (4%)
  local copies, waits for them, and re-layouts  8.49 us (4%)
  waiting for transfers between devices  5.84 us (3%)
  starting transfers between devices  5.19 us (3%)
    pallas_call x1, Pallas kernels, backward(): pl.pallas_call(functools.partial(back_kernel, extra_bits), out_shape=tupl...  133 us
    dot_general x6, matrix products, linear(): lax.dot_general(rows, weight_matrix, (((1,), (0,)), ((), ())), preferred_...  18.6 us
    pallas_call x1, Pallas kernels, to_float32(): pl.pallas_call(widen_kernel, grid=(steps,), out_shape=tuple((jax.ShapeDty...  15.7 us
    ppermute x3, waiting for transfers between devices, to_partner(): return lax.ppermute(block, 'mod', [(0, 1), (1, 0)])  5.84 us
    pallas_call x1, Pallas kernels, attention_forward(): pl.pallas_call(forward_kernel, grid=(seqs,), out_shape=(jax.ShapeDtypeStr...  5.67 us
    ppermute x3, starting transfers between devices, to_partner(): return lax.ppermute(block, 'mod', [(0, 1), (1, 0)])  5.19 us
    dot_general x1, matrix products, weight_grad(): lax.dot_general(layer_inputs, gradient_rows, (((0,), (0,)), ((), ())), pr...  4.31 us
  transfers between devices with their start and end apart: 3, of which 1 were waited for; matrix products, arithmetic and copies ran while one was open for 16% of the time, Pallas kernels for 75%

profile of v6, /device:TPU:0, one launch (start us, length us, event | category | flops | bytes accessed | tf_op | source)
XLA Modules:
  0.0 206.2 jit_solution(1388304682839965108)
XLA Ops:
  0.7 0.0 copy-start.12
  0.7 0.0 copy-start.23
  0.7 0.0 copy-start.22
  0.7 0.0 copy-start.15
  0.7 0.0 copy-start.16
  0.7 0.0 copy-start.17
  0.7 0.0 copy-start.18
  0.7 0.0 copy-start.19
  0.7 0.0 copy-start.20
  0.8 0.0 copy-start.21
  0.8 0.0 copy-start.13
  0.8 0.0 copy-start.8
  0.8 1.3 constant_dynamic-slice_fusion.6
  2.0 3.0 %collective-permute-start = (bf16[2,128,768]{2,1,0:T(8,128)(2,1)S(1)}, bf16[2,128,768]{2,1,0:T(8,128)(2,1)S(1)}, u32[]{:S(2)}, u32[]{:S(2)}) collective-permute-start(bf16[2,128,768]{2,1,0:T(8,128)(2,1)S(1)} %get-tuple-element.78), channel_id=1, source_target_pairs={{0,1},{1,0},{2,3},{3,2},{4,5},{5,4},{6,7},{7,6},{8,9},{9,8},{10,11... | collective-permute-start | bytes 1179656 | tf_op jit(solution)/shard_map/ppermute | solution.py:745
  5.1 0.6 broadcast_in_dim.21.refs_18_
  5.7 0.6 convert_element_type.79
  6.3 0.1 dynamic_slice.28
  6.3 0.1 fusion.15
  6.5 0.6 convert_element_type.80
  7.1 0.6 convert_element_type.84
  7.7 0.6 convert_element_type.82
  8.3 0.1 constant_dynamic-slice_fusion
  8.4 5.8 %collective-permute-done = bf16[2,128,768]{2,1,0:T(8,128)(2,1)S(1)} collective-permute-done((bf16[2,128,768]{2,1,0:T(8,128)(2,1)S(1)}, bf16[2,128,768]{2,1,0:T(8,128)(2,1)S(1)}, u32[]{:S(2)}, u32[]{:S(2)}) %collective-permute-start) | collective-permute-done | bytes 393248 | tf_op jit(solution)/shard_map/ppermute | solution.py:745
  14.2 0.3 maximum_select_fusion
  14.5 0.0 copy-start.6
  14.5 1.8 collective-permute-start.2
  16.3 1.7 convolution_convert_fusion.1.k_ref.refs_5_
  18.0 1.7 add_convert_fusion.1.v_ref.refs_6_
  19.7 0.0 copy-done.4
  19.7 1.7 fusion.13.q_ref.refs_4_
  21.3 0.8 broadcast_in_dim.20.bias_ref.refs_20_
  22.2 5.7 %shard_map.314 = (bf16[512,768]{1,0:T(8,128)(2,1)}, f32[2,6,2,256]{3,2,1,0:T(2,128)}) custom-call(bf16[512,768]{1,0:T(8,128)(2,1)} %fusion.13.q_ref.refs_4_, bf16[512,768]{1,0:T(8,128)(2,1)} %convolution_convert_fusion.1.k_ref.refs_5_, bf16[512,768]{1,0:T(8,128)(2,1)} %add_convert_fusion.1.v_ref.refs_6_, f32[512,128]{1,0:T(8,128)} %broadcast_in_dim.20.bias_ref.refs_20_), custom_call_target="tpu_custom_call" | custom-call | tf_op jit(solution)/shard_map/pallas_call | solution.py:715
  27.8 0.0 copy-done.2
  27.9 2.4 %fusion.17 = (f32[512]{0:T(512)S(1)}, f32[512,768]{1,0:T(8,128)S(1)}) fusion(f32[768]{0:T(1024)S(1)} %convert_element_type.78, bf16[512,768]{1,0:T(8,128)(2,1)} %get-tuple-element.36.refs_7_, bf16[768,768]{1,0:T(8,128)(2,1)} %refs_16_.1, bf16[512,768]{1,0:T(8,128)(2,1)S(1)} %bitcast.45), kind=kOutput, calls=%fused_computation.62 | convolution fusion | flops 605552128 | bytes 4330496 | tf_op jit(solution)/shard_map/dot_general | solution.py:767
  30.2 0.3 multiply_reduce_fusion.1
  30.6 0.9 copy.36.refs_17_
  31.4 1.2 fusion.12
  32.6 0.0 copy-start.3
  32.6 0.0 copy-start
  32.7 0.0 slice-start.1
  32.7 0.0 copy-start.10
  32.7 0.0 copy-start.11
  32.7 0.0 copy-start.14
  32.7 8.5 %fusion.4 = (bf16[512,3072]{1,0:T(8,128)(2,1)}, bf16[512,3072]{1,0:T(8,128)(2,1)S(1)}) fusion(f32[3072]{0:T(1024)} %convert_element_type.82, bf16[512,768]{1,0:T(8,128)(2,1)S(1)} %get-tuple-element.68.refs_9_, bf16[768,3072]{1,0:T(8,128)(2,1)} %refs_2_.1), kind=kOutput, calls=%fused_computation.5 | convolution fusion | flops 2434793472 | bytes 11808768 | tf_op jit(solution)/shard_map/dot_general | solution.py:767
  41.2 2.7 %fusion.18 = (f32[512]{0:T(512)S(1)}, f32[512,768]{1,0:T(8,128)S(1)}) fusion(f32[768]{0:T(1024)S(1)} %copy-done.14, bf16[512,3072]{1,0:T(8,128)(2,1)S(1)} %get-tuple-element.71, bf16[3072,768]{1,0:T(8,128)(2,1)S(1)} %bitcast.40, f32[768]{0:T(1024)S(1)} %copy-done.11, f32[512,768]{1,0:T(8,128)S(1)} %get-tuple-element.69.refs_12_, f32[768]{0:T(1024)S(1)} %copy-done.10), kind=kOutput, calls=%fused_computation.63 | convolution fusion | flops 2417884672 | bytes 11021312 | tf_op jit(solution)/shard_map/dot_general | solution.py:767
  44.0 0.3 multiply_reduce_fusion
  44.3 0.0 collective-permute-done.2
  44.3 0.4 convert_reduce_fusion
  44.7 0.7 fusion.11
  45.5 1.9 convert_reduce_fusion.1
  47.3 0.1 constant_dynamic-slice_fusion.2
  47.4 0.4 collective-permute-start.1
  47.8 4.3 %convolution_convert_fusion.refs_0_ = bf16[3072,768]{1,0:T(8,128)(2,1)} fusion(bf16[512,3072]{1,0:T(8,128)(2,1)S(1)} %get-tuple-element.71, bf16[512,768]{1,0:T(8,128)(2,1)S(1)} %get-tuple-element.66.refs_10_), kind=kOutput, calls=%fused_computation.8 | convolution fusion | flops 2418278400 | bytes 8650752 | tf_op jit(solution)/shard_map/dot_general | solution.py:775
  52.1 0.6 broadcast_in_dim.24.refs_23_
  52.6 0.6 broadcast_in_dim.23.refs_22_
  53.2 0.6 broadcast_in_dim.22.refs_21_
  53.8 132.8 %shard_map.315 = (bf16[3072,768]{1,0:T(8,128)(2,1)}, bf16[768,3072]{1,0:T(8,128)(2,1)}, bf16[768,768]{1,0:T(8,128)(2,1)}, bf16[768,768]{1,0:T(8,128)(2,1)}, bf16...) custom-call(bf16[3072,768]{1,0:T(8,128)(2,1)} %convolution_convert_fusion.ref, ...), custom_call_target="tpu_custom_call" | custom-call | tf_op jit(solution)/shard_map/pallas_call | solution.py:604
  186.6 0.7 slice.32
  187.3 0.6 reshape.128
  188.0 15.7 %shard_map.316 = (f32[3072,768]{1,0:T(8,128)}, f32[768,3072]{1,0:T(8,128)}, f32[768,768]{1,0:T(8,128)}, f32[768,768]{1,0:T(8,128)}, f32[768,768]{1,0:T(8,128)}, /*index=5*/f32[768,768]{1,0:T(8,128)}) custom-call(bf16[3072,768]{1,0:T(8,128)(2,1)} %get-tuple-element.40.refs_0_, bf16[768,3072]{1,0:T(8,128)(2,1)} %get-tuple-element.41.refs_1_, ...), custom_call_target="tpu_custom_call" | custom-call | tf_op jit(solution)/shard_map/pallas_call | solution.py:732
  203.7 0.7 slice_reduce_fusion
  204.3 0.0 collective-permute-done.1
  204.3 1.0 maximum_select_fusion.1
  205.3 0.9 copy.40
  (46 shorter events, 0.1 us)
Async XLA Ops:
  0.7 4.4 %copy-start.12 = (bf16[768]{0:T(1024)(128)(2,1)S(1)}, bf16[768]{0:T(1024)(128)(2,1)}, u32[]{:S(2)}) copy-start(bf16[768]{0:T(1024)(128)(2,1)} %param.29) | copy-start | bytes 4612
  0.7 5.6 %copy-start.23 = (s32[4]{0:T(128)S(1)}, s32[4]{0:T(128)}, u32[]{:S(2)}) copy-start(s32[4]{0:T(128)} %param.21) | copy-start | bytes 52
  0.7 5.7 %copy-start.22 = (s32[4,128]{1,0:T(4,128)S(1)}, s32[4,128]{1,0:T(4,128)}, u32[]{:S(2)}) copy-start(s32[4,128]{1,0:T(4,128)} %param.20) | copy-start | bytes 6148
  0.7 5.7 %copy-start.15 = (bf16[768]{0:T(1024)(128)(2,1)S(1)}, bf16[768]{0:T(1024)(128)(2,1)}, u32[]{:S(2)}) copy-start(bf16[768]{0:T(1024)(128)(2,1)} %param.35) | copy-start | bytes 4612
  0.7 5.7 %copy-start.16 = (bf16[768]{0:T(1024)(128)(2,1)S(1)}, bf16[768]{0:T(1024)(128)(2,1)}, u32[]{:S(2)}) copy-start(bf16[768]{0:T(1024)(128)(2,1)} %param.30) | copy-start | bytes 4612
  0.7 6.3 %copy-start.17 = (bf16[768]{0:T(1024)(128)(2,1)S(1)}, bf16[768]{0:T(1024)(128)(2,1)}, u32[]{:S(2)}) copy-start(bf16[768]{0:T(1024)(128)(2,1)} %param.23) | copy-start | bytes 4612
  0.7 6.3 %copy-start.18 = (bf16[768]{0:T(1024)(128)(2,1)S(1)}, bf16[768]{0:T(1024)(128)(2,1)}, u32[]{:S(2)}) copy-start(bf16[768]{0:T(1024)(128)(2,1)} %param.26) | copy-start | bytes 4612
  0.7 6.3 %copy-start.19 = (bf16[768]{0:T(1024)(128)(2,1)S(1)}, bf16[768]{0:T(1024)(128)(2,1)}, u32[]{:S(2)}) copy-start(bf16[768]{0:T(1024)(128)(2,1)} %param.28) | copy-start | bytes 4612
  0.7 6.3 %copy-start.20 = (bf16[768]{0:T(1024)(128)(2,1)S(1)}, bf16[768]{0:T(1024)(128)(2,1)}, u32[]{:S(2)}) copy-start(bf16[768]{0:T(1024)(128)(2,1)} %param.34) | copy-start | bytes 4612
  0.8 6.9 %copy-start.21 = (bf16[768]{0:T(1024)(128)(2,1)S(1)}, bf16[768]{0:T(1024)(128)(2,1)}, u32[]{:S(2)}) copy-start(bf16[768]{0:T(1024)(128)(2,1)} %param.36) | copy-start | bytes 4612
  0.8 6.9 %copy-start.13 = (bf16[3072]{0:T(1024)(128)(2,1)S(1)}, bf16[3072]{0:T(1024)(128)(2,1)}, u32[]{:S(2)}) copy-start(bf16[3072]{0:T(1024)(128)(2,1)} %param.32) | copy-start | bytes 18436
  0.8 7.5 %copy-start.8 = (bf16[4,128,768]{2,1,0:T(8,128)(2,1)S(1)}, bf16[4,128,768]{2,1,0:T(8,128)(2,1)}, u32[]{:S(2)}) copy-start(bf16[4,128,768]{2,1,0:T(8,128)(2,1)} %param.37) | copy-start | bytes 2359300
  2.0 12.1 %collective-permute-start = (bf16[2,128,768]{2,1,0:T(8,128)(2,1)S(1)}, bf16[2,128,768]{2,1,0:T(8,128)(2,1)S(1)}, u32[]{:S(2)}, u32[]{:S(2)}) collective-permute-start(bf16[2,128,768]{2,1,0:T(8,128)(2,1)S(1)} %get-tuple-element.78), channel_id=1, source_target_pairs={{0,1},{1,0},{2,3},{3,2},{4,5},{5,4},{6,7},{7,6},{8,9},{9,8},{10,11... | collective-permute-start | bytes 1179656 | tf_op jit(solution)/shard_map/ppermute | solution.py:745
  8.3 8.0 %copy-start.5 = (bf16[768,768]{1,0:T(8,128)(2,1)S(1)}, bf16[768,768]{1,0:T(8,128)(2,1)}, u32[]{:S(2)}) copy-start(bf16[768,768]{1,0:T(8,128)(2,1)} %refs_14_.1) | copy-start | bytes 3538948
  14.5 13.3 %copy-start.2 = (bf16[2,256,768]{2,1,0:T(8,128)(2,1)}, bf16[2,256,768]{2,1,0:T(8,128)(2,1)S(1)}, u32[]{:S(2)}) copy-start(bf16[2,256,768]{2,1,0:T(8,128)(2,1)S(1)} %maximum_select_fusion) | copy-start | bytes 2359300
  14.5 3.5 %copy-start.6 = (bf16[768,768]{1,0:T(8,128)(2,1)S(1)}, bf16[768,768]{1,0:T(8,128)(2,1)}, u32[]{:S(2)}) copy-start(bf16[768,768]{1,0:T(8,128)(2,1)} %refs_15_.1) | copy-start | bytes 3538948
  14.5 29.8 %collective-permute-start.2 = (bf16[2,128,768]{2,1,0:T(8,128)(2,1)S(1)}, bf16[2,128,768]{2,1,0:T(8,128)(2,1)S(1)}, u32[]{:S(2)}, u32[]{:S(2)}) collective-permute-start(bf16[2,128,768]{2,1,0:T(8,128)(2,1)S(1)} %get-tuple-element.37), channel_id=1, source_target_pairs={{0,1},{1,0},{2,3},{3,2},{4,5},{5,4},{6,7},{7,6},{8,9},{9,8},{10,11... | collective-permute-start | bytes 1179656 | tf_op jit(solution)/shard_map/ppermute | solution.py:745
  18.0 1.7 copy-start.4
  31.4 9.7 %slice-start = ((s8[4718592]{0:T(1024)(128)(4,1)}), s8[4194304]{0:T(1024)(128)(4,1)S(1)}, s32[]{:S(2)}) async-start(s8[4718592]{0:T(1024)(128)(4,1)} %bitcast.39), calls=%async_computation | async-start | bytes 8388608
  32.6 8.5 %copy-start.3 = (bf16[512,768]{1,0:T(8,128)(2,1)}, bf16[512,768]{1,0:T(8,128)(2,1)S(1)}, u32[]{:S(2)}) copy-start(bf16[512,768]{1,0:T(8,128)(2,1)S(1)} %get-tuple-element.68.refs_9_) | copy-start | bytes 2359300
  32.6 8.5 %copy-start = (f32[512,768]{1,0:T(8,128)}, f32[512,768]{1,0:T(8,128)S(1)}, u32[]{:S(2)}) copy-start(f32[512,768]{1,0:T(8,128)S(1)} %get-tuple-element.69.refs_12_) | copy-start | bytes 4718596
  32.7 8.5 %slice-start.1 = ((s8[4718592]{0:T(1024)(128)(4,1)}), s8[524288]{0:T(1024)(128)(4,1)S(1)}, s32[]{:S(2)}) async-start(s8[4718592]{0:T(1024)(128)(4,1)} %bitcast.39), calls=%async_computation.1 | async-start | bytes 1048576
  32.7 8.5 %copy-start.10 = (f32[768]{0:T(1024)S(1)}, f32[768]{0:T(1024)}, u32[]{:S(2)}) copy-start(f32[768]{0:T(1024)} %convert_element_type.79) | copy-start | bytes 9220
  32.7 8.5 %copy-start.11 = (f32[768]{0:T(1024)S(1)}, f32[768]{0:T(1024)}, u32[]{:S(2)}) copy-start(f32[768]{0:T(1024)} %convert_element_type.80) | copy-start | bytes 9220
  32.7 8.5 %copy-start.14 = (f32[768]{0:T(1024)S(1)}, f32[768]{0:T(1024)}, u32[]{:S(2)}) copy-start(f32[768]{0:T(1024)} %convert_element_type.84) | copy-start | bytes 9220
  47.3 4.7 %copy-start.1 = (bf16[512,768]{1,0:T(8,128)(2,1)}, bf16[512,768]{1,0:T(8,128)(2,1)S(1)}, u32[]{:S(2)}) copy-start(bf16[512,768]{1,0:T(8,128)(2,1)S(1)} %get-tuple-element.66.refs_10_) | copy-start | bytes 2359300
  47.4 156.9 %collective-permute-start.1 = (bf16[2,128,768]{2,1,0:T(8,128)(2,1)S(1)}, bf16[2,128,768]{2,1,0:T(8,128)(2,1)S(1)}, u32[]{:S(2)}, u32[]{:S(2)}) collective-permute-start(bf16[2,128,768]{2,1,0:T(8,128)(2,1)S(1)} %get-tuple-element.76), channel_id=1, source_target_pairs={{0,1},{1,0},{2,3},{3,2},{4,5},{5,4},{6,7},{7,6},{8,9},{9,8},{10,11... | collective-permute-start | bytes 1179656 | tf_op jit(solution)/shard_map/ppermute | solution.py:745
  187.9 15.7 %copy-start.9 = (f32[16,768]{1,0:T(8,128)S(1)}, f32[16,768]{1,0:T(8,128)}, u32[]{:S(2)}) copy-start(f32[16,768]{1,0:T(8,128)} %get-tuple-element.47) | copy-start | bytes 147460
  203.7 1.7 copy-start.7

commit v7 on v6

--- a/solution.py
+++ b/solution.py
@@ -727,7 +727,7 @@
 
 
 def to_float32(arrays):
-    steps = 12
+    steps = 24
     blocks = [pl.BlockSpec((a.shape[0] // steps, a.shape[1]), lambda i: (i, 0)) for a in arrays]
     return pl.pallas_call(
         widen_kernel,

time: 207 us -> 211 us (1.019)
  Pallas kernels: 154 us -> 158 us
    pallas_call x1, Pallas kernels: 15.7 us -> 20 us  [to_float32(): pl.pallas_call(widen_kernel, grid=(steps,), out_shape=tuple((jax.ShapeDty...]
where the time goes in v7:
time: 211 us; the launch traced here: 210 us
  Pallas kernels  158 us (75%)
  matrix products  22.9 us (11%)
  other arithmetic  8.64 us (4%)
  local copies, waits for them, and re-layouts  8.49 us (4%)
  waiting for transfers between devices  5.84 us (3%)
  starting transfers between devices  5.19 us (2%)
    pallas_call x1, Pallas kernels, backward(): pl.pallas_call(functools.partial(back_kernel, extra_bits), out_shape=tupl...  133 us
    pallas_call x1, Pallas kernels, to_float32(): pl.pallas_call(widen_kernel, grid=(steps,), out_shape=tuple((jax.ShapeDty...  20 us
    dot_general x6, matrix products, linear(): lax.dot_general(rows, weight_matrix, (((1,), (0,)), ((), ())), preferred_...  18.6 us
    ppermute x3, waiting for transfers between devices, to_partner(): return lax.ppermute(block, 'mod', [(0, 1), (1, 0)])  5.84 us
    pallas_call x1, Pallas kernels, attention_forward(): pl.pallas_call(forward_kernel, grid=(seqs,), out_shape=(jax.ShapeDtypeStr...  5.67 us
    ppermute x3, starting transfers between devices, to_partner(): return lax.ppermute(block, 'mod', [(0, 1), (1, 0)])  5.19 us
    dot_general x1, matrix products, weight_grad(): lax.dot_general(layer_inputs, gradient_rows, (((0,), (0,)), ((), ())), pr...  4.31 us
  transfers between devices with their start and end apart: 3, of which 1 were waited for; matrix products, arithmetic and copies ran while one was open for 16% of the time, Pallas kernels for 75%

profile of v7, /device:TPU:0, one launch (start us, length us, event | category | flops | bytes accessed | tf_op | source)
XLA Modules:
  0.0 210.5 jit_solution(11468470967363439187)
XLA Ops:
  0.7 0.0 copy-start.12
  0.7 0.0 copy-start.23
  0.7 0.0 copy-start.22
  0.7 0.0 copy-start.15
  0.7 0.0 copy-start.16
  0.7 0.0 copy-start.17
  0.7 0.0 copy-start.18
  0.7 0.0 copy-start.19
  0.7 0.0 copy-start.20
  0.8 0.0 copy-start.21
  0.8 0.0 copy-start.13
  0.8 0.0 copy-start.8
  0.8 1.3 constant_dynamic-slice_fusion.6
  2.0 3.0 %collective-permute-start = (bf16[2,128,768]{2,1,0:T(8,128)(2,1)S(1)}, bf16[2,128,768]{2,1,0:T(8,128)(2,1)S(1)}, u32[]{:S(2)}, u32[]{:S(2)}) collective-permute-start(bf16[2,128,768]{2,1,0:T(8,128)(2,1)S(1)} %get-tuple-element.78), channel_id=1, source_target_pairs={{0,1},{1,0},{2,3},{3,2},{4,5},{5,4},{6,7},{7,6},{8,9},{9,8},{10,11... | collective-permute-start | bytes 1179656 | tf_op jit(solution)/shard_map/ppermute | solution.py:745
  5.1 0.6 broadcast_in_dim.21.refs_18_
  5.7 0.6 convert_element_type.79
  6.3 0.1 dynamic_slice.28
  6.3 0.1 fusion.15
  6.5 0.6 convert_element_type.80
  7.1 0.6 convert_element_type.84
  7.7 0.6 convert_element_type.82
  8.3 0.1 constant_dynamic-slice_fusion
  8.4 5.8 %collective-permute-done = bf16[2,128,768]{2,1,0:T(8,128)(2,1)S(1)} collective-permute-done((bf16[2,128,768]{2,1,0:T(8,128)(2,1)S(1)}, bf16[2,128,768]{2,1,0:T(8,128)(2,1)S(1)}, u32[]{:S(2)}, u32[]{:S(2)}) %collective-permute-start) | collective-permute-done | bytes 393248 | tf_op jit(solution)/shard_map/ppermute | solution.py:745
  14.2 0.3 maximum_select_fusion
  14.5 0.0 copy-start.6
  14.5 1.8 collective-permute-start.2
  16.3 1.7 convolution_convert_fusion.1.k_ref.refs_5_
  18.0 1.7 add_convert_fusion.1.v_ref.refs_6_
  19.7 0.0 copy-done.4
  19.7 1.7 fusion.13.q_ref.refs_4_
  21.3 0.8 broadcast_in_dim.20.bias_ref.refs_20_
  22.2 5.7 %shard_map.314 = (bf16[512,768]{1,0:T(8,128)(2,1)}, f32[2,6,2,256]{3,2,1,0:T(2,128)}) custom-call(bf16[512,768]{1,0:T(8,128)(2,1)} %fusion.13.q_ref.refs_4_, bf16[512,768]{1,0:T(8,128)(2,1)} %convolution_convert_fusion.1.k_ref.refs_5_, bf16[512,768]{1,0:T(8,128)(2,1)} %add_convert_fusion.1.v_ref.refs_6_, f32[512,128]{1,0:T(8,128)} %broadcast_in_dim.20.bias_ref.refs_20_), custom_call_target="tpu_custom_call" | custom-call | tf_op jit(solution)/shard_map/pallas_call | solution.py:715
  27.8 0.0 copy-done.2
  27.9 2.4 %fusion.17 = (f32[512]{0:T(512)S(1)}, f32[512,768]{1,0:T(8,128)S(1)}) fusion(f32[768]{0:T(1024)S(1)} %convert_element_type.78, bf16[512,768]{1,0:T(8,128)(2,1)} %get-tuple-element.36.refs_7_, bf16[768,768]{1,0:T(8,128)(2,1)} %refs_16_.1, bf16[512,768]{1,0:T(8,128)(2,1)S(1)} %bitcast.45), kind=kOutput, calls=%fused_computation.62 | convolution fusion | flops 605552128 | bytes 4330496 | tf_op jit(solution)/shard_map/dot_general | solution.py:767
  30.2 0.3 multiply_reduce_fusion.1
  30.6 0.9 copy.36.refs_17_
  31.4 1.2 fusion.12
  32.6 0.0 copy-start.3
  32.6 0.0 copy-start
  32.7 0.0 slice-start.1
  32.7 0.0 copy-start.10
  32.7 0.0 copy-start.11
  32.7 0.0 copy-start.14
  32.7 8.5 %fusion.4 = (bf16[512,3072]{1,0:T(8,128)(2,1)}, bf16[512,3072]{1,0:T(8,128)(2,1)S(1)}) fusion(f32[3072]{0:T(1024)} %convert_element_type.82, bf16[512,768]{1,0:T(8,128)(2,1)S(1)} %get-tuple-element.68.refs_9_, bf16[768,3072]{1,0:T(8,128)(2,1)} %refs_2_.1), kind=kOutput, calls=%fused_computation.5 | convolution fusion | flops 2434793472 | bytes 11808768 | tf_op jit(solution)/shard_map/dot_general | solution.py:767
  41.2 2.7 %fusion.18 = (f32[512]{0:T(512)S(1)}, f32[512,768]{1,0:T(8,128)S(1)}) fusion(f32[768]{0:T(1024)S(1)} %copy-done.14, bf16[512,3072]{1,0:T(8,128)(2,1)S(1)} %get-tuple-element.71, bf16[3072,768]{1,0:T(8,128)(2,1)S(1)} %bitcast.40, f32[768]{0:T(1024)S(1)} %copy-done.11, f32[512,768]{1,0:T(8,128)S(1)} %get-tuple-element.69.refs_12_, f32[768]{0:T(1024)S(1)} %copy-done.10), kind=kOutput, calls=%fused_computation.63 | convolution fusion | flops 2417884672 | bytes 11021312 | tf_op jit(solution)/shard_map/dot_general | solution.py:767
  44.0 0.3 multiply_reduce_fusion
  44.3 0.0 collective-permute-done.2
  44.3 0.4 convert_reduce_fusion
  44.7 0.7 fusion.11
  45.5 1.9 convert_reduce_fusion.1
  47.3 0.1 constant_dynamic-slice_fusion.2
  47.4 0.4 collective-permute-start.1
  47.8 4.3 %convolution_convert_fusion.refs_0_ = bf16[3072,768]{1,0:T(8,128)(2,1)} fusion(bf16[512,3072]{1,0:T(8,128)(2,1)S(1)} %get-tuple-element.71, bf16[512,768]{1,0:T(8,128)(2,1)S(1)} %get-tuple-element.66.refs_10_), kind=kOutput, calls=%fused_computation.8 | convolution fusion | flops 2418278400 | bytes 8650752 | tf_op jit(solution)/shard_map/dot_general | solution.py:775
  52.1 0.6 broadcast_in_dim.24.refs_23_
  52.6 0.6 broadcast_in_dim.23.refs_22_
  53.2 0.6 broadcast_in_dim.22.refs_21_
  53.8 132.8 %shard_map.315 = (bf16[3072,768]{1,0:T(8,128)(2,1)}, bf16[768,3072]{1,0:T(8,128)(2,1)}, bf16[768,768]{1,0:T(8,128)(2,1)}, bf16[768,768]{1,0:T(8,128)(2,1)}, bf16...) custom-call(bf16[3072,768]{1,0:T(8,128)(2,1)} %convolution_convert_fusion.ref, ...), custom_call_target="tpu_custom_call" | custom-call | tf_op jit(solution)/shard_map/pallas_call | solution.py:604
  186.6 0.7 slice.32
  187.3 0.6 reshape.128
  188.0 20.0 %shard_map.316 = (f32[3072,768]{1,0:T(8,128)}, f32[768,3072]{1,0:T(8,128)}, f32[768,768]{1,0:T(8,128)}, f32[768,768]{1,0:T(8,128)}, f32[768,768]{1,0:T(8,128)}, /*index=5*/f32[768,768]{1,0:T(8,128)}) custom-call(bf16[3072,768]{1,0:T(8,128)(2,1)} %get-tuple-element.40.refs_0_, bf16[768,3072]{1,0:T(8,128)(2,1)} %get-tuple-element.41.refs_1_, ...), custom_call_target="tpu_custom_call" | custom-call | tf_op jit(solution)/shard_map/pallas_call | solution.py:732
  207.9 0.7 slice_reduce_fusion
  208.6 0.0 collective-permute-done.1
  208.6 1.0 maximum_select_fusion.1
  209.6 0.9 copy.40
  (46 shorter events, 0.1 us)
Async XLA Ops:
  0.7 4.4 %copy-start.12 = (bf16[768]{0:T(1024)(128)(2,1)S(1)}, bf16[768]{0:T(1024)(128)(2,1)}, u32[]{:S(2)}) copy-start(bf16[768]{0:T(1024)(128)(2,1)} %param.29) | copy-start | bytes 4612
  0.7 5.6 %copy-start.23 = (s32[4]{0:T(128)S(1)}, s32[4]{0:T(128)}, u32[]{:S(2)}) copy-start(s32[4]{0:T(128)} %param.21) | copy-start | bytes 52
  0.7 5.7 %copy-start.22 = (s32[4,128]{1,0:T(4,128)S(1)}, s32[4,128]{1,0:T(4,128)}, u32[]{:S(2)}) copy-start(s32[4,128]{1,0:T(4,128)} %param.20) | copy-start | bytes 6148
  0.7 5.7 %copy-start.15 = (bf16[768]{0:T(1024)(128)(2,1)S(1)}, bf16[768]{0:T(1024)(128)(2,1)}, u32[]{:S(2)}) copy-start(bf16[768]{0:T(1024)(128)(2,1)} %param.35) | copy-start | bytes 4612
  0.7 5.7 %copy-start.16 = (bf16[768]{0:T(1024)(128)(2,1)S(1)}, bf16[768]{0:T(1024)(128)(2,1)}, u32[]{:S(2)}) copy-start(bf16[768]{0:T(1024)(128)(2,1)} %param.30) | copy-start | bytes 4612
  0.7 6.3 %copy-start.17 = (bf16[768]{0:T(1024)(128)(2,1)S(1)}, bf16[768]{0:T(1024)(128)(2,1)}, u32[]{:S(2)}) copy-start(bf16[768]{0:T(1024)(128)(2,1)} %param.23) | copy-start | bytes 4612
  0.7 6.3 %copy-start.18 = (bf16[768]{0:T(1024)(128)(2,1)S(1)}, bf16[768]{0:T(1024)(128)(2,1)}, u32[]{:S(2)}) copy-start(bf16[768]{0:T(1024)(128)(2,1)} %param.26) | copy-start | bytes 4612
  0.7 6.3 %copy-start.19 = (bf16[768]{0:T(1024)(128)(2,1)S(1)}, bf16[768]{0:T(1024)(128)(2,1)}, u32[]{:S(2)}) copy-start(bf16[768]{0:T(1024)(128)(2,1)} %param.28) | copy-start | bytes 4612
  0.7 6.3 %copy-start.20 = (bf16[768]{0:T(1024)(128)(2,1)S(1)}, bf16[768]{0:T(1024)(128)(2,1)}, u32[]{:S(2)}) copy-start(bf16[768]{0:T(1024)(128)(2,1)} %param.34) | copy-start | bytes 4612
  0.8 6.9 %copy-start.21 = (bf16[768]{0:T(1024)(128)(2,1)S(1)}, bf16[768]{0:T(1024)(128)(2,1)}, u32[]{:S(2)}) copy-start(bf16[768]{0:T(1024)(128)(2,1)} %param.36) | copy-start | bytes 4612
  0.8 6.9 %copy-start.13 = (bf16[3072]{0:T(1024)(128)(2,1)S(1)}, bf16[3072]{0:T(1024)(128)(2,1)}, u32[]{:S(2)}) copy-start(bf16[3072]{0:T(1024)(128)(2,1)} %param.32) | copy-start | bytes 18436
  0.8 7.5 %copy-start.8 = (bf16[4,128,768]{2,1,0:T(8,128)(2,1)S(1)}, bf16[4,128,768]{2,1,0:T(8,128)(2,1)}, u32[]{:S(2)}) copy-start(bf16[4,128,768]{2,1,0:T(8,128)(2,1)} %param.37) | copy-start | bytes 2359300
  2.0 12.1 %collective-permute-start = (bf16[2,128,768]{2,1,0:T(8,128)(2,1)S(1)}, bf16[2,128,768]{2,1,0:T(8,128)(2,1)S(1)}, u32[]{:S(2)}, u32[]{:S(2)}) collective-permute-start(bf16[2,128,768]{2,1,0:T(8,128)(2,1)S(1)} %get-tuple-element.78), channel_id=1, source_target_pairs={{0,1},{1,0},{2,3},{3,2},{4,5},{5,4},{6,7},{7,6},{8,9},{9,8},{10,11... | collective-permute-start | bytes 1179656 | tf_op jit(solution)/shard_map/ppermute | solution.py:745
  8.3 8.0 %copy-start.5 = (bf16[768,768]{1,0:T(8,128)(2,1)S(1)}, bf16[768,768]{1,0:T(8,128)(2,1)}, u32[]{:S(2)}) copy-start(bf16[768,768]{1,0:T(8,128)(2,1)} %refs_14_.1) | copy-start | bytes 3538948
  14.5 13.3 %copy-start.2 = (bf16[2,256,768]{2,1,0:T(8,128)(2,1)}, bf16[2,256,768]{2,1,0:T(8,128)(2,1)S(1)}, u32[]{:S(2)}) copy-start(bf16[2,256,768]{2,1,0:T(8,128)(2,1)S(1)} %maximum_select_fusion) | copy-start | bytes 2359300
  14.5 3.5 %copy-start.6 = (bf16[768,768]{1,0:T(8,128)(2,1)S(1)}, bf16[768,768]{1,0:T(8,128)(2,1)}, u32[]{:S(2)}) copy-start(bf16[768,768]{1,0:T(8,128)(2,1)} %refs_15_.1) | copy-start | bytes 3538948
  14.5 29.8 %collective-permute-start.2 = (bf16[2,128,768]{2,1,0:T(8,128)(2,1)S(1)}, bf16[2,128,768]{2,1,0:T(8,128)(2,1)S(1)}, u32[]{:S(2)}, u32[]{:S(2)}) collective-permute-start(bf16[2,128,768]{2,1,0:T(8,128)(2,1)S(1)} %get-tuple-element.37), channel_id=1, source_target_pairs={{0,1},{1,0},{2,3},{3,2},{4,5},{5,4},{6,7},{7,6},{8,9},{9,8},{10,11... | collective-permute-start | bytes 1179656 | tf_op jit(solution)/shard_map/ppermute | solution.py:745
  18.0 1.7 copy-start.4
  31.4 9.7 %slice-start = ((s8[4718592]{0:T(1024)(128)(4,1)}), s8[4194304]{0:T(1024)(128)(4,1)S(1)}, s32[]{:S(2)}) async-start(s8[4718592]{0:T(1024)(128)(4,1)} %bitcast.39), calls=%async_computation | async-start | bytes 8388608
  32.6 8.5 %copy-start.3 = (bf16[512,768]{1,0:T(8,128)(2,1)}, bf16[512,768]{1,0:T(8,128)(2,1)S(1)}, u32[]{:S(2)}) copy-start(bf16[512,768]{1,0:T(8,128)(2,1)S(1)} %get-tuple-element.68.refs_9_) | copy-start | bytes 2359300
  32.6 8.5 %copy-start = (f32[512,768]{1,0:T(8,128)}, f32[512,768]{1,0:T(8,128)S(1)}, u32[]{:S(2)}) copy-start(f32[512,768]{1,0:T(8,128)S(1)} %get-tuple-element.69.refs_12_) | copy-start | bytes 4718596
  32.7 8.5 %slice-start.1 = ((s8[4718592]{0:T(1024)(128)(4,1)}), s8[524288]{0:T(1024)(128)(4,1)S(1)}, s32[]{:S(2)}) async-start(s8[4718592]{0:T(1024)(128)(4,1)} %bitcast.39), calls=%async_computation.1 | async-start | bytes 1048576
  32.7 8.5 %copy-start.10 = (f32[768]{0:T(1024)S(1)}, f32[768]{0:T(1024)}, u32[]{:S(2)}) copy-start(f32[768]{0:T(1024)} %convert_element_type.79) | copy-start | bytes 9220
  32.7 8.5 %copy-start.11 = (f32[768]{0:T(1024)S(1)}, f32[768]{0:T(1024)}, u32[]{:S(2)}) copy-start(f32[768]{0:T(1024)} %convert_element_type.80) | copy-start | bytes 9220
  32.7 8.5 %copy-start.14 = (f32[768]{0:T(1024)S(1)}, f32[768]{0:T(1024)}, u32[]{:S(2)}) copy-start(f32[768]{0:T(1024)} %convert_element_type.84) | copy-start | bytes 9220
  47.3 4.7 %copy-start.1 = (bf16[512,768]{1,0:T(8,128)(2,1)}, bf16[512,768]{1,0:T(8,128)(2,1)S(1)}, u32[]{:S(2)}) copy-start(bf16[512,768]{1,0:T(8,128)(2,1)S(1)} %get-tuple-element.66.refs_10_) | copy-start | bytes 2359300
  47.4 161.2 %collective-permute-start.1 = (bf16[2,128,768]{2,1,0:T(8,128)(2,1)S(1)}, bf16[2,128,768]{2,1,0:T(8,128)(2,1)S(1)}, u32[]{:S(2)}, u32[]{:S(2)}) collective-permute-start(bf16[2,128,768]{2,1,0:T(8,128)(2,1)S(1)} %get-tuple-element.76), channel_id=1, source_target_pairs={{0,1},{1,0},{2,3},{3,2},{4,5},{5,4},{6,7},{7,6},{8,9},{9,8},{10,11... | collective-permute-start | bytes 1179656 | tf_op jit(solution)/shard_map/ppermute | solution.py:745
  187.9 20.0 %copy-start.9 = (f32[16,768]{1,0:T(8,128)S(1)}, f32[16,768]{1,0:T(8,128)}, u32[]{:S(2)}) copy-start(f32[16,768]{1,0:T(8,128)} %get-tuple-element.47) | copy-start | bytes 147460
  207.9 1.7 copy-start.7
